TPU v7x, 256 devices: a whole 4x4x8 slice. The times are simulated.
256 devices in a mesh: dp: 16 (over z, y_hi), row: 4 (over y_lo, core), col: 4 (over x).
Axes of the slice: x: 4, y: 4 (y_hi: 2, y_lo: 2; y = y_hi * 2 + y_lo), z: 8, core: 2. Of those that a mesh axis runs over, the one named last changes fastest.
Arguments:
- tokens: bfloat16 [7168, 4096], P(('dp', 'col'), 'row'), may hold values from -6 to 6
- gate_up: bfloat16 [2, 4096, 14336], P(None, 'row', ('dp', 'col')), may hold values from -0.09375 to 0.09375
- down_weight: bfloat16 [14336, 4096], P(('dp', 'col'), 'row'), may hold values from -0.046875 to 0.046875
Outputs:
- mixed: bfloat16 [7168, 4096], P(('dp', 'col'), 'row')
- col_check: float32 [4096], P('row')
- row_check: float32 [7168], P(('dp', 'col'))
All inputs are finite; a program needn't handle non-finite values.
Results may differ from a plain program's by a relative error of at most 0.0049.
Values may be sent and summed in bfloat16 or wider, within the bound.
No kernel may reach another device: no remote copies, remote signals or barrier semaphores. Data moves between devices by JAX's collectives and lax.ppermute only.
A program may use at most 128 MiB of HBM per device.

v0:
```python
import math

import jax
import jax.numpy as jnp
from jax import lax
from jax.sharding import PartitionSpec as P


def swiglu(partial_value):
    return (jax.nn.silu(partial_value[:, 0]) * partial_value[:, 1]).astype(jnp.bfloat16)


def hidden_units(partial_value):
    share = lax.psum_scatter(partial_value, "row", scatter_dimension=0, tiled=True)
    return lax.all_gather(swiglu(share), "row", axis=0, tiled=True)


def make_accumulate(hidden, shard_piece):
    columns_wide = hidden.astype(jnp.float32)
    piece_wide = shard_piece.astype(jnp.float32)
    output_part = jnp.dot(hidden, shard_piece, preferred_element_type=jnp.float32)
    column_part = jnp.dot(
        jnp.sum(columns_wide, axis=0), piece_wide, precision=lax.Precision.HIGHEST
    )
    row_part = jnp.dot(columns_wide, jnp.sum(piece_wide, axis=1), precision=lax.Precision.HIGHEST)
    return (output_part, column_part, row_part)


def per_device(tokens, gate_up, down_weight):
    total_tokens = tokens.shape[0] * lax.axis_size(("dp", "col"))
    model_width = tokens.shape[1] * lax.axis_size("row")
    group_rows = lax.all_gather(tokens, "col", axis=0, tiled=True)
    partial_value = jnp.einsum(
        "td,gdf->tgf",
        group_rows,
        lax.all_gather(gate_up, "dp", axis=2, tiled=True),
        preferred_element_type=jnp.float32,
    )
    hidden = hidden_units(partial_value)
    output_part, column_part, row_part = make_accumulate(
        hidden, lax.all_gather(down_weight, "dp", axis=0, tiled=True)
    )
    mixed, row_share = (
        lax.psum_scatter(output_part, "col", scatter_dimension=0, tiled=True),
        lax.psum_scatter(row_part, "col", scatter_dimension=0, tiled=True),
    )
    col_check = lax.psum(column_part, ("dp", "col")) / math.sqrt(total_tokens)
    row_check = lax.psum(row_share, "row") / math.sqrt(model_width)
    return (mixed.astype(jnp.bfloat16), col_check, row_check)


def solution(mesh):
    placed = (P(("dp", "col"), "row"), P(None, "row", ("dp", "col")), P(("dp", "col"), "row"))
    return jax.shard_map(
        per_device,
        mesh=mesh,
        in_specs=placed,
        out_specs=(P(("dp", "col"), "row"), P("row"), P(("dp", "col"))),
        check_vma=False,
    )
```

profile of v0, /device:TPU:4, one launch (start us, length us, event | category | flops | bytes accessed | tf_op | source)
XLA Modules:
  0.0 743.2 jit_solution(9035475301600994231)
XLA Ops:
  7.2 0.7 all-gather.4.cloned.1.call-update
  7.9 14.6 %all_gather.12 = bf16[448,1024]{1,0:T(8,128)(2,1)S(1)} all-gather(bf16[112,1024]{1,0:T(8,128)(2,1)} %param.3), channel_id=1, replica_groups=mesh['dp'=16,'row'=4,'col'=4] {'col'}, dimensions={0}, use_global_device_ids=true | all-gather | bytes 1146880 | tf_op jit(solution)/shard_map/all_gather | solution.py:32
  22.6 192.6 %all-gather.4.cloned.1.call-done = bf16[2,1024,3584]{1,2,0:T(8,128)(2,1)} async-done(((bf16[2,1024,224]{1,2,0:T(8,128)(2,1)}), bf16[2,1024,3584]{1,2,0:T(8,128)(2,1)}) %all-gather.4.cloned.1.call-update) | async-done | bytes 14680080 | tf_op jit(solution)/shard_map/all_gather | solution.py:36
  215.2 22.2 %fusion.2 = f32[448,2,3584]{2,0,1:T(8,128)} fusion(bf16[2,1024,3584]{1,2,0:T(8,128)(2,1)} %all-gather.4.cloned.1.call-done, bf16[448,1024]{1,0:T(8,128)(2,1)S(1)} %all_gather.12), kind=kOutput, calls=%fused_computation.6 | convolution fusion | flops 6576668672 | bytes 28442624 | tf_op jit(solution)/shard_map/td,gdf->tgf/dot_general | solution.py:33
  237.4 0.0 all-gather.8.cloned.1.call-start
  237.5 0.7 all-gather.8.cloned.1.call-update
  238.2 113.8 %reduce-scatter.3.cloned.1.call-done = f32[112,2,3584]{2,0,1:T(8,128)} async-done(((f32[448,2,3584]{2,0,1:T(8,128)}), f32[112,2,3584]{2,0,1:T(8,128)}) %reduce-scatter.3.cloned.1.call-update) | async-done | bytes 3211280 | tf_op jit(solution)/shard_map/reduce_scatter | solution.py:14
  352.1 3.2 fusion.1
  355.3 0.0 reduce-scatter.5.cloned.1.call-start
  355.4 125.9 %all-gather.8.cloned.1.call-done = bf16[3584,1024]{1,0:T(8,128)(2,1)} async-done(((bf16[224,1024]{1,0:T(8,128)(2,1)}), bf16[3584,1024]{1,0:T(8,128)(2,1)}) %all-gather.8.cloned.1.call-update) | async-done | bytes 7340048 | tf_op jit(solution)/shard_map/all_gather | solution.py:41
  481.2 39.0 %all-gather.6.cloned.1.call-done = bf16[448,3584]{1,0:T(8,128)(2,1)} async-done(((bf16[112,3584]{1,0:T(8,128)(2,1)}), bf16[448,3584]{1,0:T(8,128)(2,1)}) %all-gather.6.cloned.1.call-update) | async-done | bytes 3211280 | tf_op jit(solution)/shard_map/all_gather | solution.py:15
  520.2 8.8 %fusion.4 = f32[448,1024]{1,0:T(8,128)} fusion(bf16[448,3584]{1,0:T(8,128)(2,1)} %all-gather.6.cloned.1.call-done, bf16[3584,1024]{1,0:T(8,128)(2,1)} %all-gather.8.cloned.1.call-done), kind=kOutput, calls=%fused_computation.10 | convolution fusion | flops 3288334336 | bytes 12386304 | tf_op jit(solution)/shard_map/dot_general | solution.py:21
  529.0 0.6 dynamic-slice
  530.3 4.3 convert_reduce_fusion
  534.6 0.6 convert_reduce_fusion.1
  535.2 2.6 fusion.6
  537.8 8.3 %all-reduce = f32[448]{0:T(512)S(1)} all-reduce(f32[448]{0:T(512)S(1)} %bitcast.24), channel_id=4, replica_groups=mesh['dp'=16,'row'=4,'col'=4] {'col'}, use_global_device_ids=true, to_apply=%region_5.6.clone | all-reduce | flops 448 | bytes 3584
  546.1 0.1 dynamic-slice.1
  546.2 6.0 psum.15
  552.2 5.2 fusion.5
  557.4 176.5 %psum.14 = f32[1024]{0:T(1024)S(1)} all-reduce(f32[1024]{0:T(1024)S(1)} %bitcast.23), channel_id=1, replica_groups=mesh['dp'=16,'row'=4,'col'=4] {'dp','col'}, use_global_device_ids=true, to_apply=%region_3.4 | all-reduce | flops 1024 | bytes 8192 | tf_op jit(solution)/shard_map/psum | solution.py:47
  733.9 0.5 broadcast_multiply_fusion.1
  734.4 0.6 broadcast_multiply_fusion
  735.0 1.7 convert_element_type.13
  (13 shorter events, 0.2 us)
Async XLA Ops:
  7.2 208.0 %all-gather.4.cloned.1.call-start = ((), (), s32[]{:S(2)}) async-start(), calls=%async_computation.2 | async-start | bytes 15597568 | tf_op jit(solution)/shard_map/all_gather | solution.py:36
  7.9 344.2 %reduce-scatter.3.cloned.1.call-start = ((), (), s32[]{:S(2)}) async-start(), calls=%async_computation.3 | async-start | bytes 16056320 | tf_op jit(solution)/shard_map/reduce_scatter | solution.py:14
  237.4 243.8 %all-gather.8.cloned.1.call-start = ((), (), s32[]{:S(2)}) async-start(), calls=%async_computation.5 | async-start | bytes 7798784 | tf_op jit(solution)/shard_map/all_gather | solution.py:41
  238.2 282.1 %all-gather.6.cloned.1.call-start = ((), (), s32[]{:S(2)}) async-start(), calls=%async_computation.4 | async-start | bytes 4014080 | tf_op jit(solution)/shard_map/all_gather | solution.py:15
  355.3 173.7 %copy-start.1 = (u32[256]{0:T(256)S(1)}, u32[256]{0:T(256)}, u32[]{:S(2)}) copy-start(u32[256]{0:T(256)} %constant.16) | copy-start | bytes 3076
  355.3 379.6 %reduce-scatter.5.cloned.1.call-start = ((), (), s32[]{:S(2)}) async-start(), calls=%async_computation.6 | async-start | bytes 2293760 | tf_op jit(solution)/shard_map/reduce_scatter | solution.py:44
  530.3 4.3 copy-start
Sparse Core Ops, SparseCore 0:
  10.6 204.5 all-gather.3
  237.5 114.4 reduce-scatter.2
  354.7 126.5 all-gather.7
  482.9 37.3 all-gather.5
  529.1 29.8 reduce-scatter.4
where the time goes:
time: 749 us; the launch traced here: 743 us
  waiting for transfers between devices  473 us (63%)
  blocking collectives  205 us (27%)
  matrix products  38.7 us (5%)
  between operations  14.5 us (2%)
  other arithmetic  10.9 us (1%)
    all_gather x1, waiting for transfers between devices, per_device(): lax.all_gather(gate_up, 'dp', axis=2, tiled=True)  193 us
    psum x1, blocking collectives, per_device(): col_check = lax.psum(column_part, ('dp', 'col')) / math.sqrt(total_tokens)  176 us
    all_gather x1, waiting for transfers between devices, per_device(): lax.all_gather(down_weight, 'dp', axis=0, tiled=True)  126 us
    reduce_scatter x1, waiting for transfers between devices, hidden_units(): lax.psum_scatter(partial_value, 'row', scatter_dimension=0, tiled=True)  114 us
    all_gather x1, waiting for transfers between devices, hidden_units(): return lax.all_gather(swiglu(share), 'row', axis=0, tiled=True)  39 us
    dot_general x1, matrix products, per_device(): jnp.einsum('td,gdf->tgf', group_rows, lax.all_gather(gate_up, 'dp', axis=...  22.2 us
  transfers between devices with their start and end apart: 5, of which 4 were waited for; matrix products, arithmetic and copies ran while one was open for 2% of the time, Pallas kernels for 0%

commit v1 on v0

v1 whole, which is shorter than its diff:
```python
import math

import jax
import jax.numpy as jnp
import numpy as np
from jax import lax
from jax.sharding import Mesh, PartitionSpec as P

ROW = ("yl", "c")
Y = ("yh", "yl")


def ring(n, step):
    return [(i, (i - step) % n) for i in range(n)]


def flip(n, mask):
    return [(i, i ^ mask) for i in range(n)]


def split(value):
    high = lax.reduce_precision(value, 8, 7)
    return high.astype(jnp.bfloat16), (value - high).astype(jnp.bfloat16)


def swiglu(gate, up):
    return (jax.nn.silu(gate) * up).astype(jnp.bfloat16)


def sum_over(value, axis, n):
    mask = 1
    while mask < n:
        value = value + lax.ppermute(value, axis, flip(n, mask))
        mask *= 2
    return value


def per_device(tokens, gate_up, down_weight):
    rows, width = tokens.shape
    units = gate_up.shape[2]
    nz, nx, nyh, nrow = (lax.axis_size(a) for a in ("z", "x", "yh", ROW))
    part = units // nrow
    total_tokens = rows * nz * nx * nyh
    model_width = width * nrow
    own = lax.axis_index(ROW)

    pieces = jnp.swapaxes(gate_up, 1, 2).reshape(2, nrow, part, width)
    weights = []
    for k in range(nrow):
        piece = lax.dynamic_index_in_dim(pieces, own ^ k, 1, keepdims=False)
        weights.append(piece if k == 0 else lax.ppermute(piece, ROW, flip(nrow, k)))
    weights = jnp.concatenate(weights, axis=-1)
    weights = lax.all_gather(weights, "z", axis=0, tiled=False)

    sums = jnp.sum(down_weight.astype(jnp.float32), axis=1)
    sums = sum_over(sum_over(sums, "c", 2), "yl", 2)
    down = down_weight.reshape(nrow, part, width)
    order = [own ^ k for k in range(nrow)]
    down = jnp.concatenate([lax.dynamic_slice_in_dim(down, q, 1, 0) for q in order])
    sums = jnp.concatenate(
        [lax.dynamic_slice_in_dim(sums.reshape(nrow, part), q, 1, 0) for q in order]
    )
    down = lax.all_gather(down, "z", axis=0, tiled=False)
    sums = lax.all_gather(sums, "z", axis=0, tiled=False)

    group = jnp.concatenate(
        [tokens] + [lax.ppermute(tokens, "x", ring(nx, k)) for k in range(1, nx)]
    )
    group = [group] + [lax.ppermute(group, Y, flip(2 * nyh, k)) for k in range(1, 2 * nyh)]
    mine = [jnp.concatenate([group[d], group[2 + d]]) for d in (0, 1)]
    other = [lax.ppermute(m, "c", flip(2, 1)) for m in mine]
    wide = jnp.concatenate([mine[0], other[0], mine[1], other[1]], axis=-1)

    gate_up_sum = jnp.einsum("td,zgfd->tgzf", wide, weights, preferred_element_type=jnp.float32)
    hidden = swiglu(gate_up_sum[:, 0], gate_up_sum[:, 1])
    far = lax.ppermute(hidden, "yl", flip(2, 1))
    hidden = [hidden, lax.ppermute(hidden, "c", flip(2, 1)), far, lax.ppermute(far, "c", flip(2, 1))]
    hidden = jnp.stack(hidden, axis=2)
    hidden_wide = hidden.astype(jnp.float32)

    unit_sums = sum_over(jnp.sum(hidden_wide, axis=0), "z", nz)
    out = jnp.einsum("tzkf,zkfd->td", hidden, down, preferred_element_type=jnp.float32)
    col = jnp.einsum(
        "zkf,zkfd->d", unit_sums, down.astype(jnp.float32), precision=lax.Precision.HIGHEST
    )
    row = jnp.einsum("tzkf,zkf->t", hidden_wide, sums, precision=lax.Precision.HIGHEST)

    out = out.reshape(nyh, nx, rows, width)
    row = row.reshape(nyh, nx, rows)
    received = []
    for dy in range(nyh):
        for dx in range(nx):
            row_pad = jnp.pad(row[dy, dx], (0, width - rows))
            extra = jnp.stack([*split(col), *split(row_pad)])
            extra = jnp.pad(extra, ((0, 4), (0, 0)))
            sent = jnp.concatenate([out[dy, dx].astype(jnp.bfloat16), extra])
            if dx or dy:
                perm = [
                    (h * nx + i, (h ^ dy) * nx + (i + dx) % nx)
                    for h in range(nyh)
                    for i in range(nx)
                ]
                sent = lax.ppermute(sent, ("yh", "x"), perm)
            received.append(sent.astype(jnp.float32))
    result = sum(received)
    mixed = result[:rows].astype(jnp.bfloat16)
    col_check = (result[rows] + result[rows + 1]) / math.sqrt(total_tokens)
    row_check = (result[rows + 2] + result[rows + 3])[:rows] / math.sqrt(model_width)
    return (mixed, col_check, row_check)


def solution(mesh):
    shape = mesh.shape
    devices = np.asarray(mesh.devices).reshape(shape["dp"] // 2, 2, shape["row"] // 2, 2, shape["col"])
    fine = Mesh(devices, ("z", "yh", "yl", "c", "x"))
    batch, wide = ("z", "yh", "x"), ("yl", "c")
    return jax.shard_map(
        per_device,
        mesh=fine,
        in_specs=(P(batch, wide), P(None, wide, batch), P(batch, wide)),
        out_specs=(P(batch, wide), P(wide), P(batch)),
        check_vma=False,
    )
```

time: 749 us -> 242 us (0.32)
  waiting for transfers between devices: 473 us -> 123 us
  blocking collectives: 205 us -> 21.3 us
  starting transfers between devices: 0.2 us -> 36.8 us
  matrix products: 38.7 us -> 30.5 us
    all_gather x3 -> x2, waiting for transfers between devices: 357 us -> 22.2 us  [the longest x1 22.2 us: per_device(): weights = lax.all_gather(weights, 'z', axis=0, tiled=False)]
    psum x2 -> x0, blocking collectives: 183 us -> none  [the longest x1 176 us: per_device(): col_check = lax.psum(column_part, ('dp', 'col')) / math.sqrt(total_tokens)]
    reduce_scatter x2 -> x0, waiting for transfers between devices: 114 us -> none  [the longest x1 114 us: hidden_units(): lax.psum_scatter(partial_value, 'row', scatter_dimension=0, tiled=True)]
    ppermute x0 -> x26, waiting for transfers between devices: none -> 101 us  [the longest x3 39.7 us: per_device(): lax.ppermute(group, Y, flip(2 * nyh, k))]
    ppermute x0 -> x26, starting transfers between devices: none -> 36.7 us  [the longest x7 16 us: per_device(): sent = lax.ppermute(sent, ('yh', 'x'), perm)]
    unnamed x1 -> x0, blocking collectives: 8.35 us -> none
    dot_general x4, matrix products: 38.7 us -> 30.5 us  [the longest x1 19.3 us: per_device(): jnp.einsum('td,zgfd->tgzf', wide, weights, preferred_element_type=jnp.flo...]
  transfers between devices with their start and end apart: 5 -> 28, of which waited for: 4 -> 20; matrix products, arithmetic and copies ran while one was open for 2% -> 16% of each run, Pallas kernels for 0% -> 0%
where the time goes in v1:
time: 242 us; the launch traced here: 241 us
  waiting for transfers between devices  123 us (51%)
  starting transfers between devices  36.8 us (15%)
  matrix products  30.5 us (13%)
  blocking collectives  21.3 us (9%)
  between operations  14.5 us (6%)
  other arithmetic  7.71 us (3%)
  local copies, waits for them, and re-layouts  7.6 us (3%)
    ppermute x3, waiting for transfers between devices, per_device(): lax.ppermute(group, Y, flip(2 * nyh, k))  39.7 us
    all_gather x1, waiting for transfers between devices, per_device(): weights = lax.all_gather(weights, 'z', axis=0, tiled=False)  22.2 us
    all_gather x1, blocking collectives, per_device(): sums = lax.all_gather(sums, 'z', axis=0, tiled=False)  21.3 us
    dot_general x1, matrix products, per_device(): jnp.einsum('td,zgfd->tgzf', wide, weights, preferred_element_type=jnp.flo...  19.3 us
    ppermute x1, waiting for transfers between devices, per_device(): far = lax.ppermute(hidden, 'yl', flip(2, 1))  18.5 us
    ppermute x7, starting transfers between devices, per_device(): sent = lax.ppermute(sent, ('yh', 'x'), perm)  16 us
    ppermute x5, waiting for transfers between devices, sum_over(): value = value + lax.ppermute(value, axis, flip(n, mask))  11.9 us
    ppermute x3, waiting for transfers between devices, per_device(): weights.append(piece if k == 0 else lax.ppermute(piece, ROW, flip(nrow, k)))  10.6 us
  transfers between devices with their start and end apart: 28, of which 20 were waited for; matrix products, arithmetic and copies ran while one was open for 16% of the time, Pallas kernels for 0%

profile of v1, /device:TPU:4, one launch (start us, length us, event | category | flops | bytes accessed | tf_op | source)
XLA Modules:
  0.0 241.2 jit_solution(12218489831087876332)
XLA Ops:
  10.6 6.6 %collective-permute-done.1 = bf16[2,56,1024]{2,1,0:T(8,128)(2,1)S(1)} collective-permute-done((bf16[2,56,1024]{2,1,0:T(8,128)(2,1)S(1)}, bf16[2,56,1024]{2,1,0:T(8,128)(2,1)S(1)}, u32[]{:S(2)}, u32[]{:S(2)}) %collective-permute-start.1) | collective-permute-done | bytes 229408 | tf_op jit(solution)/shard_map/ppermute | solution.py:51
  17.2 4.0 %collective-permute-done.2 = bf16[2,56,1024]{2,1,0:T(8,128)(2,1)S(1)} collective-permute-done((bf16[2,56,1024]{2,1,0:T(8,128)(2,1)S(1)}, bf16[2,56,1024]{2,1,0:T(8,128)(2,1)S(1)}, u32[]{:S(2)}, u32[]{:S(2)}) %collective-permute-start.2) | collective-permute-done | bytes 229408 | tf_op jit(solution)/shard_map/ppermute | solution.py:51
  22.9 2.7 %collective-permute-start.4 = (bf16[112,1024]{1,0:T(8,128)(2,1)S(1)}, bf16[112,1024]{1,0:T(8,128)(2,1)S(1)}, u32[]{:S(2)}, u32[]{:S(2)}) collective-permute-start(bf16[112,1024]{1,0:T(8,128)(2,1)S(1)} %copy-done.5), channel_id=1, source_target_pairs={{0,2},{1,3},{2,0},{3,1},{4,6},{5,7},{6,4},{7,5},{8,10},{9,11},{10,... | collective-permute-start | bytes 688136 | tf_op jit(solution)/shard_map/ppermute | solution.py:67
  28.0 2.8 %collective-permute-done.3 = bf16[112,1024]{1,0:T(8,128)(2,1)S(1)} collective-permute-done((bf16[112,1024]{1,0:T(8,128)(2,1)S(1)}, bf16[112,1024]{1,0:T(8,128)(2,1)S(1)}, u32[]{:S(2)}, u32[]{:S(2)}) %collective-permute-start.3) | collective-permute-done | bytes 229408 | tf_op jit(solution)/shard_map/ppermute | solution.py:67
  33.7 3.2 %collective-permute-done.5 = bf16[112,1024]{1,0:T(8,128)(2,1)S(1)} collective-permute-done((bf16[112,1024]{1,0:T(8,128)(2,1)S(1)}, bf16[112,1024]{1,0:T(8,128)(2,1)S(1)}, u32[]{:S(2)}, u32[]{:S(2)}) %collective-permute-start.5) | collective-permute-done | bytes 229408 | tf_op jit(solution)/shard_map/ppermute | solution.py:67
  39.1 2.2 collective-permute-start.9
  42.1 18.7 %collective-permute-done.8 = bf16[448,1024]{1,0:T(8,128)(2,1)S(1)} collective-permute-done((bf16[448,1024]{1,0:T(8,128)(2,1)S(1)}, bf16[448,1024]{1,0:T(8,128)(2,1)S(1)}, u32[]{:S(2)}, u32[]{:S(2)}) %collective-permute-start.8) | collective-permute-done | bytes 917536 | tf_op jit(solution)/shard_map/ppermute | solution.py:69
  60.9 19.6 %collective-permute-done.9 = bf16[448,1024]{1,0:T(8,128)(2,1)S(1)} collective-permute-done((bf16[448,1024]{1,0:T(8,128)(2,1)S(1)}, bf16[448,1024]{1,0:T(8,128)(2,1)S(1)}, u32[]{:S(2)}, u32[]{:S(2)}) %collective-permute-start.9) | collective-permute-done | bytes 917536 | tf_op jit(solution)/shard_map/ppermute | solution.py:69
  84.6 2.8 %collective-permute-done.7 = bf16[896,1024]{1,0:T(8,128)(2,1)} collective-permute-done((bf16[896,1024]{1,0:T(8,128)(2,1)}, bf16[896,1024]{1,0:T(8,128)(2,1)}, u32[]{:S(2)}, u32[]{:S(2)}) %collective-permute-start.7) | collective-permute-done | bytes 1835040 | tf_op jit(solution)/shard_map/ppermute | solution.py:71
  87.4 22.2 %all-gather.7.cloned.1.call-done = bf16[16,56,4096]{2,1,0:T(8,128)(2,1)} async-done(((bf16[2,56,4096]{2,1,0:T(8,128)(2,1)}), bf16[16,56,4096]{2,1,0:T(8,128)(2,1)}) %all-gather.7.cloned.1.call-update) | async-done | bytes 7340048 | tf_op jit(solution)/shard_map/all_gather | solution.py:53
  109.6 19.3 %fusion.11 = f32[896,2,8,56]{0,3,1,2:T(8,128)S(1)} fusion(bf16[8,2,56,4096]{3,2,1,0:T(8,128)(2,1)} %bitcast.137, bf16[896,1024]{1,0:T(8,128)(2,1)} %collective-permute-done.10, bf16[896,1024]{1,0:T(8,128)(2,1)} %copy-done.4, bf16[896,1024]{1,0:T(8,128)(2,1)} %collective-permute-done.7, bf16[896,1024]{1,0:T(8,128)(2,1)} %constant_dynamic-update-slice_fusion.4), kind=kOutput, calls=%fused_computation.15 | convolution fusion | flops 6606028800 | bytes 17891328 | tf_op jit(solution)/shard_map/td,zgfd->tgzf/dot_general | solution.py:74
  131.7 18.5 %collective-permute-done.12 = bf16[896,8,56]{0,2,1:T(8,128)(2,1)} collective-permute-done((bf16[896,8,56]{0,2,1:T(8,128)(2,1)}, bf16[896,8,56]{0,2,1:T(8,128)(2,1)}, u32[]{:S(2)}, u32[]{:S(2)}) %collective-permute-start.12) | collective-permute-done | bytes 802848 | tf_op jit(solution)/shard_map/ppermute | solution.py:76
  154.0 2.1 collective-permute-done.18
  156.2 21.3 %all-gather.3 = f32[8,4,56]{2,1,0:T(4,128)S(1)} all-gather(f32[1,4,56]{2,1,0:T(4,128)S(1)} %maximum_bitcast_fusion.4), channel_id=4, replica_groups=mesh['z'=8,'yh'=2,'yl'=2,'c'=2,'x'=4] {'z'}, dimensions={0}, use_global_device_ids=true | all-gather | bytes 8064 | tf_op jit(solution)/shard_map/all_gather | solution.py:64
  178.8 3.2 %fusion.24 = f32[896]{0:T(1024)S(1)} fusion(f32[8,4,56,1]{2,1,0,3:T(4,128)S(1)} %bitcast.134, bf16[896,8,1,56]{0,3,1,2:T(8,128)(2,1)} %bitcast.17, bf16[896,8,1,56]{0,3,1,2:T(8,128)(2,1)} %bitcast.16, bf16[896,8,1,56]{0,3,1,2:T(8,128)(2,1)} %bitcast.15, bf16[896,8,1,56]{0,3,1,2:T(8,128)(2,1)S(1)} %fusion.22), kind=kOutput, calls=%fused_computation.31 | convolution fusion | flops 24084480 | bytes 3222016 | tf_op jit(solution)/shard_map/tzkf,zkf->t/dot_general | solution.py:86
  182.1 2.2 convert_reduce_fusion
  186.0 6.3 %bitcast_convert_fusion = bf16[896,1024]{1,0:T(8,128)(2,1)S(1)} fusion(bf16[8,4,56,1024]{3,2,1,0:T(8,128)(2,1)} %bitcast.138, bf16[896,8,1,56]{0,3,1,2:T(8,128)(2,1)} %bitcast.17, bf16[896,8,1,56]{0,3,1,2:T(8,128)(2,1)} %bitcast.16, bf16[896,8,1,56]{0,3,1,2:T(8,128)(2,1)} %bitcast.15, bf16[896,8,1,56]{0,3,1,2:T(8,128)(2,1)S(1)} %copy-done.1), kind=kOutput, calls=%fused_computation.9 | convolution fusion | flops 3294068736 | bytes 8716288 | tf_op jit(solution)/shard_map/tzkf,zkfd->td/dot_general | solution.py:82
  194.2 3.2 %collective-permute-done.15 = f32[8,4,56]{2,0,1:T(8,128)S(1)} collective-permute-done((f32[8,4,56]{2,0,1:T(8,128)S(1)}, f32[8,4,56]{2,0,1:T(8,128)S(1)}, u32[]{:S(2)}, u32[]{:S(2)}) %collective-permute-start.15) | collective-permute-done | bytes 7200 | tf_op jit(solution)/shard_map/ppermute | solution.py:33
  197.4 2.4 collective-permute-start.16
  200.0 5.1 %collective-permute-done.16 = f32[8,4,56]{2,0,1:T(8,128)S(1)} collective-permute-done((f32[8,4,56]{2,0,1:T(8,128)S(1)}, f32[8,4,56]{2,0,1:T(8,128)S(1)}, u32[]{:S(2)}, u32[]{:S(2)}) %collective-permute-start.16) | collective-permute-done | bytes 7200 | tf_op jit(solution)/shard_map/ppermute | solution.py:33
  210.6 3.1 %collective-permute-start.22 = (bf16[120,1024]{1,0:T(8,128)(2,1)S(1)}, bf16[120,1024]{1,0:T(8,128)(2,1)S(1)}, u32[]{:S(2)}, u32[]{:S(2)}) collective-permute-start(bf16[120,1024]{1,0:T(8,128)(2,1)S(1)} %fusion.37), channel_id=1, source_target_pairs={{0,16},{1,17},{2,18},{3,19},{16,0},{17,1},{18,2},{19,3},{4,20},{5,... | collective-permute-start | bytes 737288 | tf_op jit(solution)/shard_map/ppermute | solution.py:103
  215.3 8.3 %collective-permute-start.24 = (bf16[120,1024]{1,0:T(8,128)(2,1)S(1)}, bf16[120,1024]{1,0:T(8,128)(2,1)S(1)}, u32[]{:S(2)}, u32[]{:S(2)}) collective-permute-start(bf16[120,1024]{1,0:T(8,128)(2,1)S(1)} %fusion.39), channel_id=1, source_target_pairs={{0,18},{1,19},{2,16},{3,17},{16,2},{17,3},{18,0},{19,1},{4,22},{5,... | collective-permute-start | bytes 737288 | tf_op jit(solution)/shard_map/ppermute | solution.py:103
  224.2 3.6 %collective-permute-done.24 = bf16[120,1024]{1,0:T(8,128)(2,1)S(1)} collective-permute-done((bf16[120,1024]{1,0:T(8,128)(2,1)S(1)}, bf16[120,1024]{1,0:T(8,128)(2,1)S(1)}, u32[]{:S(2)}, u32[]{:S(2)}) %collective-permute-start.24) | collective-permute-done | bytes 245792 | tf_op jit(solution)/shard_map/ppermute | solution.py:103
  227.8 4.4 %collective-permute-done.25 = bf16[120,1024]{1,0:T(8,128)(2,1)S(1)} collective-permute-done((bf16[120,1024]{1,0:T(8,128)(2,1)S(1)}, bf16[120,1024]{1,0:T(8,128)(2,1)S(1)}, u32[]{:S(2)}, u32[]{:S(2)}) %collective-permute-start.25) | collective-permute-done | bytes 245792 | tf_op jit(solution)/shard_map/ppermute | solution.py:103
  (115 shorter events, 39.0 us)
Async XLA Ops:
  7.2 102.4 %all-gather.7.cloned.1.call-start = ((), (), s32[]{:S(2)}) async-start(), calls=%async_computation | async-start | bytes 8257536 | tf_op jit(solution)/shard_map/all_gather | solution.py:53
  8.7 8.5 %collective-permute-start.1 = (bf16[2,56,1024]{2,1,0:T(8,128)(2,1)S(1)}, bf16[2,56,1024]{2,1,0:T(8,128)(2,1)S(1)}, u32[]{:S(2)}, u32[]{:S(2)}) collective-permute-start(bf16[2,56,1024]{2,1,0:T(8,128)(2,1)S(1)} %get-tuple-element.12), channel_id=1, source_target_pairs={{0,8},{4,12},{8,0},{12,4},{1,9},{5,13},{9,1},{13,5},{2,10},{6,14},... | collective-permute-start | bytes 688136 | tf_op jit(solution)/shard_map/ppermute | solution.py:51
  10.4 10.8 %collective-permute-start.2 = (bf16[2,56,1024]{2,1,0:T(8,128)(2,1)S(1)}, bf16[2,56,1024]{2,1,0:T(8,128)(2,1)S(1)}, u32[]{:S(2)}, u32[]{:S(2)}) collective-permute-start(bf16[2,56,1024]{2,1,0:T(8,128)(2,1)S(1)} %get-tuple-element.14), channel_id=1, source_target_pairs={{0,12},{4,8},{8,4},{12,0},{1,13},{5,9},{9,5},{13,1},{2,14},{6,10},... | collective-permute-start | bytes 688136 | tf_op jit(solution)/shard_map/ppermute | solution.py:51
  22.2 163.8 %all-gather.9.cloned.1.call-start = ((), (), s32[]{:S(2)}) async-start(), calls=%async_computation.1 | async-start | bytes 4128768 | tf_op jit(solution)/shard_map/all_gather | solution.py:63
  22.3 8.5 %collective-permute-start.3 = (bf16[112,1024]{1,0:T(8,128)(2,1)S(1)}, bf16[112,1024]{1,0:T(8,128)(2,1)S(1)}, u32[]{:S(2)}, u32[]{:S(2)}) collective-permute-start(bf16[112,1024]{1,0:T(8,128)(2,1)S(1)} %copy-done.5), channel_id=1, source_target_pairs={{0,3},{1,0},{2,1},{3,2},{4,7},{5,4},{6,5},{7,6},{8,11},{9,8},{10,9... | collective-permute-start | bytes 688136 | tf_op jit(solution)/shard_map/ppermute | solution.py:67
  22.9 10.0 %collective-permute-start.4 = (bf16[112,1024]{1,0:T(8,128)(2,1)S(1)}, bf16[112,1024]{1,0:T(8,128)(2,1)S(1)}, u32[]{:S(2)}, u32[]{:S(2)}) collective-permute-start(bf16[112,1024]{1,0:T(8,128)(2,1)S(1)} %copy-done.5), channel_id=1, source_target_pairs={{0,2},{1,3},{2,0},{3,1},{4,6},{5,7},{6,4},{7,5},{8,10},{9,11},{10,... | collective-permute-start | bytes 688136 | tf_op jit(solution)/shard_map/ppermute | solution.py:67
  25.6 11.2 %collective-permute-start.5 = (bf16[112,1024]{1,0:T(8,128)(2,1)S(1)}, bf16[112,1024]{1,0:T(8,128)(2,1)S(1)}, u32[]{:S(2)}, u32[]{:S(2)}) collective-permute-start(bf16[112,1024]{1,0:T(8,128)(2,1)S(1)} %copy-done.5), channel_id=1, source_target_pairs={{0,1},{1,2},{2,3},{3,0},{4,5},{5,6},{6,7},{7,4},{8,9},{9,10},{10,1... | collective-permute-start | bytes 688136 | tf_op jit(solution)/shard_map/ppermute | solution.py:67
  37.6 23.2 %collective-permute-start.8 = (bf16[448,1024]{1,0:T(8,128)(2,1)S(1)}, bf16[448,1024]{1,0:T(8,128)(2,1)S(1)}, u32[]{:S(2)}, u32[]{:S(2)}) collective-permute-start(bf16[448,1024]{1,0:T(8,128)(2,1)S(1)} %get-tuple-element.23), channel_id=1, source_target_pairs={{0,8},{8,0},{16,24},{24,16},{1,9},{9,1},{17,25},{25,17},{2,10},{10... | collective-permute-start | bytes 2752520 | tf_op jit(solution)/shard_map/ppermute | solution.py:69
  39.1 41.4 %collective-permute-start.9 = (bf16[448,1024]{1,0:T(8,128)(2,1)S(1)}, bf16[448,1024]{1,0:T(8,128)(2,1)S(1)}, u32[]{:S(2)}, u32[]{:S(2)}) collective-permute-start(bf16[448,1024]{1,0:T(8,128)(2,1)S(1)} %get-tuple-element.23), channel_id=1, source_target_pairs={{0,24},{8,16},{16,8},{24,0},{1,25},{9,17},{17,9},{25,1},{2,26},{10... | collective-permute-start | bytes 2752520 | tf_op jit(solution)/shard_map/ppermute | solution.py:69
  41.3 40.7 %collective-permute-start.6 = (bf16[448,1024]{1,0:T(8,128)(2,1)S(1)}, bf16[448,1024]{1,0:T(8,128)(2,1)S(1)}, u32[]{:S(2)}, u32[]{:S(2)}) collective-permute-start(bf16[448,1024]{1,0:T(8,128)(2,1)S(1)} %get-tuple-element.23), channel_id=1, source_target_pairs={{0,16},{8,24},{16,0},{24,8},{1,17},{9,25},{17,1},{25,9},{2,18},{10... | collective-permute-start | bytes 2752520 | tf_op jit(solution)/shard_map/ppermute | solution.py:69
  83.0 4.4 %collective-permute-start.7 = (bf16[896,1024]{1,0:T(8,128)(2,1)}, bf16[896,1024]{1,0:T(8,128)(2,1)}, u32[]{:S(2)}, u32[]{:S(2)}) collective-permute-start(bf16[896,1024]{1,0:T(8,128)(2,1)} %constant_dynamic-update-slice_fusion.4), channel_id=1, source_target_pairs={{0,4},{4,0},{1,5},{5,1},{2,6},{6,2},{3,7},{7,3},{8,12},{12,8},{9,1... | collective-permute-start | bytes 5505032 | tf_op jit(solution)/shard_map/ppermute | solution.py:71
  130.2 19.9 %collective-permute-start.12 = (bf16[896,8,56]{0,2,1:T(8,128)(2,1)}, bf16[896,8,56]{0,2,1:T(8,128)(2,1)}, u32[]{:S(2)}, u32[]{:S(2)}) collective-permute-start(bf16[896,8,56]{0,2,1:T(8,128)(2,1)} %fusion.23), channel_id=1, source_target_pairs={{0,8},{8,0},{1,9},{9,1},{2,10},{10,2},{3,11},{11,3},{4,12},{12,4},... | collective-permute-start | bytes 2408456 | tf_op jit(solution)/shard_map/ppermute | solution.py:76
  131.7 46.2 %collective-permute-start.11 = (bf16[896,8,56]{0,2,1:T(8,128)(2,1)}, bf16[896,8,56]{0,2,1:T(8,128)(2,1)}, u32[]{:S(2)}, u32[]{:S(2)}) collective-permute-start(bf16[896,8,56]{0,2,1:T(8,128)(2,1)} %fusion.23), channel_id=1, source_target_pairs={{0,4},{4,0},{1,5},{5,1},{2,6},{6,2},{3,7},{7,3},{8,12},{12,8},{9,1... | collective-permute-start | bytes 2408456 | tf_op jit(solution)/shard_map/ppermute | solution.py:77
  150.2 27.7 %collective-permute-start.13 = (bf16[896,8,56]{0,2,1:T(8,128)(2,1)}, bf16[896,8,56]{0,2,1:T(8,128)(2,1)}, u32[]{:S(2)}, u32[]{:S(2)}) collective-permute-start(bf16[896,8,56]{0,2,1:T(8,128)(2,1)} %collective-permute-done.12), channel_id=1, source_target_pairs={{0,4},{4,0},{1,5},{5,1},{2,6},{6,2},{3,7},{7,3},{8,12},{12,8},{9,1... | collective-permute-start | bytes 2408456 | tf_op jit(solution)/shard_map/ppermute | solution.py:77
  184.3 8.3 %collective-permute-start.14 = (f32[8,4,56]{2,0,1:T(8,128)S(1)}, f32[8,4,56]{2,0,1:T(8,128)S(1)}, u32[]{:S(2)}, u32[]{:S(2)}) collective-permute-start(f32[8,4,56]{2,0,1:T(8,128)S(1)} %convert_reduce_fusion), channel_id=1, source_target_pairs={{0,32},{32,0},{64,96},{96,64},{128,160},{160,128},{192,224},{224,1... | collective-permute-start | bytes 21512 | tf_op jit(solution)/shard_map/ppermute | solution.py:33
  192.6 4.7 %collective-permute-start.15 = (f32[8,4,56]{2,0,1:T(8,128)S(1)}, f32[8,4,56]{2,0,1:T(8,128)S(1)}, u32[]{:S(2)}, u32[]{:S(2)}) collective-permute-start(f32[8,4,56]{2,0,1:T(8,128)S(1)} %add.120), channel_id=1, source_target_pairs={{0,64},{32,96},{64,0},{96,32},{128,192},{160,224},{192,128},{224,1... | collective-permute-start | bytes 21512 | tf_op jit(solution)/shard_map/ppermute | solution.py:33
  197.4 7.6 %collective-permute-start.16 = (f32[8,4,56]{2,0,1:T(8,128)S(1)}, f32[8,4,56]{2,0,1:T(8,128)S(1)}, u32[]{:S(2)}, u32[]{:S(2)}) collective-permute-start(f32[8,4,56]{2,0,1:T(8,128)S(1)} %add.121), channel_id=1, source_target_pairs={{0,128},{32,160},{64,192},{96,224},{128,0},{160,32},{192,64},{224,... | collective-permute-start | bytes 21512 | tf_op jit(solution)/shard_map/ppermute | solution.py:33
  206.9 8.4 %collective-permute-start.19 = (bf16[120,1024]{1,0:T(8,128)(2,1)S(1)}, bf16[120,1024]{1,0:T(8,128)(2,1)S(1)}, u32[]{:S(2)}, u32[]{:S(2)}) collective-permute-start(bf16[120,1024]{1,0:T(8,128)(2,1)S(1)} %fusion.34), channel_id=1, source_target_pairs={{0,1},{1,2},{2,3},{3,0},{16,17},{17,18},{18,19},{19,16},{4,5},{5,6... | collective-permute-start | bytes 737288 | tf_op jit(solution)/shard_map/ppermute | solution.py:103
  208.4 15.3 %collective-permute-start.20 = (bf16[120,1024]{1,0:T(8,128)(2,1)S(1)}, bf16[120,1024]{1,0:T(8,128)(2,1)S(1)}, u32[]{:S(2)}, u32[]{:S(2)}) collective-permute-start(bf16[120,1024]{1,0:T(8,128)(2,1)S(1)} %fusion.35), channel_id=1, source_target_pairs={{0,2},{1,3},{2,0},{3,1},{16,18},{17,19},{18,16},{19,17},{4,6},{5,7... | collective-permute-start | bytes 737288 | tf_op jit(solution)/shard_map/ppermute | solution.py:103
  209.3 14.3 %collective-permute-start.21 = (bf16[120,1024]{1,0:T(8,128)(2,1)S(1)}, bf16[120,1024]{1,0:T(8,128)(2,1)S(1)}, u32[]{:S(2)}, u32[]{:S(2)}) collective-permute-start(bf16[120,1024]{1,0:T(8,128)(2,1)S(1)} %fusion.36), channel_id=1, source_target_pairs={{0,3},{1,0},{2,1},{3,2},{16,19},{17,16},{18,17},{19,18},{4,7},{5,4... | collective-permute-start | bytes 737288 | tf_op jit(solution)/shard_map/ppermute | solution.py:103
  210.6 13.6 %collective-permute-start.22 = (bf16[120,1024]{1,0:T(8,128)(2,1)S(1)}, bf16[120,1024]{1,0:T(8,128)(2,1)S(1)}, u32[]{:S(2)}, u32[]{:S(2)}) collective-permute-start(bf16[120,1024]{1,0:T(8,128)(2,1)S(1)} %fusion.37), channel_id=1, source_target_pairs={{0,16},{1,17},{2,18},{3,19},{16,0},{17,1},{18,2},{19,3},{4,20},{5,... | collective-permute-start | bytes 737288 | tf_op jit(solution)/shard_map/ppermute | solution.py:103
  213.8 10.4 %collective-permute-start.23 = (bf16[120,1024]{1,0:T(8,128)(2,1)S(1)}, bf16[120,1024]{1,0:T(8,128)(2,1)S(1)}, u32[]{:S(2)}, u32[]{:S(2)}) collective-permute-start(bf16[120,1024]{1,0:T(8,128)(2,1)S(1)} %fusion.38), channel_id=1, source_target_pairs={{0,17},{1,18},{2,19},{3,16},{16,1},{17,2},{18,3},{19,0},{4,21},{5,... | collective-permute-start | bytes 737288 | tf_op jit(solution)/shard_map/ppermute | solution.py:103
  215.3 12.5 %collective-permute-start.24 = (bf16[120,1024]{1,0:T(8,128)(2,1)S(1)}, bf16[120,1024]{1,0:T(8,128)(2,1)S(1)}, u32[]{:S(2)}, u32[]{:S(2)}) collective-permute-start(bf16[120,1024]{1,0:T(8,128)(2,1)S(1)} %fusion.39), channel_id=1, source_target_pairs={{0,18},{1,19},{2,16},{3,17},{16,2},{17,3},{18,0},{19,1},{4,22},{5,... | collective-permute-start | bytes 737288 | tf_op jit(solution)/shard_map/ppermute | solution.py:103
  223.6 8.6 %collective-permute-start.25 = (bf16[120,1024]{1,0:T(8,128)(2,1)S(1)}, bf16[120,1024]{1,0:T(8,128)(2,1)S(1)}, u32[]{:S(2)}, u32[]{:S(2)}) collective-permute-start(bf16[120,1024]{1,0:T(8,128)(2,1)S(1)} %fusion.40), channel_id=1, source_target_pairs={{0,19},{1,16},{2,17},{3,18},{16,3},{17,0},{18,1},{19,2},{4,23},{5,... | collective-permute-start | bytes 737288 | tf_op jit(solution)/shard_map/ppermute | solution.py:103
  (11 other events, 89.7 us)
Sparse Core Ops, SparseCore 0:
  22.3 87.2 all-gather.6
  111.4 48.4 all-gather.8

commit v2 on v0

v2 whole, which is shorter than its diff:
```python
import functools
import math

import jax
import jax.numpy as jnp
import numpy as np
from jax import lax
from jax.experimental import pallas as pl
from jax.experimental.pallas import tpu as pltpu
from jax.sharding import Mesh, PartitionSpec as P

ROW = ("yl", "c")
EXTRA = 8
MINOR = (((1,), (1,)), ((), ()))
MAJOR = (((0,), (0,)), ((), ()))
F32 = jnp.float32
BF16 = jnp.bfloat16


def shift(n, step):
    return [(i, (i + step) % n) for i in range(n)]


def flip(n, mask):
    return [(i, i ^ mask) for i in range(n)]


def sum_over(value, axis, n):
    mask = 1
    while mask < n:
        value = value + lax.ppermute(value, axis, flip(n, mask))
        mask *= 2
    return value


def hidden_kernel(*refs):
    x_refs, weights_ref, out_ref = refs[:8], refs[8], refs[9]
    count, part = out_ref.shape[:2]
    depth = x_refs[0].shape[1]
    total = None
    for k in range(4):
        near = 4 * (k % 2) + k // 2
        x = jnp.concatenate([x_refs[near][...], x_refs[near + 2][...]])
        weights = weights_ref[:, pl.ds(k * depth, depth)]
        product = lax.dot_general(weights, x, MINOR, preferred_element_type=F32)
        total = product if total is None else total + product
    for j in range(count):
        gate = total[2 * part * j : 2 * part * j + part]
        up = total[2 * part * j + part : 2 * part * (j + 1)]
        out_ref[j] = (gate / (1.0 + jnp.exp(-gate)) * up).astype(BF16)


def hidden_units(mine, other, weights):
    count, units, wide = weights.shape
    total = 2 * mine[0].shape[0]
    return pl.pallas_call(
        hidden_kernel,
        out_shape=jax.ShapeDtypeStruct((count, units // 2, total), BF16),
        compiler_params=pltpu.CompilerParams(vmem_limit_bytes=56 << 20),
        cost_estimate=pl.CostEstimate(
            flops=2 * count * units * total * wide,
            transcendentals=count * units * total // 2,
            bytes_accessed=2 * (total + count * units) * wide,
        ),
        name="hidden",
    )(*mine, *other, weights.reshape(count * units, wide))


def output_kernel(pieces, blocks, *refs):
    hidden_refs, (down_ref, units_ref, weights_ref) = refs[:pieces], refs[pieces : pieces + 3]
    out_refs, (total, col, row) = refs[pieces + 3 : -3], refs[-3:]
    units = sum(r.shape[0] for r in hidden_refs)
    width = down_ref.shape[1]
    rows = total.shape[0] // blocks

    @pl.when(pl.program_id(0) == 0)
    def _():
        for sums in (total, col, row):
            sums[...] = jnp.zeros_like(sums)

    def fold(value):
        return jnp.sum(value.reshape(units // 8, 8, value.shape[1]), axis=0)

    hidden = jnp.concatenate([r[...].astype(F32) for r in hidden_refs])
    down = down_ref[pl.ds(0, units), :]
    total[...] += lax.dot_general(hidden.astype(BF16), down, MAJOR, preferred_element_type=F32)
    col[...] += fold(units_ref[...] * down.astype(F32))
    row[...] += fold(weights_ref[...] * hidden)

    @pl.when(pl.program_id(0) == pl.num_programs(0) - 1)
    def _():
        lines = []
        for sums in (col, row):
            value = jnp.sum(sums[...], axis=0, keepdims=True)
            high = value.astype(BF16).astype(F32)
            for line in (high, value - high):
                short = width - line.shape[1]
                if short:
                    line = jnp.concatenate([line, jnp.zeros((1, short), F32)], axis=1)
                lines.append(line)
        lines.append(jnp.zeros((EXTRA - len(lines), width), F32))
        lines = jnp.concatenate(lines).astype(BF16)
        for j in range(blocks):
            out_refs[j][pl.ds(0, rows), :] = total[pl.ds(j * rows, rows), :].astype(BF16)
            out_refs[j][pl.ds(rows, EXTRA), :] = lines


def outputs(hidden, down, unit_sums, weight_sums, blocks):
    steps, _, total = hidden[0].shape
    units = sum(h.shape[1] for h in hidden)
    width = down.shape[2]
    operands = [*hidden, down, unit_sums, weight_sums]
    piece = (total // blocks + EXTRA, width)
    return pl.pallas_call(
        functools.partial(output_kernel, len(hidden), blocks),
        out_shape=[jax.ShapeDtypeStruct(piece, BF16)] * blocks,
        grid=(steps,),
        in_specs=[pl.BlockSpec((None, *a.shape[1:]), lambda s: (s, 0, 0)) for a in operands],
        out_specs=[pl.BlockSpec(piece, lambda s: (0, 0))] * blocks,
        scratch_shapes=[
            pltpu.VMEM((total, width), F32),
            pltpu.VMEM((8, width), F32),
            pltpu.VMEM((8, total), F32),
        ],
        compiler_params=pltpu.CompilerParams(vmem_limit_bytes=48 << 20),
        cost_estimate=pl.CostEstimate(
            flops=2 * steps * units * total * width,
            transcendentals=0,
            bytes_accessed=2 * steps * units * (total + width) + 2 * total * width,
        ),
        name="outputs",
    )(*operands)


def per_device(tokens, gate_up, down_weight):
    rows, width = tokens.shape
    units = gate_up.shape[2]
    nz, nx, nyh, nyl, nrow = (lax.axis_size(a) for a in ("z", "x", "yh", "yl", ROW))
    part = units // nrow
    total_tokens = rows * nz * nx * nyh
    model_width = width * nrow
    own = lax.axis_index(ROW)

    def across(array, mask):
        return lax.ppermute(array, ("yh", "yl"), flip(nyh * nyl, mask))

    def swap(array):
        return lax.ppermute(array, "c", flip(2, 1))

    pieces = jnp.swapaxes(gate_up, 1, 2).reshape(2, nrow, part, width)
    weights = []
    for k in range(nrow):
        piece = lax.dynamic_index_in_dim(pieces, own ^ k, 1, keepdims=False)
        piece = piece.reshape(2 * part, width)
        weights.append(piece if k == 0 else lax.ppermute(piece, ROW, flip(nrow, k)))
    weights = lax.all_gather(jnp.concatenate(weights, axis=1), "z", axis=0, tiled=False)

    def ordered(array):
        array = array.reshape(nrow, part, -1)
        array = jnp.concatenate(
            [lax.dynamic_slice_in_dim(array, own ^ k, 1, 0) for k in range(nrow)]
        )
        return array.reshape(units, -1)

    sums = jnp.sum(down_weight.astype(F32), axis=1)
    sums = ordered(sum_over(sum_over(sums, "c", 2), "yl", 2)).reshape(1, units)
    high = lax.reduce_precision(sums, 8, 7)
    middle = lax.reduce_precision(sums - high, 8, 7)
    lines = jnp.concatenate([high, middle, sums - high - middle]).astype(BF16)
    lines = jnp.pad(lines, ((0, EXTRA - 3), (0, width - units)))
    down = jnp.concatenate([ordered(down_weight), lines])
    down = lax.all_gather(down, "z", axis=0, tiled=False)

    mine = jnp.concatenate(
        [tokens] + [lax.ppermute(tokens, "x", shift(nx, -k)) for k in range(1, nx)]
    )
    mine = [mine] + [across(mine, k) for k in range(1, nyh * nyl)]
    other = [swap(m) for m in mine]

    hidden = hidden_units(mine, other, weights)
    far = lax.ppermute(hidden, "yl", flip(2, 1))
    hidden = [hidden, swap(hidden), far, swap(far)]
    unit_sums = jnp.concatenate([jnp.sum(h.astype(F32), axis=2) for h in hidden], axis=1)
    unit_sums = sum_over(unit_sums, "z", nz)[:, :, None]
    weight_sums = jnp.sum(down[:, units : units + 3, :units].astype(F32), axis=1)[:, :, None]

    targets = [(dy, dx) for dy in range(nyh) for dx in range(nx)]
    received = []
    for (dy, dx), piece in zip(
        targets, outputs(hidden, down, unit_sums, weight_sums, len(targets))
    ):
        perm = [(h * nx + i, (h ^ dy) * nx + (i + dx) % nx) for h in range(nyh) for i in range(nx)]
        if dx or dy:
            piece = lax.ppermute(piece, ("yh", "x"), perm)
        received.append(piece.astype(F32))
    mixed = sum(p[:rows] for p in received).astype(BF16)
    lines = sum(p[rows : rows + 2] for p in received)
    col_check = (lines[0] + lines[1]) / math.sqrt(total_tokens)
    row_check = 0.0
    for j, piece in enumerate(received):
        line = piece[rows + 2, j * rows : (j + 1) * rows] + piece[rows + 3, j * rows : (j + 1) * rows]
        row_check = row_check + line
    return (mixed, col_check, row_check / math.sqrt(model_width))


def solution(mesh):
    shape = mesh.shape
    sizes = (shape["dp"] // 2, 2, shape["row"] // 2, 2, shape["col"])
    fine = Mesh(np.asarray(mesh.devices).reshape(sizes), ("z", "yh", "yl", "c", "x"))
    batch = ("z", "yh", "x")
    return jax.shard_map(
        per_device,
        mesh=fine,
        in_specs=(P(batch, ROW), P(None, ROW, batch), P(batch, ROW)),
        out_specs=(P(batch, ROW), P(ROW), P(batch)),
        check_vma=False,
    )
```

time: 749 us -> 217 us (0.29)
  waiting for transfers between devices: 473 us -> 137 us
  blocking collectives: 205 us -> 0 us
  matrix products: 38.7 us -> 0 us
  starting transfers between devices: 0.2 us -> 27.8 us
  Pallas kernels: 0 us -> 22.6 us
    all_gather x3 -> x2, waiting for transfers between devices: 357 us -> 20.9 us  [the longest x1 18.2 us: per_device(): lax.all_gather(jnp.concatenate(weights, axis=1), 'z', axis=0, tiled=False)]
    psum x2 -> x0, blocking collectives: 183 us -> none  [the longest x1 176 us: per_device(): col_check = lax.psum(column_part, ('dp', 'col')) / math.sqrt(total_tokens)]
    ppermute x0 -> x28, waiting for transfers between devices: none -> 116 us  [the longest x3 42.2 us: across(): return lax.ppermute(array, ('yh', 'yl'), flip(nyh * nyl, mask))]
    reduce_scatter x2 -> x0, waiting for transfers between devices: 114 us -> none  [the longest x1 114 us: hidden_units(): lax.psum_scatter(partial_value, 'row', scatter_dimension=0, tiled=True)]
    dot_general x4 -> x0, matrix products: 38.7 us -> none  [the longest x1 22.2 us: per_device(): jnp.einsum('td,gdf->tgf', group_rows, lax.all_gather(gate_up, 'dp', axis=...]
    ppermute x0 -> x28, starting transfers between devices: none -> 27.7 us  [the longest x7 8.08 us: per_device(): piece = lax.ppermute(piece, ('yh', 'x'), perm)]
    pallas_call x0 -> x2, Pallas kernels: none -> 22.6 us  [the longest x1 14 us: hidden_units(): pl.pallas_call(hidden_kernel, out_shape=jax.ShapeDtypeStruct((count, unit...]
    all_gather x1 -> x0, blocking collectives: 14.6 us -> none  [per_device(): group_rows = lax.all_gather(tokens, 'col', axis=0, tiled=True)]
  transfers between devices with their start and end apart: 5 -> 30, of which waited for: 4 -> 23; matrix products, arithmetic and copies ran while one was open for 2% -> 3% of each run, Pallas kernels for 0% -> 6%
where the time goes in v2:
time: 217 us; the launch traced here: 216 us
  waiting for transfers between devices  137 us (63%)
  starting transfers between devices  27.8 us (13%)
  Pallas kernels  22.6 us (10%)
  between operations  14.4 us (7%)
  local copies, waits for them, and re-layouts  7.75 us (4%)
  other arithmetic  7.32 us (3%)
    ppermute x3, waiting for transfers between devices, across(): return lax.ppermute(array, ('yh', 'yl'), flip(nyh * nyl, mask))  42.2 us
    ppermute x7, waiting for transfers between devices, per_device(): piece = lax.ppermute(piece, ('yh', 'x'), perm)  25.5 us
    ppermute x1, waiting for transfers between devices, per_device(): far = lax.ppermute(hidden, 'yl', flip(2, 1))  18.4 us
    all_gather x1, waiting for transfers between devices, per_device(): lax.all_gather(jnp.concatenate(weights, axis=1), 'z', axis=0, tiled=False)  18.2 us
    pallas_call x1, Pallas kernels, hidden_units(): pl.pallas_call(hidden_kernel, out_shape=jax.ShapeDtypeStruct((count, unit...  14 us
    ppermute x3, waiting for transfers between devices, per_device(): weights.append(piece if k == 0 else lax.ppermute(piece, ROW, flip(nrow, k)))  10.6 us
    ppermute x5, waiting for transfers between devices, sum_over(): value = value + lax.ppermute(value, axis, flip(n, mask))  9.83 us
    pallas_call x1, Pallas kernels, outputs(): pl.pallas_call(functools.partial(output_kernel, len(hidden), blocks), out...  8.63 us
  transfers between devices with their start and end apart: 30, of which 23 were waited for; matrix products, arithmetic and copies ran while one was open for 3% of the time, Pallas kernels for 6%

profile of v2, /device:TPU:4, one launch (start us, length us, event | category | flops | bytes accessed | tf_op | source)
XLA Modules:
  0.0 216.4 jit_solution(14315088410202075188)
XLA Ops:
  8.7 1.7 collective-permute-start.11
  10.6 6.6 %collective-permute-done.11 = bf16[112,1024]{1,0:T(8,128)(2,1)S(1)} collective-permute-done((bf16[112,1024]{1,0:T(8,128)(2,1)S(1)}, bf16[112,1024]{1,0:T(8,128)(2,1)S(1)}, u32[]{:S(2)}, u32[]{:S(2)}) %collective-permute-start.11) | collective-permute-done | bytes 229408 | tf_op jit(solution)/shard_map/ppermute | solution.py:155
  17.2 4.0 %collective-permute-done.12 = bf16[112,1024]{1,0:T(8,128)(2,1)S(1)} collective-permute-done((bf16[112,1024]{1,0:T(8,128)(2,1)S(1)}, bf16[112,1024]{1,0:T(8,128)(2,1)S(1)}, u32[]{:S(2)}, u32[]{:S(2)}) %collective-permute-start.12) | collective-permute-done | bytes 229408 | tf_op jit(solution)/shard_map/ppermute | solution.py:155
  25.3 1.9 collective-permute-done.17
  28.9 2.7 %collective-permute-start.1 = (bf16[112,1024]{1,0:T(8,128)(2,1)S(1)}, bf16[112,1024]{1,0:T(8,128)(2,1)S(1)}, u32[]{:S(2)}, u32[]{:S(2)}) collective-permute-start(bf16[112,1024]{1,0:T(8,128)(2,1)S(1)} %copy-done.4), channel_id=1, source_target_pairs={{0,2},{1,3},{2,0},{3,1},{4,6},{5,7},{6,4},{7,5},{8,10},{9,11},{10,... | collective-permute-start | bytes 688136 | tf_op jit(solution)/shard_map/ppermute | solution.py:175
  33.3 3.7 %collective-permute-done = bf16[112,1024]{1,0:T(8,128)(2,1)S(1)} collective-permute-done((bf16[112,1024]{1,0:T(8,128)(2,1)S(1)}, bf16[112,1024]{1,0:T(8,128)(2,1)S(1)}, u32[]{:S(2)}, u32[]{:S(2)}) %collective-permute-start) | collective-permute-done | bytes 229408 | tf_op jit(solution)/shard_map/ppermute | solution.py:175
  36.9 2.1 collective-permute-done.1
  39.0 2.7 %collective-permute-done.2 = bf16[112,1024]{1,0:T(8,128)(2,1)S(1)} collective-permute-done((bf16[112,1024]{1,0:T(8,128)(2,1)S(1)}, bf16[112,1024]{1,0:T(8,128)(2,1)S(1)}, u32[]{:S(2)}, u32[]{:S(2)}) %collective-permute-start.2) | collective-permute-done | bytes 229408 | tf_op jit(solution)/shard_map/ppermute | solution.py:175
  43.4 2.9 %collective-permute-start.4 = (bf16[448,1024]{1,0:T(8,128)(2,1)S(1)}, bf16[448,1024]{1,0:T(8,128)(2,1)S(1)}, u32[]{:S(2)}, u32[]{:S(2)}) collective-permute-start(bf16[448,1024]{1,0:T(8,128)(2,1)S(1)} %constant_dynamic-update-slice_fusion.refs_0_), channel_id=1, source_target_pairs={{0,16},{8,24},{16,0},{24,8},{1,17},{9,25},{17,1},{25,9},{2,18},{10... | collective-permute-start | bytes 2752520 | tf_op jit(solution)/shard_map/ppermute | solution.py:145
  46.5 18.5 %collective-permute-done.3.refs_1_ = bf16[448,1024]{1,0:T(8,128)(2,1)S(1)} collective-permute-done((bf16[448,1024]{1,0:T(8,128)(2,1)S(1)}, bf16[448,1024]{1,0:T(8,128)(2,1)S(1)}, u32[]{:S(2)}, u32[]{:S(2)}) %collective-permute-start.3) | collective-permute-done | bytes 917536 | tf_op jit(solution)/shard_map/ppermute | solution.py:145
  65.0 21.2 %collective-permute-done.4.refs_2_ = bf16[448,1024]{1,0:T(8,128)(2,1)S(1)} collective-permute-done((bf16[448,1024]{1,0:T(8,128)(2,1)S(1)}, bf16[448,1024]{1,0:T(8,128)(2,1)S(1)}, u32[]{:S(2)}, u32[]{:S(2)}) %collective-permute-start.4) | collective-permute-done | bytes 917536 | tf_op jit(solution)/shard_map/ppermute | solution.py:145
  86.2 2.6 %collective-permute-done.5.refs_3_ = bf16[448,1024]{1,0:T(8,128)(2,1)S(1)} collective-permute-done((bf16[448,1024]{1,0:T(8,128)(2,1)S(1)}, bf16[448,1024]{1,0:T(8,128)(2,1)S(1)}, u32[]{:S(2)}, u32[]{:S(2)}) %collective-permute-start.5) | collective-permute-done | bytes 917536 | tf_op jit(solution)/shard_map/ppermute | solution.py:145
  91.4 18.2 %all-gather.5.cloned.1.call-done.refs_8_ = bf16[896,4096]{1,0:T(8,128)(2,1)} async-done(((bf16[112,4096]{1,0:T(8,128)(2,1)}), bf16[896,4096]{1,0:T(8,128)(2,1)}) %all-gather.5.cloned.1.call-update) | async-done | bytes 7340048 | tf_op jit(solution)/shard_map/all_gather | solution.py:156
  109.6 14.0 %hidden.1.refs_0_ = bf16[8,56,896]{2,1,0:T(8,128)(2,1)} custom-call(bf16[448,1024]{1,0:T(8,128)(2,1)} %copy-done.5, bf16[448,1024]{1,0:T(8,128)(2,1)} %copy-done.6, bf16[448,1024]{1,0:T(8,128)(2,1)} %copy-done.7, bf16[448,1024]{1,0:T(8,128)(2,1)} %copy-done.8, bf16[448,1024]{1,0:T(8,128)(2,1)} %copy-done.9, bf16[448,1024]{1,0:T(8,128)(2,1)} %copy-done.10, ...), custom_call_target="tpu_custom_call" | custom-call | flops 6576668672 | bytes 14680064 | tf_op jit(solution)/shard_map/hidden/pallas_call | solution.py:56
  125.1 18.4 %collective-permute-done.14.refs_2_ = bf16[8,56,896]{2,1,0:T(8,128)(2,1)S(1)} collective-permute-done((bf16[8,56,896]{2,1,0:T(8,128)(2,1)}, bf16[8,56,896]{2,1,0:T(8,128)(2,1)S(1)}, u32[]{:S(2)}, u32[]{:S(2)}) %collective-permute-start.14) | collective-permute-done | bytes 802848 | tf_op jit(solution)/shard_map/ppermute | solution.py:181
  147.0 3.8 %collective-permute-done.18 = f32[8,224]{1,0:T(8,128)S(1)} collective-permute-done((f32[8,224]{1,0:T(8,128)S(1)}, f32[8,224]{1,0:T(8,128)S(1)}, u32[]{:S(2)}, u32[]{:S(2)}) %collective-permute-start.18) | collective-permute-done | bytes 7200 | tf_op jit(solution)/shard_map/ppermute | solution.py:31
  152.2 3.3 %collective-permute-done.19 = f32[8,224]{1,0:T(8,128)S(1)} collective-permute-done((f32[8,224]{1,0:T(8,128)S(1)}, f32[8,224]{1,0:T(8,128)S(1)}, u32[]{:S(2)}, u32[]{:S(2)}) %collective-permute-start.19) | collective-permute-done | bytes 7200 | tf_op jit(solution)/shard_map/ppermute | solution.py:31
  155.5 3.1 %collective-permute-start.20 = (f32[8,224]{1,0:T(8,128)S(1)}, f32[8,224]{1,0:T(8,128)S(1)}, u32[]{:S(2)}, u32[]{:S(2)}) collective-permute-start(f32[8,224]{1,0:T(8,128)S(1)} %add.161), channel_id=1, source_target_pairs={{0,128},{32,160},{64,192},{96,224},{128,0},{160,32},{192,64},{224,... | collective-permute-start | bytes 21512 | tf_op jit(solution)/shard_map/ppermute | solution.py:31
  158.6 2.7 %all-gather.7.cloned.1.call-done = bf16[1856,1024]{1,0:T(8,128)(2,1)} async-done(((bf16[232,1024]{1,0:T(8,128)(2,1)}), bf16[1856,1024]{1,0:T(8,128)(2,1)}) %all-gather.7.cloned.1.call-update) | async-done | bytes 3801104 | tf_op jit(solution)/shard_map/all_gather | solution.py:172
  164.8 8.6 %outputs.1 = (bf16[120,1024]{1,0:T(8,128)(2,1)S(1)}, bf16[120,1024]{1,0:T(8,128)(2,1)S(1)}, bf16[120,1024]{1,0:T(8,128)(2,1)S(1)}, bf16[120,1024]{1,0:T(8,128)(2...) custom-call(bf16[8,56,896]{2,1,0:T(8,128)(2,1)S(1)} %copy-done, ...), custom_call_target="tpu_custom_call" | custom-call | flops 3288334336 | bytes 8716288 | tf_op jit(solution)/shard_map/outputs/pallas_call | solution.py:114
  176.9 3.0 %collective-permute-start.24 = (bf16[120,1024]{1,0:T(8,128)(2,1)S(1)}, bf16[120,1024]{1,0:T(8,128)(2,1)S(1)}, u32[]{:S(2)}, u32[]{:S(2)}) collective-permute-start(bf16[120,1024]{1,0:T(8,128)(2,1)S(1)} %get-tuple-element.15), channel_id=1, source_target_pairs={{0,16},{1,17},{2,18},{3,19},{16,0},{17,1},{18,2},{19,3},{4,20},{5,... | collective-permute-start | bytes 737288 | tf_op jit(solution)/shard_map/ppermute | solution.py:194
  180.8 5.6 %collective-permute-done.21 = bf16[120,1024]{1,0:T(8,128)(2,1)S(1)} collective-permute-done((bf16[120,1024]{1,0:T(8,128)(2,1)S(1)}, bf16[120,1024]{1,0:T(8,128)(2,1)S(1)}, u32[]{:S(2)}, u32[]{:S(2)}) %collective-permute-start.21) | collective-permute-done | bytes 245792 | tf_op jit(solution)/shard_map/ppermute | solution.py:194
  190.1 4.5 %collective-permute-done.25 = bf16[120,1024]{1,0:T(8,128)(2,1)S(1)} collective-permute-done((bf16[120,1024]{1,0:T(8,128)(2,1)S(1)}, bf16[120,1024]{1,0:T(8,128)(2,1)S(1)}, u32[]{:S(2)}, u32[]{:S(2)}) %collective-permute-start.25) | collective-permute-done | bytes 245792 | tf_op jit(solution)/shard_map/ppermute | solution.py:194
  194.6 11.1 %collective-permute-done.26 = bf16[120,1024]{1,0:T(8,128)(2,1)S(1)} collective-permute-done((bf16[120,1024]{1,0:T(8,128)(2,1)S(1)}, bf16[120,1024]{1,0:T(8,128)(2,1)S(1)}, u32[]{:S(2)}, u32[]{:S(2)}) %collective-permute-start.26) | collective-permute-done | bytes 245792 | tf_op jit(solution)/shard_map/ppermute | solution.py:194
  (105 shorter events, 35.4 us)
Async XLA Ops:
  7.2 102.4 %all-gather.5.cloned.1.call-start = ((), (), s32[]{:S(2)}) async-start(), calls=%async_computation | async-start | bytes 8257536 | tf_op jit(solution)/shard_map/all_gather | solution.py:156
  8.7 8.5 %collective-permute-start.11 = (bf16[112,1024]{1,0:T(8,128)(2,1)S(1)}, bf16[112,1024]{1,0:T(8,128)(2,1)S(1)}, u32[]{:S(2)}, u32[]{:S(2)}) collective-permute-start(bf16[112,1024]{1,0:T(8,128)(2,1)S(1)} %bitcast.31), channel_id=1, source_target_pairs={{0,8},{4,12},{8,0},{12,4},{1,9},{5,13},{9,1},{13,5},{2,10},{6,14},... | collective-permute-start | bytes 688136 | tf_op jit(solution)/shard_map/ppermute | solution.py:155
  10.4 10.8 %collective-permute-start.12 = (bf16[112,1024]{1,0:T(8,128)(2,1)S(1)}, bf16[112,1024]{1,0:T(8,128)(2,1)S(1)}, u32[]{:S(2)}, u32[]{:S(2)}) collective-permute-start(bf16[112,1024]{1,0:T(8,128)(2,1)S(1)} %bitcast.30), channel_id=1, source_target_pairs={{0,12},{4,8},{8,4},{12,0},{1,13},{5,9},{9,5},{13,1},{2,14},{6,10},... | collective-permute-start | bytes 688136 | tf_op jit(solution)/shard_map/ppermute | solution.py:155
  22.2 139.0 %all-gather.7.cloned.1.call-start = ((), (), s32[]{:S(2)}) async-start(), calls=%async_computation.1 | async-start | bytes 4276224 | tf_op jit(solution)/shard_map/all_gather | solution.py:172
  28.3 8.6 %collective-permute-start = (bf16[112,1024]{1,0:T(8,128)(2,1)S(1)}, bf16[112,1024]{1,0:T(8,128)(2,1)S(1)}, u32[]{:S(2)}, u32[]{:S(2)}) collective-permute-start(bf16[112,1024]{1,0:T(8,128)(2,1)S(1)} %copy-done.4), channel_id=1, source_target_pairs={{0,3},{1,0},{2,1},{3,2},{4,7},{5,4},{6,5},{7,6},{8,11},{9,8},{10,9... | collective-permute-start | bytes 688136 | tf_op jit(solution)/shard_map/ppermute | solution.py:175
  28.9 10.1 %collective-permute-start.1 = (bf16[112,1024]{1,0:T(8,128)(2,1)S(1)}, bf16[112,1024]{1,0:T(8,128)(2,1)S(1)}, u32[]{:S(2)}, u32[]{:S(2)}) collective-permute-start(bf16[112,1024]{1,0:T(8,128)(2,1)S(1)} %copy-done.4), channel_id=1, source_target_pairs={{0,2},{1,3},{2,0},{3,1},{4,6},{5,7},{6,4},{7,5},{8,10},{9,11},{10,... | collective-permute-start | bytes 688136 | tf_op jit(solution)/shard_map/ppermute | solution.py:175
  31.6 10.1 %collective-permute-start.2 = (bf16[112,1024]{1,0:T(8,128)(2,1)S(1)}, bf16[112,1024]{1,0:T(8,128)(2,1)S(1)}, u32[]{:S(2)}, u32[]{:S(2)}) collective-permute-start(bf16[112,1024]{1,0:T(8,128)(2,1)S(1)} %copy-done.4), channel_id=1, source_target_pairs={{0,1},{1,2},{2,3},{3,0},{4,5},{5,6},{6,7},{7,4},{8,9},{9,10},{10,1... | collective-permute-start | bytes 688136 | tf_op jit(solution)/shard_map/ppermute | solution.py:175
  41.7 23.3 %collective-permute-start.3 = (bf16[448,1024]{1,0:T(8,128)(2,1)S(1)}, bf16[448,1024]{1,0:T(8,128)(2,1)S(1)}, u32[]{:S(2)}, u32[]{:S(2)}) collective-permute-start(bf16[448,1024]{1,0:T(8,128)(2,1)S(1)} %constant_dynamic-update-slice_fusion.refs_0_), channel_id=1, source_target_pairs={{0,8},{8,0},{16,24},{24,16},{1,9},{9,1},{17,25},{25,17},{2,10},{10... | collective-permute-start | bytes 2752520 | tf_op jit(solution)/shard_map/ppermute | solution.py:145
  43.4 42.8 %collective-permute-start.4 = (bf16[448,1024]{1,0:T(8,128)(2,1)S(1)}, bf16[448,1024]{1,0:T(8,128)(2,1)S(1)}, u32[]{:S(2)}, u32[]{:S(2)}) collective-permute-start(bf16[448,1024]{1,0:T(8,128)(2,1)S(1)} %constant_dynamic-update-slice_fusion.refs_0_), channel_id=1, source_target_pairs={{0,16},{8,24},{16,0},{24,8},{1,17},{9,25},{17,1},{25,9},{2,18},{10... | collective-permute-start | bytes 2752520 | tf_op jit(solution)/shard_map/ppermute | solution.py:145
  46.3 42.5 %collective-permute-start.5 = (bf16[448,1024]{1,0:T(8,128)(2,1)S(1)}, bf16[448,1024]{1,0:T(8,128)(2,1)S(1)}, u32[]{:S(2)}, u32[]{:S(2)}) collective-permute-start(bf16[448,1024]{1,0:T(8,128)(2,1)S(1)} %constant_dynamic-update-slice_fusion.refs_0_), channel_id=1, source_target_pairs={{0,24},{8,16},{16,8},{24,0},{1,25},{9,17},{17,9},{25,1},{2,26},{10... | collective-permute-start | bytes 2752520 | tf_op jit(solution)/shard_map/ppermute | solution.py:145
  46.5 42.3 %collective-permute-start.6 = (bf16[448,1024]{1,0:T(8,128)(2,1)S(1)}, bf16[448,1024]{1,0:T(8,128)(2,1)S(1)}, u32[]{:S(2)}, u32[]{:S(2)}) collective-permute-start(bf16[448,1024]{1,0:T(8,128)(2,1)S(1)} %constant_dynamic-update-slice_fusion.refs_0_), channel_id=1, source_target_pairs={{0,4},{4,0},{1,5},{5,1},{2,6},{6,2},{3,7},{7,3},{8,12},{12,8},{9,1... | collective-permute-start | bytes 2752520 | tf_op jit(solution)/shard_map/ppermute | solution.py:148
  65.0 23.8 %collective-permute-start.7 = (bf16[448,1024]{1,0:T(8,128)(2,1)S(1)}, bf16[448,1024]{1,0:T(8,128)(2,1)S(1)}, u32[]{:S(2)}, u32[]{:S(2)}) collective-permute-start(bf16[448,1024]{1,0:T(8,128)(2,1)S(1)} %collective-permute-done.3.refs_1_), channel_id=1, source_target_pairs={{0,4},{4,0},{1,5},{5,1},{2,6},{6,2},{3,7},{7,3},{8,12},{12,8},{9,1... | collective-permute-start | bytes 2752520 | tf_op jit(solution)/shard_map/ppermute | solution.py:148
  123.6 19.8 %collective-permute-start.14 = (bf16[8,56,896]{2,1,0:T(8,128)(2,1)}, bf16[8,56,896]{2,1,0:T(8,128)(2,1)S(1)}, u32[]{:S(2)}, u32[]{:S(2)}) collective-permute-start(bf16[8,56,896]{2,1,0:T(8,128)(2,1)} %hidden.1.refs_0_), channel_id=1, source_target_pairs={{0,8},{8,0},{1,9},{9,1},{2,10},{10,2},{3,11},{11,3},{4,12},{12,4},... | collective-permute-start | bytes 2408456 | tf_op jit(solution)/shard_map/ppermute | solution.py:181
  125.1 19.9 %collective-permute-start.13 = (bf16[8,56,896]{2,1,0:T(8,128)(2,1)}, bf16[8,56,896]{2,1,0:T(8,128)(2,1)S(1)}, u32[]{:S(2)}, u32[]{:S(2)}) collective-permute-start(bf16[8,56,896]{2,1,0:T(8,128)(2,1)} %hidden.1.refs_0_), channel_id=1, source_target_pairs={{0,4},{4,0},{1,5},{5,1},{2,6},{6,2},{3,7},{7,3},{8,12},{12,8},{9,1... | collective-permute-start | bytes 2408456 | tf_op jit(solution)/shard_map/ppermute | solution.py:148
  146.9 3.8 %collective-permute-start.18 = (f32[8,224]{1,0:T(8,128)S(1)}, f32[8,224]{1,0:T(8,128)S(1)}, u32[]{:S(2)}, u32[]{:S(2)}) collective-permute-start(f32[8,224]{1,0:T(8,128)S(1)} %pad_maximum_fusion.3), channel_id=1, source_target_pairs={{0,32},{32,0},{64,96},{96,64},{128,160},{160,128},{192,224},{224,1... | collective-permute-start | bytes 21512 | tf_op jit(solution)/shard_map/ppermute | solution.py:31
  150.8 4.7 %collective-permute-start.19 = (f32[8,224]{1,0:T(8,128)S(1)}, f32[8,224]{1,0:T(8,128)S(1)}, u32[]{:S(2)}, u32[]{:S(2)}) collective-permute-start(f32[8,224]{1,0:T(8,128)S(1)} %fusion.19), channel_id=1, source_target_pairs={{0,64},{32,96},{64,0},{96,32},{128,192},{160,224},{192,128},{224,1... | collective-permute-start | bytes 21512 | tf_op jit(solution)/shard_map/ppermute | solution.py:31
  155.5 7.8 %collective-permute-start.20 = (f32[8,224]{1,0:T(8,128)S(1)}, f32[8,224]{1,0:T(8,128)S(1)}, u32[]{:S(2)}, u32[]{:S(2)}) collective-permute-start(f32[8,224]{1,0:T(8,128)S(1)} %add.161), channel_id=1, source_target_pairs={{0,128},{32,160},{64,192},{96,224},{128,0},{160,32},{192,64},{224,... | collective-permute-start | bytes 21512 | tf_op jit(solution)/shard_map/ppermute | solution.py:31
  173.5 12.9 %collective-permute-start.21 = (bf16[120,1024]{1,0:T(8,128)(2,1)S(1)}, bf16[120,1024]{1,0:T(8,128)(2,1)S(1)}, u32[]{:S(2)}, u32[]{:S(2)}) collective-permute-start(bf16[120,1024]{1,0:T(8,128)(2,1)S(1)} %get-tuple-element.12), channel_id=1, source_target_pairs={{0,1},{1,2},{2,3},{3,0},{16,17},{17,18},{18,19},{19,16},{4,5},{5,6... | collective-permute-start | bytes 737288 | tf_op jit(solution)/shard_map/ppermute | solution.py:194
  174.9 13.0 %collective-permute-start.22 = (bf16[120,1024]{1,0:T(8,128)(2,1)S(1)}, bf16[120,1024]{1,0:T(8,128)(2,1)S(1)}, u32[]{:S(2)}, u32[]{:S(2)}) collective-permute-start(bf16[120,1024]{1,0:T(8,128)(2,1)S(1)} %get-tuple-element.13), channel_id=1, source_target_pairs={{0,2},{1,3},{2,0},{3,1},{16,18},{17,19},{18,16},{19,17},{4,6},{5,7... | collective-permute-start | bytes 737288 | tf_op jit(solution)/shard_map/ppermute | solution.py:194
  175.8 14.2 %collective-permute-start.23 = (bf16[120,1024]{1,0:T(8,128)(2,1)S(1)}, bf16[120,1024]{1,0:T(8,128)(2,1)S(1)}, u32[]{:S(2)}, u32[]{:S(2)}) collective-permute-start(bf16[120,1024]{1,0:T(8,128)(2,1)S(1)} %get-tuple-element.14), channel_id=1, source_target_pairs={{0,3},{1,0},{2,1},{3,2},{16,19},{17,16},{18,17},{19,18},{4,7},{5,4... | collective-permute-start | bytes 737288 | tf_op jit(solution)/shard_map/ppermute | solution.py:194
  176.9 13.1 %collective-permute-start.24 = (bf16[120,1024]{1,0:T(8,128)(2,1)S(1)}, bf16[120,1024]{1,0:T(8,128)(2,1)S(1)}, u32[]{:S(2)}, u32[]{:S(2)}) collective-permute-start(bf16[120,1024]{1,0:T(8,128)(2,1)S(1)} %get-tuple-element.15), channel_id=1, source_target_pairs={{0,16},{1,17},{2,18},{3,19},{16,0},{17,1},{18,2},{19,3},{4,20},{5,... | collective-permute-start | bytes 737288 | tf_op jit(solution)/shard_map/ppermute | solution.py:194
  180.0 14.6 %collective-permute-start.25 = (bf16[120,1024]{1,0:T(8,128)(2,1)S(1)}, bf16[120,1024]{1,0:T(8,128)(2,1)S(1)}, u32[]{:S(2)}, u32[]{:S(2)}) collective-permute-start(bf16[120,1024]{1,0:T(8,128)(2,1)S(1)} %get-tuple-element.16), channel_id=1, source_target_pairs={{0,17},{1,18},{2,19},{3,16},{16,1},{17,2},{18,3},{19,0},{4,21},{5,... | collective-permute-start | bytes 737288 | tf_op jit(solution)/shard_map/ppermute | solution.py:194
  186.4 19.3 %collective-permute-start.26 = (bf16[120,1024]{1,0:T(8,128)(2,1)S(1)}, bf16[120,1024]{1,0:T(8,128)(2,1)S(1)}, u32[]{:S(2)}, u32[]{:S(2)}) collective-permute-start(bf16[120,1024]{1,0:T(8,128)(2,1)S(1)} %get-tuple-element.17), channel_id=1, source_target_pairs={{0,18},{1,19},{2,16},{3,17},{16,2},{17,3},{18,0},{19,1},{4,22},{5,... | collective-permute-start | bytes 737288 | tf_op jit(solution)/shard_map/ppermute | solution.py:194
  187.9 19.4 %collective-permute-start.27 = (bf16[120,1024]{1,0:T(8,128)(2,1)S(1)}, bf16[120,1024]{1,0:T(8,128)(2,1)S(1)}, u32[]{:S(2)}, u32[]{:S(2)}) collective-permute-start(bf16[120,1024]{1,0:T(8,128)(2,1)S(1)} %get-tuple-element.18), channel_id=1, source_target_pairs={{0,19},{1,16},{2,17},{3,18},{16,3},{17,0},{18,1},{19,2},{4,23},{5,... | collective-permute-start | bytes 737288 | tf_op jit(solution)/shard_map/ppermute | solution.py:194
  (18 other events, 195.2 us)
Sparse Core Ops, SparseCore 0:
  22.3 87.2 all-gather.4
  111.4 49.8 all-gather.6

commit v3 on v2

--- a/solution.py
+++ b/solution.py
@@ -185,14 +185,15 @@
     weight_sums = jnp.sum(down[:, units : units + 3, :units].astype(F32), axis=1)[:, :, None]
 
     targets = [(dy, dx) for dy in range(nyh) for dx in range(nx)]
-    received = []
-    for (dy, dx), piece in zip(
-        targets, outputs(hidden, down, unit_sums, weight_sums, len(targets))
-    ):
+    far_first = sorted(range(len(targets)), key=lambda j: -2 * targets[j][0] - min(targets[j][1], nx - targets[j][1]))
+    sent = outputs(hidden, down, unit_sums, weight_sums, len(targets))
+    received = [None] * len(targets)
+    for j in far_first:
+        (dy, dx), piece = targets[j], sent[j]
         perm = [(h * nx + i, (h ^ dy) * nx + (i + dx) % nx) for h in range(nyh) for i in range(nx)]
         if dx or dy:
             piece = lax.ppermute(piece, ("yh", "x"), perm)
-        received.append(piece.astype(F32))
+        received[j] = piece.astype(F32)
     mixed = sum(p[:rows] for p in received).astype(BF16)
     lines = sum(p[rows : rows + 2] for p in received)
     col_check = (lines[0] + lines[1]) / math.sqrt(total_tokens)

time: 217 us -> 217 us (level)
  no operation moved by 1% of the time
where the time goes in v3:
time: 217 us; the launch traced here: 216 us
  waiting for transfers between devices  137 us (63%)
  starting transfers between devices  27.8 us (13%)
  Pallas kernels  22.6 us (10%)
  between operations  14.4 us (7%)
  local copies, waits for them, and re-layouts  7.75 us (4%)
  other arithmetic  7.32 us (3%)
    ppermute x3, waiting for transfers between devices, across(): return lax.ppermute(array, ('yh', 'yl'), flip(nyh * nyl, mask))  42.2 us
    ppermute x7, waiting for transfers between devices, per_device(): piece = lax.ppermute(piece, ('yh', 'x'), perm)  25.5 us
    ppermute x1, waiting for transfers between devices, per_device(): far = lax.ppermute(hidden, 'yl', flip(2, 1))  18.4 us
    all_gather x1, waiting for transfers between devices, per_device(): lax.all_gather(jnp.concatenate(weights, axis=1), 'z', axis=0, tiled=False)  18.2 us
    pallas_call x1, Pallas kernels, hidden_units(): pl.pallas_call(hidden_kernel, out_shape=jax.ShapeDtypeStruct((count, unit...  14 us
    ppermute x3, waiting for transfers between devices, per_device(): weights.append(piece if k == 0 else lax.ppermute(piece, ROW, flip(nrow, k)))  10.6 us
    ppermute x5, waiting for transfers between devices, sum_over(): value = value + lax.ppermute(value, axis, flip(n, mask))  9.83 us
    pallas_call x1, Pallas kernels, outputs(): pl.pallas_call(functools.partial(output_kernel, len(hidden), blocks), out...  8.63 us
  transfers between devices with their start and end apart: 30, of which 23 were waited for; matrix products, arithmetic and copies ran while one was open for 3% of the time, Pallas kernels for 6%

profile of v3, /device:TPU:4, one launch (start us, length us, event | category | flops | bytes accessed | tf_op | source)
XLA Modules:
  0.0 216.4 jit_solution(14315088410202075188)
XLA Ops:
  8.7 1.7 collective-permute-start.11
  10.6 6.6 %collective-permute-done.11 = bf16[112,1024]{1,0:T(8,128)(2,1)S(1)} collective-permute-done((bf16[112,1024]{1,0:T(8,128)(2,1)S(1)}, bf16[112,1024]{1,0:T(8,128)(2,1)S(1)}, u32[]{:S(2)}, u32[]{:S(2)}) %collective-permute-start.11) | collective-permute-done | bytes 229408 | tf_op jit(solution)/shard_map/ppermute | solution.py:155
  17.2 4.0 %collective-permute-done.12 = bf16[112,1024]{1,0:T(8,128)(2,1)S(1)} collective-permute-done((bf16[112,1024]{1,0:T(8,128)(2,1)S(1)}, bf16[112,1024]{1,0:T(8,128)(2,1)S(1)}, u32[]{:S(2)}, u32[]{:S(2)}) %collective-permute-start.12) | collective-permute-done | bytes 229408 | tf_op jit(solution)/shard_map/ppermute | solution.py:155
  25.3 1.9 collective-permute-done.17
  28.9 2.7 %collective-permute-start.1 = (bf16[112,1024]{1,0:T(8,128)(2,1)S(1)}, bf16[112,1024]{1,0:T(8,128)(2,1)S(1)}, u32[]{:S(2)}, u32[]{:S(2)}) collective-permute-start(bf16[112,1024]{1,0:T(8,128)(2,1)S(1)} %copy-done.4), channel_id=1, source_target_pairs={{0,2},{1,3},{2,0},{3,1},{4,6},{5,7},{6,4},{7,5},{8,10},{9,11},{10,... | collective-permute-start | bytes 688136 | tf_op jit(solution)/shard_map/ppermute | solution.py:175
  33.3 3.7 %collective-permute-done = bf16[112,1024]{1,0:T(8,128)(2,1)S(1)} collective-permute-done((bf16[112,1024]{1,0:T(8,128)(2,1)S(1)}, bf16[112,1024]{1,0:T(8,128)(2,1)S(1)}, u32[]{:S(2)}, u32[]{:S(2)}) %collective-permute-start) | collective-permute-done | bytes 229408 | tf_op jit(solution)/shard_map/ppermute | solution.py:175
  36.9 2.1 collective-permute-done.1
  39.0 2.7 %collective-permute-done.2 = bf16[112,1024]{1,0:T(8,128)(2,1)S(1)} collective-permute-done((bf16[112,1024]{1,0:T(8,128)(2,1)S(1)}, bf16[112,1024]{1,0:T(8,128)(2,1)S(1)}, u32[]{:S(2)}, u32[]{:S(2)}) %collective-permute-start.2) | collective-permute-done | bytes 229408 | tf_op jit(solution)/shard_map/ppermute | solution.py:175
  43.4 2.9 %collective-permute-start.4 = (bf16[448,1024]{1,0:T(8,128)(2,1)S(1)}, bf16[448,1024]{1,0:T(8,128)(2,1)S(1)}, u32[]{:S(2)}, u32[]{:S(2)}) collective-permute-start(bf16[448,1024]{1,0:T(8,128)(2,1)S(1)} %constant_dynamic-update-slice_fusion.refs_0_), channel_id=1, source_target_pairs={{0,16},{8,24},{16,0},{24,8},{1,17},{9,25},{17,1},{25,9},{2,18},{10... | collective-permute-start | bytes 2752520 | tf_op jit(solution)/shard_map/ppermute | solution.py:145
  46.5 18.5 %collective-permute-done.3.refs_1_ = bf16[448,1024]{1,0:T(8,128)(2,1)S(1)} collective-permute-done((bf16[448,1024]{1,0:T(8,128)(2,1)S(1)}, bf16[448,1024]{1,0:T(8,128)(2,1)S(1)}, u32[]{:S(2)}, u32[]{:S(2)}) %collective-permute-start.3) | collective-permute-done | bytes 917536 | tf_op jit(solution)/shard_map/ppermute | solution.py:145
  65.0 21.2 %collective-permute-done.4.refs_2_ = bf16[448,1024]{1,0:T(8,128)(2,1)S(1)} collective-permute-done((bf16[448,1024]{1,0:T(8,128)(2,1)S(1)}, bf16[448,1024]{1,0:T(8,128)(2,1)S(1)}, u32[]{:S(2)}, u32[]{:S(2)}) %collective-permute-start.4) | collective-permute-done | bytes 917536 | tf_op jit(solution)/shard_map/ppermute | solution.py:145
  86.2 2.6 %collective-permute-done.5.refs_3_ = bf16[448,1024]{1,0:T(8,128)(2,1)S(1)} collective-permute-done((bf16[448,1024]{1,0:T(8,128)(2,1)S(1)}, bf16[448,1024]{1,0:T(8,128)(2,1)S(1)}, u32[]{:S(2)}, u32[]{:S(2)}) %collective-permute-start.5) | collective-permute-done | bytes 917536 | tf_op jit(solution)/shard_map/ppermute | solution.py:145
  91.4 18.2 %all-gather.5.cloned.1.call-done.refs_8_ = bf16[896,4096]{1,0:T(8,128)(2,1)} async-done(((bf16[112,4096]{1,0:T(8,128)(2,1)}), bf16[896,4096]{1,0:T(8,128)(2,1)}) %all-gather.5.cloned.1.call-update) | async-done | bytes 7340048 | tf_op jit(solution)/shard_map/all_gather | solution.py:156
  109.6 14.0 %hidden.1.refs_0_ = bf16[8,56,896]{2,1,0:T(8,128)(2,1)} custom-call(bf16[448,1024]{1,0:T(8,128)(2,1)} %copy-done.5, bf16[448,1024]{1,0:T(8,128)(2,1)} %copy-done.6, bf16[448,1024]{1,0:T(8,128)(2,1)} %copy-done.7, bf16[448,1024]{1,0:T(8,128)(2,1)} %copy-done.8, bf16[448,1024]{1,0:T(8,128)(2,1)} %copy-done.9, bf16[448,1024]{1,0:T(8,128)(2,1)} %copy-done.10, ...), custom_call_target="tpu_custom_call" | custom-call | flops 6576668672 | bytes 14680064 | tf_op jit(solution)/shard_map/hidden/pallas_call | solution.py:56
  125.1 18.4 %collective-permute-done.14.refs_2_ = bf16[8,56,896]{2,1,0:T(8,128)(2,1)S(1)} collective-permute-done((bf16[8,56,896]{2,1,0:T(8,128)(2,1)}, bf16[8,56,896]{2,1,0:T(8,128)(2,1)S(1)}, u32[]{:S(2)}, u32[]{:S(2)}) %collective-permute-start.14) | collective-permute-done | bytes 802848 | tf_op jit(solution)/shard_map/ppermute | solution.py:181
  147.0 3.8 %collective-permute-done.18 = f32[8,224]{1,0:T(8,128)S(1)} collective-permute-done((f32[8,224]{1,0:T(8,128)S(1)}, f32[8,224]{1,0:T(8,128)S(1)}, u32[]{:S(2)}, u32[]{:S(2)}) %collective-permute-start.18) | collective-permute-done | bytes 7200 | tf_op jit(solution)/shard_map/ppermute | solution.py:31
  152.2 3.3 %collective-permute-done.19 = f32[8,224]{1,0:T(8,128)S(1)} collective-permute-done((f32[8,224]{1,0:T(8,128)S(1)}, f32[8,224]{1,0:T(8,128)S(1)}, u32[]{:S(2)}, u32[]{:S(2)}) %collective-permute-start.19) | collective-permute-done | bytes 7200 | tf_op jit(solution)/shard_map/ppermute | solution.py:31
  155.5 3.1 %collective-permute-start.20 = (f32[8,224]{1,0:T(8,128)S(1)}, f32[8,224]{1,0:T(8,128)S(1)}, u32[]{:S(2)}, u32[]{:S(2)}) collective-permute-start(f32[8,224]{1,0:T(8,128)S(1)} %add.161), channel_id=1, source_target_pairs={{0,128},{32,160},{64,192},{96,224},{128,0},{160,32},{192,64},{224,... | collective-permute-start | bytes 21512 | tf_op jit(solution)/shard_map/ppermute | solution.py:31
  158.6 2.7 %all-gather.7.cloned.1.call-done = bf16[1856,1024]{1,0:T(8,128)(2,1)} async-done(((bf16[232,1024]{1,0:T(8,128)(2,1)}), bf16[1856,1024]{1,0:T(8,128)(2,1)}) %all-gather.7.cloned.1.call-update) | async-done | bytes 3801104 | tf_op jit(solution)/shard_map/all_gather | solution.py:172
  164.8 8.6 %outputs.1 = (bf16[120,1024]{1,0:T(8,128)(2,1)S(1)}, bf16[120,1024]{1,0:T(8,128)(2,1)S(1)}, bf16[120,1024]{1,0:T(8,128)(2,1)S(1)}, bf16[120,1024]{1,0:T(8,128)(2...) custom-call(bf16[8,56,896]{2,1,0:T(8,128)(2,1)S(1)} %copy-done, ...), custom_call_target="tpu_custom_call" | custom-call | flops 3288334336 | bytes 8716288 | tf_op jit(solution)/shard_map/outputs/pallas_call | solution.py:114
  176.9 3.0 %collective-permute-start.24 = (bf16[120,1024]{1,0:T(8,128)(2,1)S(1)}, bf16[120,1024]{1,0:T(8,128)(2,1)S(1)}, u32[]{:S(2)}, u32[]{:S(2)}) collective-permute-start(bf16[120,1024]{1,0:T(8,128)(2,1)S(1)} %get-tuple-element.15), channel_id=1, source_target_pairs={{0,16},{1,17},{2,18},{3,19},{16,0},{17,1},{18,2},{19,3},{4,20},{5,... | collective-permute-start | bytes 737288 | tf_op jit(solution)/shard_map/ppermute | solution.py:195
  180.8 5.6 %collective-permute-done.21 = bf16[120,1024]{1,0:T(8,128)(2,1)S(1)} collective-permute-done((bf16[120,1024]{1,0:T(8,128)(2,1)S(1)}, bf16[120,1024]{1,0:T(8,128)(2,1)S(1)}, u32[]{:S(2)}, u32[]{:S(2)}) %collective-permute-start.21) | collective-permute-done | bytes 245792 | tf_op jit(solution)/shard_map/ppermute | solution.py:195
  190.1 4.5 %collective-permute-done.25 = bf16[120,1024]{1,0:T(8,128)(2,1)S(1)} collective-permute-done((bf16[120,1024]{1,0:T(8,128)(2,1)S(1)}, bf16[120,1024]{1,0:T(8,128)(2,1)S(1)}, u32[]{:S(2)}, u32[]{:S(2)}) %collective-permute-start.25) | collective-permute-done | bytes 245792 | tf_op jit(solution)/shard_map/ppermute | solution.py:195
  194.6 11.1 %collective-permute-done.26 = bf16[120,1024]{1,0:T(8,128)(2,1)S(1)} collective-permute-done((bf16[120,1024]{1,0:T(8,128)(2,1)S(1)}, bf16[120,1024]{1,0:T(8,128)(2,1)S(1)}, u32[]{:S(2)}, u32[]{:S(2)}) %collective-permute-start.26) | collective-permute-done | bytes 245792 | tf_op jit(solution)/shard_map/ppermute | solution.py:195
  (105 shorter events, 35.4 us)
Async XLA Ops:
  7.2 102.4 %all-gather.5.cloned.1.call-start = ((), (), s32[]{:S(2)}) async-start(), calls=%async_computation | async-start | bytes 8257536 | tf_op jit(solution)/shard_map/all_gather | solution.py:156
  8.7 8.5 %collective-permute-start.11 = (bf16[112,1024]{1,0:T(8,128)(2,1)S(1)}, bf16[112,1024]{1,0:T(8,128)(2,1)S(1)}, u32[]{:S(2)}, u32[]{:S(2)}) collective-permute-start(bf16[112,1024]{1,0:T(8,128)(2,1)S(1)} %bitcast.31), channel_id=1, source_target_pairs={{0,8},{4,12},{8,0},{12,4},{1,9},{5,13},{9,1},{13,5},{2,10},{6,14},... | collective-permute-start | bytes 688136 | tf_op jit(solution)/shard_map/ppermute | solution.py:155
  10.4 10.8 %collective-permute-start.12 = (bf16[112,1024]{1,0:T(8,128)(2,1)S(1)}, bf16[112,1024]{1,0:T(8,128)(2,1)S(1)}, u32[]{:S(2)}, u32[]{:S(2)}) collective-permute-start(bf16[112,1024]{1,0:T(8,128)(2,1)S(1)} %bitcast.30), channel_id=1, source_target_pairs={{0,12},{4,8},{8,4},{12,0},{1,13},{5,9},{9,5},{13,1},{2,14},{6,10},... | collective-permute-start | bytes 688136 | tf_op jit(solution)/shard_map/ppermute | solution.py:155
  22.2 139.0 %all-gather.7.cloned.1.call-start = ((), (), s32[]{:S(2)}) async-start(), calls=%async_computation.1 | async-start | bytes 4276224 | tf_op jit(solution)/shard_map/all_gather | solution.py:172
  28.3 8.6 %collective-permute-start = (bf16[112,1024]{1,0:T(8,128)(2,1)S(1)}, bf16[112,1024]{1,0:T(8,128)(2,1)S(1)}, u32[]{:S(2)}, u32[]{:S(2)}) collective-permute-start(bf16[112,1024]{1,0:T(8,128)(2,1)S(1)} %copy-done.4), channel_id=1, source_target_pairs={{0,3},{1,0},{2,1},{3,2},{4,7},{5,4},{6,5},{7,6},{8,11},{9,8},{10,9... | collective-permute-start | bytes 688136 | tf_op jit(solution)/shard_map/ppermute | solution.py:175
  28.9 10.1 %collective-permute-start.1 = (bf16[112,1024]{1,0:T(8,128)(2,1)S(1)}, bf16[112,1024]{1,0:T(8,128)(2,1)S(1)}, u32[]{:S(2)}, u32[]{:S(2)}) collective-permute-start(bf16[112,1024]{1,0:T(8,128)(2,1)S(1)} %copy-done.4), channel_id=1, source_target_pairs={{0,2},{1,3},{2,0},{3,1},{4,6},{5,7},{6,4},{7,5},{8,10},{9,11},{10,... | collective-permute-start | bytes 688136 | tf_op jit(solution)/shard_map/ppermute | solution.py:175
  31.6 10.1 %collective-permute-start.2 = (bf16[112,1024]{1,0:T(8,128)(2,1)S(1)}, bf16[112,1024]{1,0:T(8,128)(2,1)S(1)}, u32[]{:S(2)}, u32[]{:S(2)}) collective-permute-start(bf16[112,1024]{1,0:T(8,128)(2,1)S(1)} %copy-done.4), channel_id=1, source_target_pairs={{0,1},{1,2},{2,3},{3,0},{4,5},{5,6},{6,7},{7,4},{8,9},{9,10},{10,1... | collective-permute-start | bytes 688136 | tf_op jit(solution)/shard_map/ppermute | solution.py:175
  41.7 23.3 %collective-permute-start.3 = (bf16[448,1024]{1,0:T(8,128)(2,1)S(1)}, bf16[448,1024]{1,0:T(8,128)(2,1)S(1)}, u32[]{:S(2)}, u32[]{:S(2)}) collective-permute-start(bf16[448,1024]{1,0:T(8,128)(2,1)S(1)} %constant_dynamic-update-slice_fusion.refs_0_), channel_id=1, source_target_pairs={{0,8},{8,0},{16,24},{24,16},{1,9},{9,1},{17,25},{25,17},{2,10},{10... | collective-permute-start | bytes 2752520 | tf_op jit(solution)/shard_map/ppermute | solution.py:145
  43.4 42.8 %collective-permute-start.4 = (bf16[448,1024]{1,0:T(8,128)(2,1)S(1)}, bf16[448,1024]{1,0:T(8,128)(2,1)S(1)}, u32[]{:S(2)}, u32[]{:S(2)}) collective-permute-start(bf16[448,1024]{1,0:T(8,128)(2,1)S(1)} %constant_dynamic-update-slice_fusion.refs_0_), channel_id=1, source_target_pairs={{0,16},{8,24},{16,0},{24,8},{1,17},{9,25},{17,1},{25,9},{2,18},{10... | collective-permute-start | bytes 2752520 | tf_op jit(solution)/shard_map/ppermute | solution.py:145
  46.3 42.5 %collective-permute-start.5 = (bf16[448,1024]{1,0:T(8,128)(2,1)S(1)}, bf16[448,1024]{1,0:T(8,128)(2,1)S(1)}, u32[]{:S(2)}, u32[]{:S(2)}) collective-permute-start(bf16[448,1024]{1,0:T(8,128)(2,1)S(1)} %constant_dynamic-update-slice_fusion.refs_0_), channel_id=1, source_target_pairs={{0,24},{8,16},{16,8},{24,0},{1,25},{9,17},{17,9},{25,1},{2,26},{10... | collective-permute-start | bytes 2752520 | tf_op jit(solution)/shard_map/ppermute | solution.py:145
  46.5 42.3 %collective-permute-start.6 = (bf16[448,1024]{1,0:T(8,128)(2,1)S(1)}, bf16[448,1024]{1,0:T(8,128)(2,1)S(1)}, u32[]{:S(2)}, u32[]{:S(2)}) collective-permute-start(bf16[448,1024]{1,0:T(8,128)(2,1)S(1)} %constant_dynamic-update-slice_fusion.refs_0_), channel_id=1, source_target_pairs={{0,4},{4,0},{1,5},{5,1},{2,6},{6,2},{3,7},{7,3},{8,12},{12,8},{9,1... | collective-permute-start | bytes 2752520 | tf_op jit(solution)/shard_map/ppermute | solution.py:148
  65.0 23.8 %collective-permute-start.7 = (bf16[448,1024]{1,0:T(8,128)(2,1)S(1)}, bf16[448,1024]{1,0:T(8,128)(2,1)S(1)}, u32[]{:S(2)}, u32[]{:S(2)}) collective-permute-start(bf16[448,1024]{1,0:T(8,128)(2,1)S(1)} %collective-permute-done.3.refs_1_), channel_id=1, source_target_pairs={{0,4},{4,0},{1,5},{5,1},{2,6},{6,2},{3,7},{7,3},{8,12},{12,8},{9,1... | collective-permute-start | bytes 2752520 | tf_op jit(solution)/shard_map/ppermute | solution.py:148
  123.6 19.8 %collective-permute-start.14 = (bf16[8,56,896]{2,1,0:T(8,128)(2,1)}, bf16[8,56,896]{2,1,0:T(8,128)(2,1)S(1)}, u32[]{:S(2)}, u32[]{:S(2)}) collective-permute-start(bf16[8,56,896]{2,1,0:T(8,128)(2,1)} %hidden.1.refs_0_), channel_id=1, source_target_pairs={{0,8},{8,0},{1,9},{9,1},{2,10},{10,2},{3,11},{11,3},{4,12},{12,4},... | collective-permute-start | bytes 2408456 | tf_op jit(solution)/shard_map/ppermute | solution.py:181
  125.1 19.9 %collective-permute-start.13 = (bf16[8,56,896]{2,1,0:T(8,128)(2,1)}, bf16[8,56,896]{2,1,0:T(8,128)(2,1)S(1)}, u32[]{:S(2)}, u32[]{:S(2)}) collective-permute-start(bf16[8,56,896]{2,1,0:T(8,128)(2,1)} %hidden.1.refs_0_), channel_id=1, source_target_pairs={{0,4},{4,0},{1,5},{5,1},{2,6},{6,2},{3,7},{7,3},{8,12},{12,8},{9,1... | collective-permute-start | bytes 2408456 | tf_op jit(solution)/shard_map/ppermute | solution.py:148
  146.9 3.8 %collective-permute-start.18 = (f32[8,224]{1,0:T(8,128)S(1)}, f32[8,224]{1,0:T(8,128)S(1)}, u32[]{:S(2)}, u32[]{:S(2)}) collective-permute-start(f32[8,224]{1,0:T(8,128)S(1)} %pad_maximum_fusion.3), channel_id=1, source_target_pairs={{0,32},{32,0},{64,96},{96,64},{128,160},{160,128},{192,224},{224,1... | collective-permute-start | bytes 21512 | tf_op jit(solution)/shard_map/ppermute | solution.py:31
  150.8 4.7 %collective-permute-start.19 = (f32[8,224]{1,0:T(8,128)S(1)}, f32[8,224]{1,0:T(8,128)S(1)}, u32[]{:S(2)}, u32[]{:S(2)}) collective-permute-start(f32[8,224]{1,0:T(8,128)S(1)} %fusion.19), channel_id=1, source_target_pairs={{0,64},{32,96},{64,0},{96,32},{128,192},{160,224},{192,128},{224,1... | collective-permute-start | bytes 21512 | tf_op jit(solution)/shard_map/ppermute | solution.py:31
  155.5 7.8 %collective-permute-start.20 = (f32[8,224]{1,0:T(8,128)S(1)}, f32[8,224]{1,0:T(8,128)S(1)}, u32[]{:S(2)}, u32[]{:S(2)}) collective-permute-start(f32[8,224]{1,0:T(8,128)S(1)} %add.161), channel_id=1, source_target_pairs={{0,128},{32,160},{64,192},{96,224},{128,0},{160,32},{192,64},{224,... | collective-permute-start | bytes 21512 | tf_op jit(solution)/shard_map/ppermute | solution.py:31
  173.5 12.9 %collective-permute-start.21 = (bf16[120,1024]{1,0:T(8,128)(2,1)S(1)}, bf16[120,1024]{1,0:T(8,128)(2,1)S(1)}, u32[]{:S(2)}, u32[]{:S(2)}) collective-permute-start(bf16[120,1024]{1,0:T(8,128)(2,1)S(1)} %get-tuple-element.12), channel_id=1, source_target_pairs={{0,1},{1,2},{2,3},{3,0},{16,17},{17,18},{18,19},{19,16},{4,5},{5,6... | collective-permute-start | bytes 737288 | tf_op jit(solution)/shard_map/ppermute | solution.py:195
  174.9 13.0 %collective-permute-start.22 = (bf16[120,1024]{1,0:T(8,128)(2,1)S(1)}, bf16[120,1024]{1,0:T(8,128)(2,1)S(1)}, u32[]{:S(2)}, u32[]{:S(2)}) collective-permute-start(bf16[120,1024]{1,0:T(8,128)(2,1)S(1)} %get-tuple-element.13), channel_id=1, source_target_pairs={{0,2},{1,3},{2,0},{3,1},{16,18},{17,19},{18,16},{19,17},{4,6},{5,7... | collective-permute-start | bytes 737288 | tf_op jit(solution)/shard_map/ppermute | solution.py:195
  175.8 14.2 %collective-permute-start.23 = (bf16[120,1024]{1,0:T(8,128)(2,1)S(1)}, bf16[120,1024]{1,0:T(8,128)(2,1)S(1)}, u32[]{:S(2)}, u32[]{:S(2)}) collective-permute-start(bf16[120,1024]{1,0:T(8,128)(2,1)S(1)} %get-tuple-element.14), channel_id=1, source_target_pairs={{0,3},{1,0},{2,1},{3,2},{16,19},{17,16},{18,17},{19,18},{4,7},{5,4... | collective-permute-start | bytes 737288 | tf_op jit(solution)/shard_map/ppermute | solution.py:195
  176.9 13.1 %collective-permute-start.24 = (bf16[120,1024]{1,0:T(8,128)(2,1)S(1)}, bf16[120,1024]{1,0:T(8,128)(2,1)S(1)}, u32[]{:S(2)}, u32[]{:S(2)}) collective-permute-start(bf16[120,1024]{1,0:T(8,128)(2,1)S(1)} %get-tuple-element.15), channel_id=1, source_target_pairs={{0,16},{1,17},{2,18},{3,19},{16,0},{17,1},{18,2},{19,3},{4,20},{5,... | collective-permute-start | bytes 737288 | tf_op jit(solution)/shard_map/ppermute | solution.py:195
  180.0 14.6 %collective-permute-start.25 = (bf16[120,1024]{1,0:T(8,128)(2,1)S(1)}, bf16[120,1024]{1,0:T(8,128)(2,1)S(1)}, u32[]{:S(2)}, u32[]{:S(2)}) collective-permute-start(bf16[120,1024]{1,0:T(8,128)(2,1)S(1)} %get-tuple-element.16), channel_id=1, source_target_pairs={{0,17},{1,18},{2,19},{3,16},{16,1},{17,2},{18,3},{19,0},{4,21},{5,... | collective-permute-start | bytes 737288 | tf_op jit(solution)/shard_map/ppermute | solution.py:195
  186.4 19.3 %collective-permute-start.26 = (bf16[120,1024]{1,0:T(8,128)(2,1)S(1)}, bf16[120,1024]{1,0:T(8,128)(2,1)S(1)}, u32[]{:S(2)}, u32[]{:S(2)}) collective-permute-start(bf16[120,1024]{1,0:T(8,128)(2,1)S(1)} %get-tuple-element.17), channel_id=1, source_target_pairs={{0,18},{1,19},{2,16},{3,17},{16,2},{17,3},{18,0},{19,1},{4,22},{5,... | collective-permute-start | bytes 737288 | tf_op jit(solution)/shard_map/ppermute | solution.py:195
  187.9 19.4 %collective-permute-start.27 = (bf16[120,1024]{1,0:T(8,128)(2,1)S(1)}, bf16[120,1024]{1,0:T(8,128)(2,1)S(1)}, u32[]{:S(2)}, u32[]{:S(2)}) collective-permute-start(bf16[120,1024]{1,0:T(8,128)(2,1)S(1)} %get-tuple-element.18), channel_id=1, source_target_pairs={{0,19},{1,16},{2,17},{3,18},{16,3},{17,0},{18,1},{19,2},{4,23},{5,... | collective-permute-start | bytes 737288 | tf_op jit(solution)/shard_map/ppermute | solution.py:195
  (18 other events, 195.2 us)
Sparse Core Ops, SparseCore 0:
  22.3 87.2 all-gather.4
  111.4 49.8 all-gather.6

commit v4 on v3

--- a/solution.py
+++ b/solution.py
@@ -67,8 +67,8 @@
 
 
 def output_kernel(pieces, blocks, *refs):
-    hidden_refs, (down_ref, units_ref, weights_ref) = refs[:pieces], refs[pieces : pieces + 3]
-    out_refs, (total, col, row) = refs[pieces + 3 : -3], refs[-3:]
+    hidden_refs, (down_ref, units_ref) = refs[:pieces], refs[pieces : pieces + 2]
+    out_refs, (total, col, row) = refs[pieces + 2 : -3], refs[-3:]
     units = sum(r.shape[0] for r in hidden_refs)
     width = down_ref.shape[1]
     rows = total.shape[0] // blocks
@@ -78,14 +78,17 @@
         for sums in (total, col, row):
             sums[...] = jnp.zeros_like(sums)
 
-    def fold(value):
-        return jnp.sum(value.reshape(units // 8, 8, value.shape[1]), axis=0)
-
-    hidden = jnp.concatenate([r[...].astype(F32) for r in hidden_refs])
+    hidden = jnp.concatenate([r[...].astype(F32) for r in hidden_refs]).astype(BF16)
     down = down_ref[pl.ds(0, units), :]
-    total[...] += lax.dot_general(hidden.astype(BF16), down, MAJOR, preferred_element_type=F32)
-    col[...] += fold(units_ref[...] * down.astype(F32))
-    row[...] += fold(weights_ref[...] * hidden)
+    total[...] += lax.dot_general(hidden, down, MAJOR, preferred_element_type=F32)
+    sums = units_ref[...]
+    high = sums.astype(BF16).astype(F32)
+    middle = (sums - high).astype(BF16).astype(F32)
+    rest = jnp.zeros((EXTRA - 3, units), F32)
+    terms = jnp.concatenate([high, middle, sums - high - middle, rest]).astype(BF16)
+    col[...] += jnp.dot(terms, down, preferred_element_type=F32)
+    weights = down_ref[pl.ds(units, EXTRA), pl.ds(0, units)]
+    row[...] += jnp.dot(weights, hidden, preferred_element_type=F32)
 
     @pl.when(pl.program_id(0) == pl.num_programs(0) - 1)
     def _():
@@ -105,11 +108,11 @@
             out_refs[j][pl.ds(rows, EXTRA), :] = lines
 
 
-def outputs(hidden, down, unit_sums, weight_sums, blocks):
+def outputs(hidden, down, unit_sums, blocks):
     steps, _, total = hidden[0].shape
     units = sum(h.shape[1] for h in hidden)
     width = down.shape[2]
-    operands = [*hidden, down, unit_sums, weight_sums]
+    operands = [*hidden, down, unit_sums]
     piece = (total // blocks + EXTRA, width)
     return pl.pallas_call(
         functools.partial(output_kernel, len(hidden), blocks),
@@ -181,24 +184,25 @@
     far = lax.ppermute(hidden, "yl", flip(2, 1))
     hidden = [hidden, swap(hidden), far, swap(far)]
     unit_sums = jnp.concatenate([jnp.sum(h.astype(F32), axis=2) for h in hidden], axis=1)
-    unit_sums = sum_over(unit_sums, "z", nz)[:, :, None]
-    weight_sums = jnp.sum(down[:, units : units + 3, :units].astype(F32), axis=1)[:, :, None]
+    unit_sums = sum_over(unit_sums, "z", nz)[:, None, :]
 
     targets = [(dy, dx) for dy in range(nyh) for dx in range(nx)]
-    far_first = sorted(range(len(targets)), key=lambda j: -2 * targets[j][0] - min(targets[j][1], nx - targets[j][1]))
-    sent = outputs(hidden, down, unit_sums, weight_sums, len(targets))
-    received = [None] * len(targets)
+    far_first = sorted(
+        range(len(targets)), key=lambda j: -2 * targets[j][0] - min(targets[j][1], nx - targets[j][1])
+    )
+    sent = outputs(hidden, down, unit_sums, len(targets))
+    received = {}
     for j in far_first:
         (dy, dx), piece = targets[j], sent[j]
         perm = [(h * nx + i, (h ^ dy) * nx + (i + dx) % nx) for h in range(nyh) for i in range(nx)]
         if dx or dy:
             piece = lax.ppermute(piece, ("yh", "x"), perm)
         received[j] = piece.astype(F32)
-    mixed = sum(p[:rows] for p in received).astype(BF16)
-    lines = sum(p[rows : rows + 2] for p in received)
+    mixed = sum(p[:rows] for p in received.values()).astype(BF16)
+    lines = sum(p[rows : rows + 2] for p in received.values())
     col_check = (lines[0] + lines[1]) / math.sqrt(total_tokens)
     row_check = 0.0
-    for j, piece in enumerate(received):
+    for j, piece in received.items():
         line = piece[rows + 2, j * rows : (j + 1) * rows] + piece[rows + 3, j * rows : (j + 1) * rows]
         row_check = row_check + line
     return (mixed, col_check, row_check / math.sqrt(model_width))

time: 217 us -> 211 us (0.972)
  waiting for transfers between devices: 137 us -> 130 us
  starting transfers between devices: 27.8 us -> 31.8 us
  local copies, waits for them, and re-layouts: 7.75 us -> 4.11 us
    ppermute x7, waiting for transfers between devices: 25.5 us -> 16.6 us  [per_device(): piece = lax.ppermute(piece, ('yh', 'x'), perm)]
    ppermute x5, waiting for transfers between devices: 9.83 us -> 14.7 us  [sum_over(): value = value + lax.ppermute(value, axis, flip(n, mask))]
    ppermute x7, starting transfers between devices: 8.08 us -> 12.2 us  [per_device(): piece = lax.ppermute(piece, ('yh', 'x'), perm)]
    all_gather x1, waiting for transfers between devices: 2.65 us -> 0.02 us  [per_device(): down = lax.all_gather(down, 'z', axis=0, tiled=False)]
    unnamed x27 -> x23, local copies, waits for them, and re-layouts: 4.53 us -> 2.5 us
  transfers between devices with their start and end apart: 30 -> 30, of which waited for: 23 -> 23; matrix products, arithmetic and copies ran while one was open for 3% -> 2% of each run, Pallas kernels for 6% -> 7%
where the time goes in v4:
time: 211 us; the launch traced here: 209 us
  waiting for transfers between devices  130 us (62%)
  starting transfers between devices  31.8 us (15%)
  Pallas kernels  22.6 us (11%)
  between operations  14.4 us (7%)
  other arithmetic  6.56 us (3%)
  local copies, waits for them, and re-layouts  4.11 us (2%)
    ppermute x3, waiting for transfers between devices, across(): return lax.ppermute(array, ('yh', 'yl'), flip(nyh * nyl, mask))  42.2 us
    ppermute x1, waiting for transfers between devices, per_device(): far = lax.ppermute(hidden, 'yl', flip(2, 1))  18.4 us
    all_gather x1, waiting for transfers between devices, per_device(): lax.all_gather(jnp.concatenate(weights, axis=1), 'z', axis=0, tiled=False)  18.2 us
    ppermute x7, waiting for transfers between devices, per_device(): piece = lax.ppermute(piece, ('yh', 'x'), perm)  16.6 us
    ppermute x5, waiting for transfers between devices, sum_over(): value = value + lax.ppermute(value, axis, flip(n, mask))  14.7 us
    pallas_call x1, Pallas kernels, hidden_units(): pl.pallas_call(hidden_kernel, out_shape=jax.ShapeDtypeStruct((count, unit...  14 us
    ppermute x7, starting transfers between devices, per_device(): piece = lax.ppermute(piece, ('yh', 'x'), perm)  12.2 us
    ppermute x3, waiting for transfers between devices, per_device(): weights.append(piece if k == 0 else lax.ppermute(piece, ROW, flip(nrow, k)))  10.6 us
  transfers between devices with their start and end apart: 30, of which 23 were waited for; matrix products, arithmetic and copies ran while one was open for 2% of the time, Pallas kernels for 7%

profile of v4, /device:TPU:4, one launch (start us, length us, event | category | flops | bytes accessed | tf_op | source)
XLA Modules:
  0.0 209.4 jit_solution(11222516326033557826)
XLA Ops:
  10.6 6.6 %collective-permute-done.11 = bf16[112,1024]{1,0:T(8,128)(2,1)S(1)} collective-permute-done((bf16[112,1024]{1,0:T(8,128)(2,1)S(1)}, bf16[112,1024]{1,0:T(8,128)(2,1)S(1)}, u32[]{:S(2)}, u32[]{:S(2)}) %collective-permute-start.11) | collective-permute-done | bytes 229408 | tf_op jit(solution)/shard_map/ppermute | solution.py:158
  17.2 4.0 %collective-permute-done.12 = bf16[112,1024]{1,0:T(8,128)(2,1)S(1)} collective-permute-done((bf16[112,1024]{1,0:T(8,128)(2,1)S(1)}, bf16[112,1024]{1,0:T(8,128)(2,1)S(1)}, u32[]{:S(2)}, u32[]{:S(2)}) %collective-permute-start.12) | collective-permute-done | bytes 229408 | tf_op jit(solution)/shard_map/ppermute | solution.py:158
  28.9 2.7 %collective-permute-start.1 = (bf16[112,1024]{1,0:T(8,128)(2,1)S(1)}, bf16[112,1024]{1,0:T(8,128)(2,1)S(1)}, u32[]{:S(2)}, u32[]{:S(2)}) collective-permute-start(bf16[112,1024]{1,0:T(8,128)(2,1)S(1)} %copy-done.2), channel_id=1, source_target_pairs={{0,2},{1,3},{2,0},{3,1},{4,6},{5,7},{6,4},{7,5},{8,10},{9,11},{10,... | collective-permute-start | bytes 688136 | tf_op jit(solution)/shard_map/ppermute | solution.py:178
  33.3 3.7 %collective-permute-done = bf16[112,1024]{1,0:T(8,128)(2,1)S(1)} collective-permute-done((bf16[112,1024]{1,0:T(8,128)(2,1)S(1)}, bf16[112,1024]{1,0:T(8,128)(2,1)S(1)}, u32[]{:S(2)}, u32[]{:S(2)}) %collective-permute-start) | collective-permute-done | bytes 229408 | tf_op jit(solution)/shard_map/ppermute | solution.py:178
  36.9 2.1 collective-permute-done.1
  39.0 2.7 %collective-permute-done.2 = bf16[112,1024]{1,0:T(8,128)(2,1)S(1)} collective-permute-done((bf16[112,1024]{1,0:T(8,128)(2,1)S(1)}, bf16[112,1024]{1,0:T(8,128)(2,1)S(1)}, u32[]{:S(2)}, u32[]{:S(2)}) %collective-permute-start.2) | collective-permute-done | bytes 229408 | tf_op jit(solution)/shard_map/ppermute | solution.py:178
  43.4 2.9 %collective-permute-start.4 = (bf16[448,1024]{1,0:T(8,128)(2,1)S(1)}, bf16[448,1024]{1,0:T(8,128)(2,1)S(1)}, u32[]{:S(2)}, u32[]{:S(2)}) collective-permute-start(bf16[448,1024]{1,0:T(8,128)(2,1)S(1)} %constant_dynamic-update-slice_fusion.refs_0_), channel_id=1, source_target_pairs={{0,16},{8,24},{16,0},{24,8},{1,17},{9,25},{17,1},{25,9},{2,18},{10... | collective-permute-start | bytes 2752520 | tf_op jit(solution)/shard_map/ppermute | solution.py:148
  46.5 18.5 %collective-permute-done.3.refs_1_ = bf16[448,1024]{1,0:T(8,128)(2,1)S(1)} collective-permute-done((bf16[448,1024]{1,0:T(8,128)(2,1)S(1)}, bf16[448,1024]{1,0:T(8,128)(2,1)S(1)}, u32[]{:S(2)}, u32[]{:S(2)}) %collective-permute-start.3) | collective-permute-done | bytes 917536 | tf_op jit(solution)/shard_map/ppermute | solution.py:148
  65.0 21.2 %collective-permute-done.4.refs_2_ = bf16[448,1024]{1,0:T(8,128)(2,1)S(1)} collective-permute-done((bf16[448,1024]{1,0:T(8,128)(2,1)S(1)}, bf16[448,1024]{1,0:T(8,128)(2,1)S(1)}, u32[]{:S(2)}, u32[]{:S(2)}) %collective-permute-start.4) | collective-permute-done | bytes 917536 | tf_op jit(solution)/shard_map/ppermute | solution.py:148
  86.2 2.6 %collective-permute-done.5.refs_3_ = bf16[448,1024]{1,0:T(8,128)(2,1)S(1)} collective-permute-done((bf16[448,1024]{1,0:T(8,128)(2,1)S(1)}, bf16[448,1024]{1,0:T(8,128)(2,1)S(1)}, u32[]{:S(2)}, u32[]{:S(2)}) %collective-permute-start.5) | collective-permute-done | bytes 917536 | tf_op jit(solution)/shard_map/ppermute | solution.py:148
  91.4 18.2 %all-gather.5.cloned.1.call-done.refs_8_ = bf16[896,4096]{1,0:T(8,128)(2,1)} async-done(((bf16[112,4096]{1,0:T(8,128)(2,1)}), bf16[896,4096]{1,0:T(8,128)(2,1)}) %all-gather.5.cloned.1.call-update) | async-done | bytes 7340048 | tf_op jit(solution)/shard_map/all_gather | solution.py:159
  109.6 14.0 %hidden.1.refs_0_ = bf16[8,56,896]{2,1,0:T(8,128)(2,1)} custom-call(bf16[448,1024]{1,0:T(8,128)(2,1)} %copy-done.3, bf16[448,1024]{1,0:T(8,128)(2,1)} %copy-done.4, bf16[448,1024]{1,0:T(8,128)(2,1)} %copy-done.5, bf16[448,1024]{1,0:T(8,128)(2,1)} %copy-done.6, bf16[448,1024]{1,0:T(8,128)(2,1)} %copy-done.7, bf16[448,1024]{1,0:T(8,128)(2,1)} %copy-done.8, ...), custom_call_target="tpu_custom_call" | custom-call | flops 6576668672 | bytes 14680064 | tf_op jit(solution)/shard_map/hidden/pallas_call | solution.py:56
  125.1 18.4 %collective-permute-done.14.refs_2_ = bf16[8,56,896]{2,1,0:T(8,128)(2,1)S(1)} collective-permute-done((bf16[8,56,896]{2,1,0:T(8,128)(2,1)}, bf16[8,56,896]{2,1,0:T(8,128)(2,1)S(1)}, u32[]{:S(2)}, u32[]{:S(2)}) %collective-permute-start.14) | collective-permute-done | bytes 802848 | tf_op jit(solution)/shard_map/ppermute | solution.py:184
  146.1 3.8 %collective-permute-done.18 = f32[8,224]{1,0:T(8,128)S(1)} collective-permute-done((f32[8,224]{1,0:T(8,128)S(1)}, f32[8,224]{1,0:T(8,128)S(1)}, u32[]{:S(2)}, u32[]{:S(2)}) %collective-permute-start.18) | collective-permute-done | bytes 7200 | tf_op jit(solution)/shard_map/ppermute | solution.py:31
  151.3 3.4 %collective-permute-done.19 = f32[8,224]{1,0:T(8,128)S(1)} collective-permute-done((f32[8,224]{1,0:T(8,128)S(1)}, f32[8,224]{1,0:T(8,128)S(1)}, u32[]{:S(2)}, u32[]{:S(2)}) %collective-permute-start.19) | collective-permute-done | bytes 7200 | tf_op jit(solution)/shard_map/ppermute | solution.py:31
  154.8 3.0 %collective-permute-start.20 = (f32[8,224]{1,0:T(8,128)S(1)}, f32[8,224]{1,0:T(8,128)S(1)}, u32[]{:S(2)}, u32[]{:S(2)}) collective-permute-start(f32[8,224]{1,0:T(8,128)S(1)} %add.161), channel_id=1, source_target_pairs={{0,128},{32,160},{64,192},{96,224},{128,0},{160,32},{192,64},{224,... | collective-permute-start | bytes 21512 | tf_op jit(solution)/shard_map/ppermute | solution.py:31
  157.7 4.7 %collective-permute-done.20 = f32[8,224]{1,0:T(8,128)S(1)} collective-permute-done((f32[8,224]{1,0:T(8,128)S(1)}, f32[8,224]{1,0:T(8,128)S(1)}, u32[]{:S(2)}, u32[]{:S(2)}) %collective-permute-start.20) | collective-permute-done | bytes 7200 | tf_op jit(solution)/shard_map/ppermute | solution.py:31
  162.5 8.6 %outputs.1 = (bf16[120,1024]{1,0:T(8,128)(2,1)S(1)}, bf16[120,1024]{1,0:T(8,128)(2,1)S(1)}, bf16[120,1024]{1,0:T(8,128)(2,1)S(1)}, bf16[120,1024]{1,0:T(8,128)(2...) custom-call(bf16[8,56,896]{2,1,0:T(8,128)(2,1)S(1)} %copy-done, ...), custom_call_target="tpu_custom_call" | custom-call | flops 3288334336 | bytes 8716288 | tf_op jit(solution)/shard_map/outputs/pallas_call | solution.py:117
  171.1 3.1 %collective-permute-start.21 = (bf16[120,1024]{1,0:T(8,128)(2,1)S(1)}, bf16[120,1024]{1,0:T(8,128)(2,1)S(1)}, u32[]{:S(2)}, u32[]{:S(2)}) collective-permute-start(bf16[120,1024]{1,0:T(8,128)(2,1)S(1)} %get-tuple-element.11), channel_id=1, source_target_pairs={{0,18},{1,19},{2,16},{3,17},{16,2},{17,3},{18,0},{19,1},{4,22},{5,... | collective-permute-start | bytes 737288 | tf_op jit(solution)/shard_map/ppermute | solution.py:199
  176.2 2.4 %collective-permute-start.23 = (bf16[120,1024]{1,0:T(8,128)(2,1)S(1)}, bf16[120,1024]{1,0:T(8,128)(2,1)S(1)}, u32[]{:S(2)}, u32[]{:S(2)}) collective-permute-start(bf16[120,1024]{1,0:T(8,128)(2,1)S(1)} %get-tuple-element.13), channel_id=1, source_target_pairs={{0,19},{1,16},{2,17},{3,18},{16,3},{17,0},{18,1},{19,2},{4,23},{5,... | collective-permute-start | bytes 737288 | tf_op jit(solution)/shard_map/ppermute | solution.py:199
  178.6 4.2 %collective-permute-start.24 = (bf16[120,1024]{1,0:T(8,128)(2,1)S(1)}, bf16[120,1024]{1,0:T(8,128)(2,1)S(1)}, u32[]{:S(2)}, u32[]{:S(2)}) collective-permute-start(bf16[120,1024]{1,0:T(8,128)(2,1)S(1)} %get-tuple-element.14), channel_id=1, source_target_pairs={{0,2},{1,3},{2,0},{3,1},{16,18},{17,19},{18,16},{19,17},{4,6},{5,7... | collective-permute-start | bytes 737288 | tf_op jit(solution)/shard_map/ppermute | solution.py:199
  183.3 3.2 %collective-permute-done.21 = bf16[120,1024]{1,0:T(8,128)(2,1)S(1)} collective-permute-done((bf16[120,1024]{1,0:T(8,128)(2,1)S(1)}, bf16[120,1024]{1,0:T(8,128)(2,1)S(1)}, u32[]{:S(2)}, u32[]{:S(2)}) %collective-permute-start.21) | collective-permute-done | bytes 245792 | tf_op jit(solution)/shard_map/ppermute | solution.py:199
  186.5 6.2 %collective-permute-done.22 = bf16[120,1024]{1,0:T(8,128)(2,1)S(1)} collective-permute-done((bf16[120,1024]{1,0:T(8,128)(2,1)S(1)}, bf16[120,1024]{1,0:T(8,128)(2,1)S(1)}, u32[]{:S(2)}, u32[]{:S(2)}) %collective-permute-start.22) | collective-permute-done | bytes 245792 | tf_op jit(solution)/shard_map/ppermute | solution.py:199
  192.9 3.1 %collective-permute-done.24 = bf16[120,1024]{1,0:T(8,128)(2,1)S(1)} collective-permute-done((bf16[120,1024]{1,0:T(8,128)(2,1)S(1)}, bf16[120,1024]{1,0:T(8,128)(2,1)S(1)}, u32[]{:S(2)}, u32[]{:S(2)}) %collective-permute-start.24) | collective-permute-done | bytes 245792 | tf_op jit(solution)/shard_map/ppermute | solution.py:199
  (99 shorter events, 31.9 us)
Async XLA Ops:
  7.2 102.4 %all-gather.5.cloned.1.call-start = ((), (), s32[]{:S(2)}) async-start(), calls=%async_computation | async-start | bytes 8257536 | tf_op jit(solution)/shard_map/all_gather | solution.py:159
  8.7 8.5 %collective-permute-start.11 = (bf16[112,1024]{1,0:T(8,128)(2,1)S(1)}, bf16[112,1024]{1,0:T(8,128)(2,1)S(1)}, u32[]{:S(2)}, u32[]{:S(2)}) collective-permute-start(bf16[112,1024]{1,0:T(8,128)(2,1)S(1)} %bitcast.28), channel_id=1, source_target_pairs={{0,8},{4,12},{8,0},{12,4},{1,9},{5,13},{9,1},{13,5},{2,10},{6,14},... | collective-permute-start | bytes 688136 | tf_op jit(solution)/shard_map/ppermute | solution.py:158
  10.4 10.8 %collective-permute-start.12 = (bf16[112,1024]{1,0:T(8,128)(2,1)S(1)}, bf16[112,1024]{1,0:T(8,128)(2,1)S(1)}, u32[]{:S(2)}, u32[]{:S(2)}) collective-permute-start(bf16[112,1024]{1,0:T(8,128)(2,1)S(1)} %bitcast.27), channel_id=1, source_target_pairs={{0,12},{4,8},{8,4},{12,0},{1,13},{5,9},{9,5},{13,1},{2,14},{6,10},... | collective-permute-start | bytes 688136 | tf_op jit(solution)/shard_map/ppermute | solution.py:158
  22.2 140.3 %all-gather.7.cloned.1.call-start = ((), (), s32[]{:S(2)}) async-start(), calls=%async_computation.1 | async-start | bytes 4276224 | tf_op jit(solution)/shard_map/all_gather | solution.py:175
  28.3 8.6 %collective-permute-start = (bf16[112,1024]{1,0:T(8,128)(2,1)S(1)}, bf16[112,1024]{1,0:T(8,128)(2,1)S(1)}, u32[]{:S(2)}, u32[]{:S(2)}) collective-permute-start(bf16[112,1024]{1,0:T(8,128)(2,1)S(1)} %copy-done.2), channel_id=1, source_target_pairs={{0,3},{1,0},{2,1},{3,2},{4,7},{5,4},{6,5},{7,6},{8,11},{9,8},{10,9... | collective-permute-start | bytes 688136 | tf_op jit(solution)/shard_map/ppermute | solution.py:178
  28.9 10.1 %collective-permute-start.1 = (bf16[112,1024]{1,0:T(8,128)(2,1)S(1)}, bf16[112,1024]{1,0:T(8,128)(2,1)S(1)}, u32[]{:S(2)}, u32[]{:S(2)}) collective-permute-start(bf16[112,1024]{1,0:T(8,128)(2,1)S(1)} %copy-done.2), channel_id=1, source_target_pairs={{0,2},{1,3},{2,0},{3,1},{4,6},{5,7},{6,4},{7,5},{8,10},{9,11},{10,... | collective-permute-start | bytes 688136 | tf_op jit(solution)/shard_map/ppermute | solution.py:178
  31.6 10.1 %collective-permute-start.2 = (bf16[112,1024]{1,0:T(8,128)(2,1)S(1)}, bf16[112,1024]{1,0:T(8,128)(2,1)S(1)}, u32[]{:S(2)}, u32[]{:S(2)}) collective-permute-start(bf16[112,1024]{1,0:T(8,128)(2,1)S(1)} %copy-done.2), channel_id=1, source_target_pairs={{0,1},{1,2},{2,3},{3,0},{4,5},{5,6},{6,7},{7,4},{8,9},{9,10},{10,1... | collective-permute-start | bytes 688136 | tf_op jit(solution)/shard_map/ppermute | solution.py:178
  41.7 23.3 %collective-permute-start.3 = (bf16[448,1024]{1,0:T(8,128)(2,1)S(1)}, bf16[448,1024]{1,0:T(8,128)(2,1)S(1)}, u32[]{:S(2)}, u32[]{:S(2)}) collective-permute-start(bf16[448,1024]{1,0:T(8,128)(2,1)S(1)} %constant_dynamic-update-slice_fusion.refs_0_), channel_id=1, source_target_pairs={{0,8},{8,0},{16,24},{24,16},{1,9},{9,1},{17,25},{25,17},{2,10},{10... | collective-permute-start | bytes 2752520 | tf_op jit(solution)/shard_map/ppermute | solution.py:148
  43.4 42.8 %collective-permute-start.4 = (bf16[448,1024]{1,0:T(8,128)(2,1)S(1)}, bf16[448,1024]{1,0:T(8,128)(2,1)S(1)}, u32[]{:S(2)}, u32[]{:S(2)}) collective-permute-start(bf16[448,1024]{1,0:T(8,128)(2,1)S(1)} %constant_dynamic-update-slice_fusion.refs_0_), channel_id=1, source_target_pairs={{0,16},{8,24},{16,0},{24,8},{1,17},{9,25},{17,1},{25,9},{2,18},{10... | collective-permute-start | bytes 2752520 | tf_op jit(solution)/shard_map/ppermute | solution.py:148
  46.3 42.5 %collective-permute-start.5 = (bf16[448,1024]{1,0:T(8,128)(2,1)S(1)}, bf16[448,1024]{1,0:T(8,128)(2,1)S(1)}, u32[]{:S(2)}, u32[]{:S(2)}) collective-permute-start(bf16[448,1024]{1,0:T(8,128)(2,1)S(1)} %constant_dynamic-update-slice_fusion.refs_0_), channel_id=1, source_target_pairs={{0,24},{8,16},{16,8},{24,0},{1,25},{9,17},{17,9},{25,1},{2,26},{10... | collective-permute-start | bytes 2752520 | tf_op jit(solution)/shard_map/ppermute | solution.py:148
  46.5 42.3 %collective-permute-start.6 = (bf16[448,1024]{1,0:T(8,128)(2,1)S(1)}, bf16[448,1024]{1,0:T(8,128)(2,1)S(1)}, u32[]{:S(2)}, u32[]{:S(2)}) collective-permute-start(bf16[448,1024]{1,0:T(8,128)(2,1)S(1)} %constant_dynamic-update-slice_fusion.refs_0_), channel_id=1, source_target_pairs={{0,4},{4,0},{1,5},{5,1},{2,6},{6,2},{3,7},{7,3},{8,12},{12,8},{9,1... | collective-permute-start | bytes 2752520 | tf_op jit(solution)/shard_map/ppermute | solution.py:151
  65.0 23.8 %collective-permute-start.7 = (bf16[448,1024]{1,0:T(8,128)(2,1)S(1)}, bf16[448,1024]{1,0:T(8,128)(2,1)S(1)}, u32[]{:S(2)}, u32[]{:S(2)}) collective-permute-start(bf16[448,1024]{1,0:T(8,128)(2,1)S(1)} %collective-permute-done.3.refs_1_), channel_id=1, source_target_pairs={{0,4},{4,0},{1,5},{5,1},{2,6},{6,2},{3,7},{7,3},{8,12},{12,8},{9,1... | collective-permute-start | bytes 2752520 | tf_op jit(solution)/shard_map/ppermute | solution.py:151
  123.6 19.8 %collective-permute-start.14 = (bf16[8,56,896]{2,1,0:T(8,128)(2,1)}, bf16[8,56,896]{2,1,0:T(8,128)(2,1)S(1)}, u32[]{:S(2)}, u32[]{:S(2)}) collective-permute-start(bf16[8,56,896]{2,1,0:T(8,128)(2,1)} %hidden.1.refs_0_), channel_id=1, source_target_pairs={{0,8},{8,0},{1,9},{9,1},{2,10},{10,2},{3,11},{11,3},{4,12},{12,4},... | collective-permute-start | bytes 2408456 | tf_op jit(solution)/shard_map/ppermute | solution.py:184
  125.1 19.9 %collective-permute-start.13 = (bf16[8,56,896]{2,1,0:T(8,128)(2,1)}, bf16[8,56,896]{2,1,0:T(8,128)(2,1)S(1)}, u32[]{:S(2)}, u32[]{:S(2)}) collective-permute-start(bf16[8,56,896]{2,1,0:T(8,128)(2,1)} %hidden.1.refs_0_), channel_id=1, source_target_pairs={{0,4},{4,0},{1,5},{5,1},{2,6},{6,2},{3,7},{7,3},{8,12},{12,8},{9,1... | collective-permute-start | bytes 2408456 | tf_op jit(solution)/shard_map/ppermute | solution.py:151
  146.0 3.8 %collective-permute-start.18 = (f32[8,224]{1,0:T(8,128)S(1)}, f32[8,224]{1,0:T(8,128)S(1)}, u32[]{:S(2)}, u32[]{:S(2)}) collective-permute-start(f32[8,224]{1,0:T(8,128)S(1)} %pad_maximum_fusion.3), channel_id=1, source_target_pairs={{0,32},{32,0},{64,96},{96,64},{128,160},{160,128},{192,224},{224,1... | collective-permute-start | bytes 21512 | tf_op jit(solution)/shard_map/ppermute | solution.py:31
  149.9 4.8 %collective-permute-start.19 = (f32[8,224]{1,0:T(8,128)S(1)}, f32[8,224]{1,0:T(8,128)S(1)}, u32[]{:S(2)}, u32[]{:S(2)}) collective-permute-start(f32[8,224]{1,0:T(8,128)S(1)} %fusion.19), channel_id=1, source_target_pairs={{0,64},{32,96},{64,0},{96,32},{128,192},{160,224},{192,128},{224,1... | collective-permute-start | bytes 21512 | tf_op jit(solution)/shard_map/ppermute | solution.py:31
  154.8 7.7 %collective-permute-start.20 = (f32[8,224]{1,0:T(8,128)S(1)}, f32[8,224]{1,0:T(8,128)S(1)}, u32[]{:S(2)}, u32[]{:S(2)}) collective-permute-start(f32[8,224]{1,0:T(8,128)S(1)} %add.161), channel_id=1, source_target_pairs={{0,128},{32,160},{64,192},{96,224},{128,0},{160,32},{192,64},{224,... | collective-permute-start | bytes 21512 | tf_op jit(solution)/shard_map/ppermute | solution.py:31
  171.1 15.4 %collective-permute-start.21 = (bf16[120,1024]{1,0:T(8,128)(2,1)S(1)}, bf16[120,1024]{1,0:T(8,128)(2,1)S(1)}, u32[]{:S(2)}, u32[]{:S(2)}) collective-permute-start(bf16[120,1024]{1,0:T(8,128)(2,1)S(1)} %get-tuple-element.11), channel_id=1, source_target_pairs={{0,18},{1,19},{2,16},{3,17},{16,2},{17,3},{18,0},{19,1},{4,22},{5,... | collective-permute-start | bytes 737288 | tf_op jit(solution)/shard_map/ppermute | solution.py:199
  174.2 18.5 %collective-permute-start.22 = (bf16[120,1024]{1,0:T(8,128)(2,1)S(1)}, bf16[120,1024]{1,0:T(8,128)(2,1)S(1)}, u32[]{:S(2)}, u32[]{:S(2)}) collective-permute-start(bf16[120,1024]{1,0:T(8,128)(2,1)S(1)} %get-tuple-element.12), channel_id=1, source_target_pairs={{0,17},{1,18},{2,19},{3,16},{16,1},{17,2},{18,3},{19,0},{4,21},{5,... | collective-permute-start | bytes 737288 | tf_op jit(solution)/shard_map/ppermute | solution.py:199
  176.2 16.7 %collective-permute-start.23 = (bf16[120,1024]{1,0:T(8,128)(2,1)S(1)}, bf16[120,1024]{1,0:T(8,128)(2,1)S(1)}, u32[]{:S(2)}, u32[]{:S(2)}) collective-permute-start(bf16[120,1024]{1,0:T(8,128)(2,1)S(1)} %get-tuple-element.13), channel_id=1, source_target_pairs={{0,19},{1,16},{2,17},{3,18},{16,3},{17,0},{18,1},{19,2},{4,23},{5,... | collective-permute-start | bytes 737288 | tf_op jit(solution)/shard_map/ppermute | solution.py:199
  178.6 17.4 %collective-permute-start.24 = (bf16[120,1024]{1,0:T(8,128)(2,1)S(1)}, bf16[120,1024]{1,0:T(8,128)(2,1)S(1)}, u32[]{:S(2)}, u32[]{:S(2)}) collective-permute-start(bf16[120,1024]{1,0:T(8,128)(2,1)S(1)} %get-tuple-element.14), channel_id=1, source_target_pairs={{0,2},{1,3},{2,0},{3,1},{16,18},{17,19},{18,16},{19,17},{4,6},{5,7... | collective-permute-start | bytes 737288 | tf_op jit(solution)/shard_map/ppermute | solution.py:199
  182.8 14.6 %collective-permute-start.25 = (bf16[120,1024]{1,0:T(8,128)(2,1)S(1)}, bf16[120,1024]{1,0:T(8,128)(2,1)S(1)}, u32[]{:S(2)}, u32[]{:S(2)}) collective-permute-start(bf16[120,1024]{1,0:T(8,128)(2,1)S(1)} %get-tuple-element.15), channel_id=1, source_target_pairs={{0,16},{1,17},{2,18},{3,19},{16,0},{17,1},{18,2},{19,3},{4,20},{5,... | collective-permute-start | bytes 737288 | tf_op jit(solution)/shard_map/ppermute | solution.py:199
  186.5 11.7 %collective-permute-start.26 = (bf16[120,1024]{1,0:T(8,128)(2,1)S(1)}, bf16[120,1024]{1,0:T(8,128)(2,1)S(1)}, u32[]{:S(2)}, u32[]{:S(2)}) collective-permute-start(bf16[120,1024]{1,0:T(8,128)(2,1)S(1)} %get-tuple-element.16), channel_id=1, source_target_pairs={{0,1},{1,2},{2,3},{3,0},{16,17},{17,18},{18,19},{19,16},{4,5},{5,6... | collective-permute-start | bytes 737288 | tf_op jit(solution)/shard_map/ppermute | solution.py:199
  192.7 7.6 %collective-permute-start.27 = (bf16[120,1024]{1,0:T(8,128)(2,1)S(1)}, bf16[120,1024]{1,0:T(8,128)(2,1)S(1)}, u32[]{:S(2)}, u32[]{:S(2)}) collective-permute-start(bf16[120,1024]{1,0:T(8,128)(2,1)S(1)} %get-tuple-element.17), channel_id=1, source_target_pairs={{0,3},{1,0},{2,1},{3,2},{16,19},{17,16},{18,17},{19,18},{4,7},{5,4... | collective-permute-start | bytes 737288 | tf_op jit(solution)/shard_map/ppermute | solution.py:199
  (16 other events, 213.4 us)
Sparse Core Ops, SparseCore 0:
  22.3 87.2 all-gather.4
  111.4 49.8 all-gather.6

commit v5 on v4

--- a/solution.py
+++ b/solution.py
@@ -11,6 +11,7 @@
 
 ROW = ("yl", "c")
 EXTRA = 8
+GROUP = 8
 MINOR = (((1,), (1,)), ((), ()))
 MAJOR = (((0,), (0,)), ((), ()))
 F32 = jnp.float32
@@ -31,6 +32,19 @@
         value = value + lax.ppermute(value, axis, flip(n, mask))
         mask *= 2
     return value
+
+
+def gate(sent, waited=()):
+    count = len(sent)
+    anywhere = pl.BlockSpec(memory_space=pl.ANY)
+    return pl.pallas_call(
+        lambda *refs: None,
+        out_shape=[jax.ShapeDtypeStruct(a.shape, a.dtype) for a in sent],
+        in_specs=[anywhere] * (count + len(waited)),
+        out_specs=[anywhere] * count,
+        input_output_aliases={i: i for i in range(count)},
+        name="gate",
+    )(*sent, *waited)
 
 
 def hidden_kernel(*refs):
@@ -69,8 +83,8 @@
 def output_kernel(pieces, blocks, *refs):
     hidden_refs, (down_ref, units_ref) = refs[:pieces], refs[pieces : pieces + 2]
     out_refs, (total, col, row) = refs[pieces + 2 : -3], refs[-3:]
-    units = sum(r.shape[0] for r in hidden_refs)
-    width = down_ref.shape[1]
+    group, _, units = units_ref.shape
+    width = down_ref.shape[2]
     rows = total.shape[0] // blocks
 
     @pl.when(pl.program_id(0) == 0)
@@ -78,17 +92,19 @@
         for sums in (total, col, row):
             sums[...] = jnp.zeros_like(sums)
 
-    hidden = jnp.concatenate([r[...].astype(F32) for r in hidden_refs]).astype(BF16)
-    down = down_ref[pl.ds(0, units), :]
+    hidden = jnp.concatenate([r[i] for i in range(group) for r in hidden_refs])
+    down = jnp.concatenate([down_ref[i, pl.ds(0, units), :] for i in range(group)])
     total[...] += lax.dot_general(hidden, down, MAJOR, preferred_element_type=F32)
-    sums = units_ref[...]
-    high = sums.astype(BF16).astype(F32)
-    middle = (sums - high).astype(BF16).astype(F32)
-    rest = jnp.zeros((EXTRA - 3, units), F32)
-    terms = jnp.concatenate([high, middle, sums - high - middle, rest]).astype(BF16)
-    col[...] += jnp.dot(terms, down, preferred_element_type=F32)
-    weights = down_ref[pl.ds(units, EXTRA), pl.ds(0, units)]
-    row[...] += jnp.dot(weights, hidden, preferred_element_type=F32)
+    for i in range(group):
+        span = slice(i * units, (i + 1) * units)
+        sums = units_ref[i]
+        high = sums.astype(BF16).astype(F32)
+        middle = (sums - high).astype(BF16).astype(F32)
+        rest = jnp.zeros((EXTRA - 3, units), F32)
+        terms = jnp.concatenate([high, middle, sums - high - middle, rest]).astype(BF16)
+        col[...] += jnp.dot(terms, down[span], preferred_element_type=F32)
+        weights = down_ref[i, pl.ds(units, EXTRA), pl.ds(0, units)]
+        row[...] += jnp.dot(weights, hidden[span], preferred_element_type=F32)
 
     @pl.when(pl.program_id(0) == pl.num_programs(0) - 1)
     def _():
@@ -117,8 +133,8 @@
     return pl.pallas_call(
         functools.partial(output_kernel, len(hidden), blocks),
         out_shape=[jax.ShapeDtypeStruct(piece, BF16)] * blocks,
-        grid=(steps,),
-        in_specs=[pl.BlockSpec((None, *a.shape[1:]), lambda s: (s, 0, 0)) for a in operands],
+        grid=(steps // math.gcd(steps, GROUP),),
+        in_specs=[pl.BlockSpec((math.gcd(steps, GROUP), *a.shape[1:]), lambda s: (s, 0, 0)) for a in operands],
         out_specs=[pl.BlockSpec(piece, lambda s: (0, 0))] * blocks,
         scratch_shapes=[
             pltpu.VMEM((total, width), F32),
@@ -181,10 +197,13 @@
     other = [swap(m) for m in mine]
 
     hidden = hidden_units(mine, other, weights)
+    unit_sums = sum_over(jnp.sum(hidden.astype(F32), axis=2), "z", nz)
     far = lax.ppermute(hidden, "yl", flip(2, 1))
+    (far,) = gate([far], [unit_sums])
     hidden = [hidden, swap(hidden), far, swap(far)]
-    unit_sums = jnp.concatenate([jnp.sum(h.astype(F32), axis=2) for h in hidden], axis=1)
-    unit_sums = sum_over(unit_sums, "z", nz)[:, None, :]
+    far = lax.ppermute(unit_sums, "yl", flip(2, 1))
+    unit_sums = [unit_sums, swap(unit_sums), far, swap(far)]
+    unit_sums = jnp.concatenate(unit_sums, axis=1)[:, None, :]
 
     targets = [(dy, dx) for dy in range(nyh) for dx in range(nx)]
     far_first = sorted(

time: 211 us -> 211 us (level)
  starting transfers between devices: 31.8 us -> 34.9 us
    ppermute x1, waiting for transfers between devices: 18.4 us -> 0.42 us  [per_device(): far = lax.ppermute(hidden, 'yl', flip(2, 1))]
    all_gather x1, waiting for transfers between devices: 0.02 us -> 11.2 us  [per_device(): down = lax.all_gather(down, 'z', axis=0, tiled=False)]
    ppermute x7, waiting for transfers between devices: 16.6 us -> 18.9 us  [per_device(): piece = lax.ppermute(piece, ('yh', 'x'), perm)]
    unnamed x23 -> x27, local copies, waits for them, and re-layouts: 2.5 us -> 4.51 us
  transfers between devices with their start and end apart: 30 -> 33, of which waited for: 23 -> 25; matrix products, arithmetic and copies ran while one was open for 2% -> 2% of each run, Pallas kernels for 7% -> 7%
where the time goes in v5:
time: 211 us
  waiting for transfers between devices  128 us (61%)
  starting transfers between devices  34.9 us (17%)
  Pallas kernels  20.6 us (10%)
  between operations  14.3 us (7%)
  other arithmetic  7.33 us (3%)
  local copies, waits for them, and re-layouts  6.12 us (3%)
    ppermute x3, waiting for transfers between devices, across(): return lax.ppermute(array, ('yh', 'yl'), flip(nyh * nyl, mask))  42.2 us
    ppermute x7, waiting for transfers between devices, per_device(): piece = lax.ppermute(piece, ('yh', 'x'), perm)  18.9 us
    all_gather x1, waiting for transfers between devices, per_device(): lax.all_gather(jnp.concatenate(weights, axis=1), 'z', axis=0, tiled=False)  18.2 us
    ppermute x5, waiting for transfers between devices, sum_over(): value = value + lax.ppermute(value, axis, flip(n, mask))  14.1 us
    pallas_call x1, Pallas kernels, hidden_units(): pl.pallas_call(hidden_kernel, out_shape=jax.ShapeDtypeStruct((count, unit...  14 us
    ppermute x7, starting transfers between devices, per_device(): piece = lax.ppermute(piece, ('yh', 'x'), perm)  13.4 us
    all_gather x1, waiting for transfers between devices, per_device(): down = lax.all_gather(down, 'z', axis=0, tiled=False)  11.2 us
    ppermute x3, waiting for transfers between devices, per_device(): weights.append(piece if k == 0 else lax.ppermute(piece, ROW, flip(nrow, k)))  10.6 us
  transfers between devices with their start and end apart: 33, of which 25 were waited for; matrix products, arithmetic and copies ran while one was open for 2% of the time, Pallas kernels for 7%

profile of v5, /device:TPU:4, one launch (start us, length us, event | category | flops | bytes accessed | tf_op | source)
XLA Modules:
  0.0 210.8 jit_solution(387972565615764138)
XLA Ops:
  10.6 6.6 %collective-permute-done.11 = bf16[112,1024]{1,0:T(8,128)(2,1)S(1)} collective-permute-done((bf16[112,1024]{1,0:T(8,128)(2,1)S(1)}, bf16[112,1024]{1,0:T(8,128)(2,1)S(1)}, u32[]{:S(2)}, u32[]{:S(2)}) %collective-permute-start.11) | collective-permute-done | bytes 229408 | tf_op jit(solution)/shard_map/ppermute | solution.py:174
  17.2 4.0 %collective-permute-done.12 = bf16[112,1024]{1,0:T(8,128)(2,1)S(1)} collective-permute-done((bf16[112,1024]{1,0:T(8,128)(2,1)S(1)}, bf16[112,1024]{1,0:T(8,128)(2,1)S(1)}, u32[]{:S(2)}, u32[]{:S(2)}) %collective-permute-start.12) | collective-permute-done | bytes 229408 | tf_op jit(solution)/shard_map/ppermute | solution.py:174
  28.9 2.7 %collective-permute-start.1 = (bf16[112,1024]{1,0:T(8,128)(2,1)S(1)}, bf16[112,1024]{1,0:T(8,128)(2,1)S(1)}, u32[]{:S(2)}, u32[]{:S(2)}) collective-permute-start(bf16[112,1024]{1,0:T(8,128)(2,1)S(1)} %copy-done.4), channel_id=1, source_target_pairs={{0,2},{1,3},{2,0},{3,1},{4,6},{5,7},{6,4},{7,5},{8,10},{9,11},{10,... | collective-permute-start | bytes 688136 | tf_op jit(solution)/shard_map/ppermute | solution.py:194
  33.3 3.7 %collective-permute-done = bf16[112,1024]{1,0:T(8,128)(2,1)S(1)} collective-permute-done((bf16[112,1024]{1,0:T(8,128)(2,1)S(1)}, bf16[112,1024]{1,0:T(8,128)(2,1)S(1)}, u32[]{:S(2)}, u32[]{:S(2)}) %collective-permute-start) | collective-permute-done | bytes 229408 | tf_op jit(solution)/shard_map/ppermute | solution.py:194
  39.0 2.7 %collective-permute-done.2 = bf16[112,1024]{1,0:T(8,128)(2,1)S(1)} collective-permute-done((bf16[112,1024]{1,0:T(8,128)(2,1)S(1)}, bf16[112,1024]{1,0:T(8,128)(2,1)S(1)}, u32[]{:S(2)}, u32[]{:S(2)}) %collective-permute-start.2) | collective-permute-done | bytes 229408 | tf_op jit(solution)/shard_map/ppermute | solution.py:194
  43.4 2.9 %collective-permute-start.4 = (bf16[448,1024]{1,0:T(8,128)(2,1)S(1)}, bf16[448,1024]{1,0:T(8,128)(2,1)S(1)}, u32[]{:S(2)}, u32[]{:S(2)}) collective-permute-start(bf16[448,1024]{1,0:T(8,128)(2,1)S(1)} %constant_dynamic-update-slice_fusion.refs_0_), channel_id=1, source_target_pairs={{0,16},{8,24},{16,0},{24,8},{1,17},{9,25},{17,1},{25,9},{2,18},{10... | collective-permute-start | bytes 2752520 | tf_op jit(solution)/shard_map/ppermute | solution.py:164
  46.6 18.5 %collective-permute-done.3.refs_1_ = bf16[448,1024]{1,0:T(8,128)(2,1)S(1)} collective-permute-done((bf16[448,1024]{1,0:T(8,128)(2,1)S(1)}, bf16[448,1024]{1,0:T(8,128)(2,1)S(1)}, u32[]{:S(2)}, u32[]{:S(2)}) %collective-permute-start.3) | collective-permute-done | bytes 917536 | tf_op jit(solution)/shard_map/ppermute | solution.py:164
  65.1 21.2 %collective-permute-done.4.refs_2_ = bf16[448,1024]{1,0:T(8,128)(2,1)S(1)} collective-permute-done((bf16[448,1024]{1,0:T(8,128)(2,1)S(1)}, bf16[448,1024]{1,0:T(8,128)(2,1)S(1)}, u32[]{:S(2)}, u32[]{:S(2)}) %collective-permute-start.4) | collective-permute-done | bytes 917536 | tf_op jit(solution)/shard_map/ppermute | solution.py:164
  86.3 2.6 %collective-permute-done.5.refs_3_ = bf16[448,1024]{1,0:T(8,128)(2,1)S(1)} collective-permute-done((bf16[448,1024]{1,0:T(8,128)(2,1)S(1)}, bf16[448,1024]{1,0:T(8,128)(2,1)S(1)}, u32[]{:S(2)}, u32[]{:S(2)}) %collective-permute-start.5) | collective-permute-done | bytes 917536 | tf_op jit(solution)/shard_map/ppermute | solution.py:164
  91.4 18.2 %all-gather.5.cloned.1.call-done.refs_8_ = bf16[896,4096]{1,0:T(8,128)(2,1)} async-done(((bf16[112,4096]{1,0:T(8,128)(2,1)}), bf16[896,4096]{1,0:T(8,128)(2,1)}) %all-gather.5.cloned.1.call-update) | async-done | bytes 7340048 | tf_op jit(solution)/shard_map/all_gather | solution.py:175
  109.6 14.0 %hidden.1.refs_0_ = bf16[8,56,896]{2,1,0:T(8,128)(2,1)} custom-call(bf16[448,1024]{1,0:T(8,128)(2,1)} %copy-done.5, bf16[448,1024]{1,0:T(8,128)(2,1)} %copy-done.6, bf16[448,1024]{1,0:T(8,128)(2,1)} %copy-done.7, bf16[448,1024]{1,0:T(8,128)(2,1)} %copy-done.8, bf16[448,1024]{1,0:T(8,128)(2,1)} %copy-done.9, bf16[448,1024]{1,0:T(8,128)(2,1)} %copy-done.10, ...), custom_call_target="tpu_custom_call" | custom-call | flops 6576668672 | bytes 14680064 | tf_op jit(solution)/shard_map/hidden/pallas_call | solution.py:70
  126.6 3.7 %collective-permute-done.15 = f32[8,56]{1,0:T(8,128)S(1)} collective-permute-done((f32[8,56]{1,0:T(8,128)S(1)}, f32[8,56]{1,0:T(8,128)S(1)}, u32[]{:S(2)}, u32[]{:S(2)}) %collective-permute-start.15) | collective-permute-done | bytes 1824 | tf_op jit(solution)/shard_map/ppermute | solution.py:32
  131.7 3.2 %collective-permute-done.16 = f32[8,56]{1,0:T(8,128)S(1)} collective-permute-done((f32[8,56]{1,0:T(8,128)S(1)}, f32[8,56]{1,0:T(8,128)S(1)}, u32[]{:S(2)}, u32[]{:S(2)}) %collective-permute-start.16) | collective-permute-done | bytes 1824 | tf_op jit(solution)/shard_map/ppermute | solution.py:32
  134.9 3.0 %collective-permute-start.17 = (f32[8,56]{1,0:T(8,128)S(1)}, f32[8,56]{1,0:T(8,128)S(1)}, u32[]{:S(2)}, u32[]{:S(2)}) collective-permute-start(f32[8,56]{1,0:T(8,128)S(1)} %add.159), channel_id=1, source_target_pairs={{0,128},{32,160},{64,192},{96,224},{128,0},{160,32},{192,64},{224,... | collective-permute-start | bytes 5384 | tf_op jit(solution)/shard_map/ppermute | solution.py:32
  137.9 4.6 %collective-permute-done.17 = f32[8,56]{1,0:T(8,128)S(1)} collective-permute-done((f32[8,56]{1,0:T(8,128)S(1)}, f32[8,56]{1,0:T(8,128)S(1)}, u32[]{:S(2)}, u32[]{:S(2)}) %collective-permute-start.17) | collective-permute-done | bytes 1824 | tf_op jit(solution)/shard_map/ppermute | solution.py:32
  150.2 11.2 %all-gather.7.cloned.1.call-done = bf16[1856,1024]{1,0:T(8,128)(2,1)} async-done(((bf16[232,1024]{1,0:T(8,128)(2,1)}), bf16[1856,1024]{1,0:T(8,128)(2,1)}) %all-gather.7.cloned.1.call-update) | async-done | bytes 3801104 | tf_op jit(solution)/shard_map/all_gather | solution.py:191
  162.5 6.5 %outputs.1 = (bf16[120,1024]{1,0:T(8,128)(2,1)S(1)}, bf16[120,1024]{1,0:T(8,128)(2,1)S(1)}, bf16[120,1024]{1,0:T(8,128)(2,1)S(1)}, bf16[120,1024]{1,0:T(8,128)(2...) custom-call(bf16[8,56,896]{2,1,0:T(8,128)(2,1)S(1)} %copy-done, ...), custom_call_target="tpu_custom_call" | custom-call | flops 3288334336 | bytes 8716288 | tf_op jit(solution)/shard_map/outputs/pallas_call | solution.py:133
  169.0 3.1 %collective-permute-start.24 = (bf16[120,1024]{1,0:T(8,128)(2,1)S(1)}, bf16[120,1024]{1,0:T(8,128)(2,1)S(1)}, u32[]{:S(2)}, u32[]{:S(2)}) collective-permute-start(bf16[120,1024]{1,0:T(8,128)(2,1)S(1)} %get-tuple-element.11), channel_id=1, source_target_pairs={{0,18},{1,19},{2,16},{3,17},{16,2},{17,3},{18,0},{19,1},{4,22},{5,... | collective-permute-start | bytes 737288 | tf_op jit(solution)/shard_map/ppermute | solution.py:218
  174.1 2.4 %collective-permute-start.26 = (bf16[120,1024]{1,0:T(8,128)(2,1)S(1)}, bf16[120,1024]{1,0:T(8,128)(2,1)S(1)}, u32[]{:S(2)}, u32[]{:S(2)}) collective-permute-start(bf16[120,1024]{1,0:T(8,128)(2,1)S(1)} %get-tuple-element.13), channel_id=1, source_target_pairs={{0,19},{1,16},{2,17},{3,18},{16,3},{17,0},{18,1},{19,2},{4,23},{5,... | collective-permute-start | bytes 737288 | tf_op jit(solution)/shard_map/ppermute | solution.py:218
  176.5 4.2 %collective-permute-start.27 = (bf16[120,1024]{1,0:T(8,128)(2,1)S(1)}, bf16[120,1024]{1,0:T(8,128)(2,1)S(1)}, u32[]{:S(2)}, u32[]{:S(2)}) collective-permute-start(bf16[120,1024]{1,0:T(8,128)(2,1)S(1)} %get-tuple-element.14), channel_id=1, source_target_pairs={{0,2},{1,3},{2,0},{3,1},{16,18},{17,19},{18,16},{19,17},{4,6},{5,7... | collective-permute-start | bytes 737288 | tf_op jit(solution)/shard_map/ppermute | solution.py:218
  181.2 2.3 %collective-permute-done.24 = bf16[120,1024]{1,0:T(8,128)(2,1)S(1)} collective-permute-done((bf16[120,1024]{1,0:T(8,128)(2,1)S(1)}, bf16[120,1024]{1,0:T(8,128)(2,1)S(1)}, u32[]{:S(2)}, u32[]{:S(2)}) %collective-permute-start.24) | collective-permute-done | bytes 245792 | tf_op jit(solution)/shard_map/ppermute | solution.py:218
  184.7 9.3 %collective-permute-done.25 = bf16[120,1024]{1,0:T(8,128)(2,1)S(1)} collective-permute-done((bf16[120,1024]{1,0:T(8,128)(2,1)S(1)}, bf16[120,1024]{1,0:T(8,128)(2,1)S(1)}, u32[]{:S(2)}, u32[]{:S(2)}) %collective-permute-start.25) | collective-permute-done | bytes 245792 | tf_op jit(solution)/shard_map/ppermute | solution.py:218
  196.6 2.2 %collective-permute-done.29 = bf16[120,1024]{1,0:T(8,128)(2,1)S(1)} collective-permute-done((bf16[120,1024]{1,0:T(8,128)(2,1)S(1)}, bf16[120,1024]{1,0:T(8,128)(2,1)S(1)}, u32[]{:S(2)}, u32[]{:S(2)}) %collective-permute-start.29) | collective-permute-done | bytes 245792 | tf_op jit(solution)/shard_map/ppermute | solution.py:218
  198.8 2.9 %collective-permute-done.30 = bf16[120,1024]{1,0:T(8,128)(2,1)S(1)} collective-permute-done((bf16[120,1024]{1,0:T(8,128)(2,1)S(1)}, bf16[120,1024]{1,0:T(8,128)(2,1)S(1)}, u32[]{:S(2)}, u32[]{:S(2)}) %collective-permute-start.30) | collective-permute-done | bytes 245792 | tf_op jit(solution)/shard_map/ppermute | solution.py:218
  (107 shorter events, 40.9 us)
Async XLA Ops:
  7.2 102.5 %all-gather.5.cloned.1.call-start = ((), (), s32[]{:S(2)}) async-start(), calls=%async_computation | async-start | bytes 8257536 | tf_op jit(solution)/shard_map/all_gather | solution.py:175
  8.7 8.5 %collective-permute-start.11 = (bf16[112,1024]{1,0:T(8,128)(2,1)S(1)}, bf16[112,1024]{1,0:T(8,128)(2,1)S(1)}, u32[]{:S(2)}, u32[]{:S(2)}) collective-permute-start(bf16[112,1024]{1,0:T(8,128)(2,1)S(1)} %bitcast.28), channel_id=1, source_target_pairs={{0,8},{4,12},{8,0},{12,4},{1,9},{5,13},{9,1},{13,5},{2,10},{6,14},... | collective-permute-start | bytes 688136 | tf_op jit(solution)/shard_map/ppermute | solution.py:174
  10.4 10.8 %collective-permute-start.12 = (bf16[112,1024]{1,0:T(8,128)(2,1)S(1)}, bf16[112,1024]{1,0:T(8,128)(2,1)S(1)}, u32[]{:S(2)}, u32[]{:S(2)}) collective-permute-start(bf16[112,1024]{1,0:T(8,128)(2,1)S(1)} %bitcast.27), channel_id=1, source_target_pairs={{0,12},{4,8},{8,4},{12,0},{1,13},{5,9},{9,5},{13,1},{2,14},{6,10},... | collective-permute-start | bytes 688136 | tf_op jit(solution)/shard_map/ppermute | solution.py:174
  22.2 139.1 %all-gather.7.cloned.1.call-start = ((), (), s32[]{:S(2)}) async-start(), calls=%async_computation.1 | async-start | bytes 4276224 | tf_op jit(solution)/shard_map/all_gather | solution.py:191
  28.3 8.6 %collective-permute-start = (bf16[112,1024]{1,0:T(8,128)(2,1)S(1)}, bf16[112,1024]{1,0:T(8,128)(2,1)S(1)}, u32[]{:S(2)}, u32[]{:S(2)}) collective-permute-start(bf16[112,1024]{1,0:T(8,128)(2,1)S(1)} %copy-done.4), channel_id=1, source_target_pairs={{0,3},{1,0},{2,1},{3,2},{4,7},{5,4},{6,5},{7,6},{8,11},{9,8},{10,9... | collective-permute-start | bytes 688136 | tf_op jit(solution)/shard_map/ppermute | solution.py:194
  28.9 10.1 %collective-permute-start.1 = (bf16[112,1024]{1,0:T(8,128)(2,1)S(1)}, bf16[112,1024]{1,0:T(8,128)(2,1)S(1)}, u32[]{:S(2)}, u32[]{:S(2)}) collective-permute-start(bf16[112,1024]{1,0:T(8,128)(2,1)S(1)} %copy-done.4), channel_id=1, source_target_pairs={{0,2},{1,3},{2,0},{3,1},{4,6},{5,7},{6,4},{7,5},{8,10},{9,11},{10,... | collective-permute-start | bytes 688136 | tf_op jit(solution)/shard_map/ppermute | solution.py:194
  31.7 10.1 %collective-permute-start.2 = (bf16[112,1024]{1,0:T(8,128)(2,1)S(1)}, bf16[112,1024]{1,0:T(8,128)(2,1)S(1)}, u32[]{:S(2)}, u32[]{:S(2)}) collective-permute-start(bf16[112,1024]{1,0:T(8,128)(2,1)S(1)} %copy-done.4), channel_id=1, source_target_pairs={{0,1},{1,2},{2,3},{3,0},{4,5},{5,6},{6,7},{7,4},{8,9},{9,10},{10,1... | collective-permute-start | bytes 688136 | tf_op jit(solution)/shard_map/ppermute | solution.py:194
  41.8 23.3 %collective-permute-start.3 = (bf16[448,1024]{1,0:T(8,128)(2,1)S(1)}, bf16[448,1024]{1,0:T(8,128)(2,1)S(1)}, u32[]{:S(2)}, u32[]{:S(2)}) collective-permute-start(bf16[448,1024]{1,0:T(8,128)(2,1)S(1)} %constant_dynamic-update-slice_fusion.refs_0_), channel_id=1, source_target_pairs={{0,8},{8,0},{16,24},{24,16},{1,9},{9,1},{17,25},{25,17},{2,10},{10... | collective-permute-start | bytes 2752520 | tf_op jit(solution)/shard_map/ppermute | solution.py:164
  43.4 42.8 %collective-permute-start.4 = (bf16[448,1024]{1,0:T(8,128)(2,1)S(1)}, bf16[448,1024]{1,0:T(8,128)(2,1)S(1)}, u32[]{:S(2)}, u32[]{:S(2)}) collective-permute-start(bf16[448,1024]{1,0:T(8,128)(2,1)S(1)} %constant_dynamic-update-slice_fusion.refs_0_), channel_id=1, source_target_pairs={{0,16},{8,24},{16,0},{24,8},{1,17},{9,25},{17,1},{25,9},{2,18},{10... | collective-permute-start | bytes 2752520 | tf_op jit(solution)/shard_map/ppermute | solution.py:164
  46.3 42.5 %collective-permute-start.5 = (bf16[448,1024]{1,0:T(8,128)(2,1)S(1)}, bf16[448,1024]{1,0:T(8,128)(2,1)S(1)}, u32[]{:S(2)}, u32[]{:S(2)}) collective-permute-start(bf16[448,1024]{1,0:T(8,128)(2,1)S(1)} %constant_dynamic-update-slice_fusion.refs_0_), channel_id=1, source_target_pairs={{0,24},{8,16},{16,8},{24,0},{1,25},{9,17},{17,9},{25,1},{2,26},{10... | collective-permute-start | bytes 2752520 | tf_op jit(solution)/shard_map/ppermute | solution.py:164
  46.6 42.3 %collective-permute-start.6 = (bf16[448,1024]{1,0:T(8,128)(2,1)S(1)}, bf16[448,1024]{1,0:T(8,128)(2,1)S(1)}, u32[]{:S(2)}, u32[]{:S(2)}) collective-permute-start(bf16[448,1024]{1,0:T(8,128)(2,1)S(1)} %constant_dynamic-update-slice_fusion.refs_0_), channel_id=1, source_target_pairs={{0,4},{4,0},{1,5},{5,1},{2,6},{6,2},{3,7},{7,3},{8,12},{12,8},{9,1... | collective-permute-start | bytes 2752520 | tf_op jit(solution)/shard_map/ppermute | solution.py:167
  65.1 23.8 %collective-permute-start.7 = (bf16[448,1024]{1,0:T(8,128)(2,1)S(1)}, bf16[448,1024]{1,0:T(8,128)(2,1)S(1)}, u32[]{:S(2)}, u32[]{:S(2)}) collective-permute-start(bf16[448,1024]{1,0:T(8,128)(2,1)S(1)} %collective-permute-done.3.refs_1_), channel_id=1, source_target_pairs={{0,4},{4,0},{1,5},{5,1},{2,6},{6,2},{3,7},{7,3},{8,12},{12,8},{9,1... | collective-permute-start | bytes 2752520 | tf_op jit(solution)/shard_map/ppermute | solution.py:167
  123.7 19.8 %collective-permute-start.14 = (bf16[8,56,896]{2,1,0:T(8,128)(2,1)}, bf16[8,56,896]{2,1,0:T(8,128)(2,1)S(1)}, u32[]{:S(2)}, u32[]{:S(2)}) collective-permute-start(bf16[8,56,896]{2,1,0:T(8,128)(2,1)} %hidden.1.refs_0_), channel_id=1, source_target_pairs={{0,8},{8,0},{1,9},{9,1},{2,10},{10,2},{3,11},{11,3},{4,12},{12,4},... | collective-permute-start | bytes 2408456 | tf_op jit(solution)/shard_map/ppermute | solution.py:201
  130.3 4.6 %collective-permute-start.16 = (f32[8,56]{1,0:T(8,128)S(1)}, f32[8,56]{1,0:T(8,128)S(1)}, u32[]{:S(2)}, u32[]{:S(2)}) collective-permute-start(f32[8,56]{1,0:T(8,128)S(1)} %add.158), channel_id=1, source_target_pairs={{0,64},{32,96},{64,0},{96,32},{128,192},{160,224},{192,128},{224,1... | collective-permute-start | bytes 5384 | tf_op jit(solution)/shard_map/ppermute | solution.py:32
  134.9 7.6 %collective-permute-start.17 = (f32[8,56]{1,0:T(8,128)S(1)}, f32[8,56]{1,0:T(8,128)S(1)}, u32[]{:S(2)}, u32[]{:S(2)}) collective-permute-start(f32[8,56]{1,0:T(8,128)S(1)} %add.159), channel_id=1, source_target_pairs={{0,128},{32,160},{64,192},{96,224},{128,0},{160,32},{192,64},{224,... | collective-permute-start | bytes 5384 | tf_op jit(solution)/shard_map/ppermute | solution.py:32
  137.9 23.4 %collective-permute-start.13 = (bf16[8,56,896]{2,1,0:T(8,128)(2,1)}, bf16[8,56,896]{2,1,0:T(8,128)(2,1)S(1)}, u32[]{:S(2)}, u32[]{:S(2)}) collective-permute-start(bf16[8,56,896]{2,1,0:T(8,128)(2,1)} %hidden.1.refs_0_), channel_id=1, source_target_pairs={{0,4},{4,0},{1,5},{5,1},{2,6},{6,2},{3,7},{7,3},{8,12},{12,8},{9,1... | collective-permute-start | bytes 2408456 | tf_op jit(solution)/shard_map/ppermute | solution.py:167
  144.4 16.9 %collective-permute-start.18 = (bf16[8,56,896]{2,1,0:T(8,128)(2,1)}, bf16[8,56,896]{2,1,0:T(8,128)(2,1)S(1)}, u32[]{:S(2)}, u32[]{:S(2)}) collective-permute-start(bf16[8,56,896]{2,1,0:T(8,128)(2,1)} %gate.1.refs_2_), channel_id=1, source_target_pairs={{0,4},{4,0},{1,5},{5,1},{2,6},{6,2},{3,7},{7,3},{8,12},{12,8},{9,1... | collective-permute-start | bytes 2408456 | tf_op jit(solution)/shard_map/ppermute | solution.py:167
  169.0 14.6 %collective-permute-start.24 = (bf16[120,1024]{1,0:T(8,128)(2,1)S(1)}, bf16[120,1024]{1,0:T(8,128)(2,1)S(1)}, u32[]{:S(2)}, u32[]{:S(2)}) collective-permute-start(bf16[120,1024]{1,0:T(8,128)(2,1)S(1)} %get-tuple-element.11), channel_id=1, source_target_pairs={{0,18},{1,19},{2,16},{3,17},{16,2},{17,3},{18,0},{19,1},{4,22},{5,... | collective-permute-start | bytes 737288 | tf_op jit(solution)/shard_map/ppermute | solution.py:218
  172.1 21.9 %collective-permute-start.25 = (bf16[120,1024]{1,0:T(8,128)(2,1)S(1)}, bf16[120,1024]{1,0:T(8,128)(2,1)S(1)}, u32[]{:S(2)}, u32[]{:S(2)}) collective-permute-start(bf16[120,1024]{1,0:T(8,128)(2,1)S(1)} %get-tuple-element.12), channel_id=1, source_target_pairs={{0,17},{1,18},{2,19},{3,16},{16,1},{17,2},{18,3},{19,0},{4,21},{5,... | collective-permute-start | bytes 737288 | tf_op jit(solution)/shard_map/ppermute | solution.py:218
  174.1 20.1 %collective-permute-start.26 = (bf16[120,1024]{1,0:T(8,128)(2,1)S(1)}, bf16[120,1024]{1,0:T(8,128)(2,1)S(1)}, u32[]{:S(2)}, u32[]{:S(2)}) collective-permute-start(bf16[120,1024]{1,0:T(8,128)(2,1)S(1)} %get-tuple-element.13), channel_id=1, source_target_pairs={{0,19},{1,16},{2,17},{3,18},{16,3},{17,0},{18,1},{19,2},{4,23},{5,... | collective-permute-start | bytes 737288 | tf_op jit(solution)/shard_map/ppermute | solution.py:218
  176.5 19.2 %collective-permute-start.27 = (bf16[120,1024]{1,0:T(8,128)(2,1)S(1)}, bf16[120,1024]{1,0:T(8,128)(2,1)S(1)}, u32[]{:S(2)}, u32[]{:S(2)}) collective-permute-start(bf16[120,1024]{1,0:T(8,128)(2,1)S(1)} %get-tuple-element.14), channel_id=1, source_target_pairs={{0,2},{1,3},{2,0},{3,1},{16,18},{17,19},{18,16},{19,17},{4,6},{5,7... | collective-permute-start | bytes 737288 | tf_op jit(solution)/shard_map/ppermute | solution.py:218
  180.7 15.8 %collective-permute-start.28 = (bf16[120,1024]{1,0:T(8,128)(2,1)S(1)}, bf16[120,1024]{1,0:T(8,128)(2,1)S(1)}, u32[]{:S(2)}, u32[]{:S(2)}) collective-permute-start(bf16[120,1024]{1,0:T(8,128)(2,1)S(1)} %get-tuple-element.15), channel_id=1, source_target_pairs={{0,16},{1,17},{2,18},{3,19},{16,0},{17,1},{18,2},{19,3},{4,20},{5,... | collective-permute-start | bytes 737288 | tf_op jit(solution)/shard_map/ppermute | solution.py:218
  183.6 15.2 %collective-permute-start.29 = (bf16[120,1024]{1,0:T(8,128)(2,1)S(1)}, bf16[120,1024]{1,0:T(8,128)(2,1)S(1)}, u32[]{:S(2)}, u32[]{:S(2)}) collective-permute-start(bf16[120,1024]{1,0:T(8,128)(2,1)S(1)} %get-tuple-element.16), channel_id=1, source_target_pairs={{0,1},{1,2},{2,3},{3,0},{16,17},{17,18},{18,19},{19,16},{4,5},{5,6... | collective-permute-start | bytes 737288 | tf_op jit(solution)/shard_map/ppermute | solution.py:218
  194.1 7.6 %collective-permute-start.30 = (bf16[120,1024]{1,0:T(8,128)(2,1)S(1)}, bf16[120,1024]{1,0:T(8,128)(2,1)S(1)}, u32[]{:S(2)}, u32[]{:S(2)}) collective-permute-start(bf16[120,1024]{1,0:T(8,128)(2,1)S(1)} %get-tuple-element.17), channel_id=1, source_target_pairs={{0,3},{1,0},{2,1},{3,2},{16,19},{17,16},{18,17},{19,18},{4,7},{5,4... | collective-permute-start | bytes 737288 | tf_op jit(solution)/shard_map/ppermute | solution.py:218
  (21 other events, 222.9 us)
Sparse Core Ops, SparseCore 0:
  22.3 87.2 all-gather.4
  111.4 49.8 all-gather.6

commit v6 on v5

--- a/solution.py
+++ b/solution.py
@@ -206,12 +206,10 @@
     unit_sums = jnp.concatenate(unit_sums, axis=1)[:, None, :]
 
     targets = [(dy, dx) for dy in range(nyh) for dx in range(nx)]
-    far_first = sorted(
-        range(len(targets)), key=lambda j: -2 * targets[j][0] - min(targets[j][1], nx - targets[j][1])
-    )
+    leave = [targets.index(t) for t in ((1, 1), (0, 2), (1, 3), (1, 2), (1, 0), (0, 1), (0, 3), (0, 0))]
     sent = outputs(hidden, down, unit_sums, len(targets))
     received = {}
-    for j in far_first:
+    for j in leave:
         (dy, dx), piece = targets[j], sent[j]
         perm = [(h * nx + i, (h ^ dy) * nx + (i + dx) % nx) for h in range(nyh) for i in range(nx)]
         if dx or dy:

time: 211 us -> 208 us (0.986)
  waiting for transfers between devices: 128 us -> 123 us
    ppermute x7, waiting for transfers between devices: 18.9 us -> 14.8 us  [per_device(): piece = lax.ppermute(piece, ('yh', 'x'), perm)]
  transfers between devices with their start and end apart: 33 -> 33, of which waited for: 25 -> 23; matrix products, arithmetic and copies ran while one was open for 2% -> 2% of each run, Pallas kernels for 7% -> 7%
where the time goes in v6:
time: 208 us; the launch traced here: 206 us
  waiting for transfers between devices  123 us (59%)
  starting transfers between devices  34.3 us (16%)
  Pallas kernels  20.6 us (10%)
  between operations  14.3 us (7%)
  other arithmetic  7.33 us (4%)
  local copies, waits for them, and re-layouts  6.12 us (3%)
    ppermute x3, waiting for transfers between devices, across(): return lax.ppermute(array, ('yh', 'yl'), flip(nyh * nyl, mask))  42.2 us
    all_gather x1, waiting for transfers between devices, per_device(): lax.all_gather(jnp.concatenate(weights, axis=1), 'z', axis=0, tiled=False)  18.2 us
    ppermute x7, waiting for transfers between devices, per_device(): piece = lax.ppermute(piece, ('yh', 'x'), perm)  14.8 us
    ppermute x5, waiting for transfers between devices, sum_over(): value = value + lax.ppermute(value, axis, flip(n, mask))  14.1 us
    pallas_call x1, Pallas kernels, hidden_units(): pl.pallas_call(hidden_kernel, out_shape=jax.ShapeDtypeStruct((count, unit...  14 us
    ppermute x7, starting transfers between devices, per_device(): piece = lax.ppermute(piece, ('yh', 'x'), perm)  12.8 us
    all_gather x1, waiting for transfers between devices, per_device(): down = lax.all_gather(down, 'z', axis=0, tiled=False)  11.2 us
    ppermute x3, waiting for transfers between devices, per_device(): weights.append(piece if k == 0 else lax.ppermute(piece, ROW, flip(nrow, k)))  10.6 us
  transfers between devices with their start and end apart: 33, of which 23 were waited for; matrix products, arithmetic and copies ran while one was open for 2% of the time, Pallas kernels for 7%

profile of v6, /device:TPU:4, one launch (start us, length us, event | category | flops | bytes accessed | tf_op | source)
XLA Modules:
  0.0 206.1 jit_solution(12919901627052175134)
XLA Ops:
  10.6 6.6 %collective-permute-done.11 = bf16[112,1024]{1,0:T(8,128)(2,1)S(1)} collective-permute-done((bf16[112,1024]{1,0:T(8,128)(2,1)S(1)}, bf16[112,1024]{1,0:T(8,128)(2,1)S(1)}, u32[]{:S(2)}, u32[]{:S(2)}) %collective-permute-start.11) | collective-permute-done | bytes 229408 | tf_op jit(solution)/shard_map/ppermute | solution.py:174
  17.2 4.0 %collective-permute-done.12 = bf16[112,1024]{1,0:T(8,128)(2,1)S(1)} collective-permute-done((bf16[112,1024]{1,0:T(8,128)(2,1)S(1)}, bf16[112,1024]{1,0:T(8,128)(2,1)S(1)}, u32[]{:S(2)}, u32[]{:S(2)}) %collective-permute-start.12) | collective-permute-done | bytes 229408 | tf_op jit(solution)/shard_map/ppermute | solution.py:174
  28.9 2.7 %collective-permute-start.1 = (bf16[112,1024]{1,0:T(8,128)(2,1)S(1)}, bf16[112,1024]{1,0:T(8,128)(2,1)S(1)}, u32[]{:S(2)}, u32[]{:S(2)}) collective-permute-start(bf16[112,1024]{1,0:T(8,128)(2,1)S(1)} %copy-done.4), channel_id=1, source_target_pairs={{0,2},{1,3},{2,0},{3,1},{4,6},{5,7},{6,4},{7,5},{8,10},{9,11},{10,... | collective-permute-start | bytes 688136 | tf_op jit(solution)/shard_map/ppermute | solution.py:194
  33.3 3.7 %collective-permute-done = bf16[112,1024]{1,0:T(8,128)(2,1)S(1)} collective-permute-done((bf16[112,1024]{1,0:T(8,128)(2,1)S(1)}, bf16[112,1024]{1,0:T(8,128)(2,1)S(1)}, u32[]{:S(2)}, u32[]{:S(2)}) %collective-permute-start) | collective-permute-done | bytes 229408 | tf_op jit(solution)/shard_map/ppermute | solution.py:194
  39.0 2.7 %collective-permute-done.2 = bf16[112,1024]{1,0:T(8,128)(2,1)S(1)} collective-permute-done((bf16[112,1024]{1,0:T(8,128)(2,1)S(1)}, bf16[112,1024]{1,0:T(8,128)(2,1)S(1)}, u32[]{:S(2)}, u32[]{:S(2)}) %collective-permute-start.2) | collective-permute-done | bytes 229408 | tf_op jit(solution)/shard_map/ppermute | solution.py:194
  43.4 2.9 %collective-permute-start.4 = (bf16[448,1024]{1,0:T(8,128)(2,1)S(1)}, bf16[448,1024]{1,0:T(8,128)(2,1)S(1)}, u32[]{:S(2)}, u32[]{:S(2)}) collective-permute-start(bf16[448,1024]{1,0:T(8,128)(2,1)S(1)} %constant_dynamic-update-slice_fusion.refs_0_), channel_id=1, source_target_pairs={{0,16},{8,24},{16,0},{24,8},{1,17},{9,25},{17,1},{25,9},{2,18},{10... | collective-permute-start | bytes 2752520 | tf_op jit(solution)/shard_map/ppermute | solution.py:164
  46.6 18.5 %collective-permute-done.3.refs_1_ = bf16[448,1024]{1,0:T(8,128)(2,1)S(1)} collective-permute-done((bf16[448,1024]{1,0:T(8,128)(2,1)S(1)}, bf16[448,1024]{1,0:T(8,128)(2,1)S(1)}, u32[]{:S(2)}, u32[]{:S(2)}) %collective-permute-start.3) | collective-permute-done | bytes 917536 | tf_op jit(solution)/shard_map/ppermute | solution.py:164
  65.1 21.2 %collective-permute-done.4.refs_2_ = bf16[448,1024]{1,0:T(8,128)(2,1)S(1)} collective-permute-done((bf16[448,1024]{1,0:T(8,128)(2,1)S(1)}, bf16[448,1024]{1,0:T(8,128)(2,1)S(1)}, u32[]{:S(2)}, u32[]{:S(2)}) %collective-permute-start.4) | collective-permute-done | bytes 917536 | tf_op jit(solution)/shard_map/ppermute | solution.py:164
  86.3 2.6 %collective-permute-done.5.refs_3_ = bf16[448,1024]{1,0:T(8,128)(2,1)S(1)} collective-permute-done((bf16[448,1024]{1,0:T(8,128)(2,1)S(1)}, bf16[448,1024]{1,0:T(8,128)(2,1)S(1)}, u32[]{:S(2)}, u32[]{:S(2)}) %collective-permute-start.5) | collective-permute-done | bytes 917536 | tf_op jit(solution)/shard_map/ppermute | solution.py:164
  91.4 18.2 %all-gather.5.cloned.1.call-done.refs_8_ = bf16[896,4096]{1,0:T(8,128)(2,1)} async-done(((bf16[112,4096]{1,0:T(8,128)(2,1)}), bf16[896,4096]{1,0:T(8,128)(2,1)}) %all-gather.5.cloned.1.call-update) | async-done | bytes 7340048 | tf_op jit(solution)/shard_map/all_gather | solution.py:175
  109.6 14.0 %hidden.1.refs_0_ = bf16[8,56,896]{2,1,0:T(8,128)(2,1)} custom-call(bf16[448,1024]{1,0:T(8,128)(2,1)} %copy-done.5, bf16[448,1024]{1,0:T(8,128)(2,1)} %copy-done.6, bf16[448,1024]{1,0:T(8,128)(2,1)} %copy-done.7, bf16[448,1024]{1,0:T(8,128)(2,1)} %copy-done.8, bf16[448,1024]{1,0:T(8,128)(2,1)} %copy-done.9, bf16[448,1024]{1,0:T(8,128)(2,1)} %copy-done.10, ...), custom_call_target="tpu_custom_call" | custom-call | flops 6576668672 | bytes 14680064 | tf_op jit(solution)/shard_map/hidden/pallas_call | solution.py:70
  126.6 3.7 %collective-permute-done.15 = f32[8,56]{1,0:T(8,128)S(1)} collective-permute-done((f32[8,56]{1,0:T(8,128)S(1)}, f32[8,56]{1,0:T(8,128)S(1)}, u32[]{:S(2)}, u32[]{:S(2)}) %collective-permute-start.15) | collective-permute-done | bytes 1824 | tf_op jit(solution)/shard_map/ppermute | solution.py:32
  131.7 3.2 %collective-permute-done.16 = f32[8,56]{1,0:T(8,128)S(1)} collective-permute-done((f32[8,56]{1,0:T(8,128)S(1)}, f32[8,56]{1,0:T(8,128)S(1)}, u32[]{:S(2)}, u32[]{:S(2)}) %collective-permute-start.16) | collective-permute-done | bytes 1824 | tf_op jit(solution)/shard_map/ppermute | solution.py:32
  134.9 3.0 %collective-permute-start.17 = (f32[8,56]{1,0:T(8,128)S(1)}, f32[8,56]{1,0:T(8,128)S(1)}, u32[]{:S(2)}, u32[]{:S(2)}) collective-permute-start(f32[8,56]{1,0:T(8,128)S(1)} %add.159), channel_id=1, source_target_pairs={{0,128},{32,160},{64,192},{96,224},{128,0},{160,32},{192,64},{224,... | collective-permute-start | bytes 5384 | tf_op jit(solution)/shard_map/ppermute | solution.py:32
  137.9 4.6 %collective-permute-done.17 = f32[8,56]{1,0:T(8,128)S(1)} collective-permute-done((f32[8,56]{1,0:T(8,128)S(1)}, f32[8,56]{1,0:T(8,128)S(1)}, u32[]{:S(2)}, u32[]{:S(2)}) %collective-permute-start.17) | collective-permute-done | bytes 1824 | tf_op jit(solution)/shard_map/ppermute | solution.py:32
  146.1 2.1 %collective-permute-done.22 = f32[8,56]{1,0:T(8,128)S(1)} collective-permute-done((f32[8,56]{1,0:T(8,128)}, f32[8,56]{1,0:T(8,128)S(1)}, u32[]{:S(2)}, u32[]{:S(2)}) %collective-permute-start.22) | collective-permute-done | bytes 1824 | tf_op jit(solution)/shard_map/ppermute | solution.py:204
  150.2 11.2 %all-gather.7.cloned.1.call-done = bf16[1856,1024]{1,0:T(8,128)(2,1)} async-done(((bf16[232,1024]{1,0:T(8,128)(2,1)}), bf16[1856,1024]{1,0:T(8,128)(2,1)}) %all-gather.7.cloned.1.call-update) | async-done | bytes 3801104 | tf_op jit(solution)/shard_map/all_gather | solution.py:191
  162.5 6.5 %outputs.1 = (bf16[120,1024]{1,0:T(8,128)(2,1)S(1)}, bf16[120,1024]{1,0:T(8,128)(2,1)S(1)}, bf16[120,1024]{1,0:T(8,128)(2,1)S(1)}, bf16[120,1024]{1,0:T(8,128)(2...) custom-call(bf16[8,56,896]{2,1,0:T(8,128)(2,1)S(1)} %copy-done, ...), custom_call_target="tpu_custom_call" | custom-call | flops 3288334336 | bytes 8716288 | tf_op jit(solution)/shard_map/outputs/pallas_call | solution.py:133
  169.0 3.7 %collective-permute-start.24 = (bf16[120,1024]{1,0:T(8,128)(2,1)S(1)}, bf16[120,1024]{1,0:T(8,128)(2,1)S(1)}, u32[]{:S(2)}, u32[]{:S(2)}) collective-permute-start(bf16[120,1024]{1,0:T(8,128)(2,1)S(1)} %get-tuple-element.11), channel_id=1, source_target_pairs={{0,17},{1,18},{2,19},{3,16},{16,1},{17,2},{18,3},{19,0},{4,21},{5,... | collective-permute-start | bytes 737288 | tf_op jit(solution)/shard_map/ppermute | solution.py:216
  174.7 5.4 %collective-permute-start.27 = (bf16[120,1024]{1,0:T(8,128)(2,1)S(1)}, bf16[120,1024]{1,0:T(8,128)(2,1)S(1)}, u32[]{:S(2)}, u32[]{:S(2)}) collective-permute-start(bf16[120,1024]{1,0:T(8,128)(2,1)S(1)} %get-tuple-element.14), channel_id=1, source_target_pairs={{0,18},{1,19},{2,16},{3,17},{16,2},{17,3},{18,0},{19,1},{4,22},{5,... | collective-permute-start | bytes 737288 | tf_op jit(solution)/shard_map/ppermute | solution.py:216
  181.8 4.7 %collective-permute-done.25 = bf16[120,1024]{1,0:T(8,128)(2,1)S(1)} collective-permute-done((bf16[120,1024]{1,0:T(8,128)(2,1)S(1)}, bf16[120,1024]{1,0:T(8,128)(2,1)S(1)}, u32[]{:S(2)}, u32[]{:S(2)}) %collective-permute-start.25) | collective-permute-done | bytes 245792 | tf_op jit(solution)/shard_map/ppermute | solution.py:216
  186.6 2.6 %collective-permute-done.26 = bf16[120,1024]{1,0:T(8,128)(2,1)S(1)} collective-permute-done((bf16[120,1024]{1,0:T(8,128)(2,1)S(1)}, bf16[120,1024]{1,0:T(8,128)(2,1)S(1)}, u32[]{:S(2)}, u32[]{:S(2)}) %collective-permute-start.26) | collective-permute-done | bytes 245792 | tf_op jit(solution)/shard_map/ppermute | solution.py:216
  189.3 2.9 %collective-permute-done.27 = bf16[120,1024]{1,0:T(8,128)(2,1)S(1)} collective-permute-done((bf16[120,1024]{1,0:T(8,128)(2,1)S(1)}, bf16[120,1024]{1,0:T(8,128)(2,1)S(1)}, u32[]{:S(2)}, u32[]{:S(2)}) %collective-permute-start.27) | collective-permute-done | bytes 245792 | tf_op jit(solution)/shard_map/ppermute | solution.py:216
  192.2 4.6 %collective-permute-done.28 = bf16[120,1024]{1,0:T(8,128)(2,1)S(1)} collective-permute-done((bf16[120,1024]{1,0:T(8,128)(2,1)S(1)}, bf16[120,1024]{1,0:T(8,128)(2,1)S(1)}, u32[]{:S(2)}, u32[]{:S(2)}) %collective-permute-start.28) | collective-permute-done | bytes 245792 | tf_op jit(solution)/shard_map/ppermute | solution.py:216
  (107 shorter events, 36.6 us)
Async XLA Ops:
  7.2 102.5 %all-gather.5.cloned.1.call-start = ((), (), s32[]{:S(2)}) async-start(), calls=%async_computation | async-start | bytes 8257536 | tf_op jit(solution)/shard_map/all_gather | solution.py:175
  8.7 8.5 %collective-permute-start.11 = (bf16[112,1024]{1,0:T(8,128)(2,1)S(1)}, bf16[112,1024]{1,0:T(8,128)(2,1)S(1)}, u32[]{:S(2)}, u32[]{:S(2)}) collective-permute-start(bf16[112,1024]{1,0:T(8,128)(2,1)S(1)} %bitcast.28), channel_id=1, source_target_pairs={{0,8},{4,12},{8,0},{12,4},{1,9},{5,13},{9,1},{13,5},{2,10},{6,14},... | collective-permute-start | bytes 688136 | tf_op jit(solution)/shard_map/ppermute | solution.py:174
  10.4 10.8 %collective-permute-start.12 = (bf16[112,1024]{1,0:T(8,128)(2,1)S(1)}, bf16[112,1024]{1,0:T(8,128)(2,1)S(1)}, u32[]{:S(2)}, u32[]{:S(2)}) collective-permute-start(bf16[112,1024]{1,0:T(8,128)(2,1)S(1)} %bitcast.27), channel_id=1, source_target_pairs={{0,12},{4,8},{8,4},{12,0},{1,13},{5,9},{9,5},{13,1},{2,14},{6,10},... | collective-permute-start | bytes 688136 | tf_op jit(solution)/shard_map/ppermute | solution.py:174
  22.2 139.1 %all-gather.7.cloned.1.call-start = ((), (), s32[]{:S(2)}) async-start(), calls=%async_computation.1 | async-start | bytes 4276224 | tf_op jit(solution)/shard_map/all_gather | solution.py:191
  28.3 8.6 %collective-permute-start = (bf16[112,1024]{1,0:T(8,128)(2,1)S(1)}, bf16[112,1024]{1,0:T(8,128)(2,1)S(1)}, u32[]{:S(2)}, u32[]{:S(2)}) collective-permute-start(bf16[112,1024]{1,0:T(8,128)(2,1)S(1)} %copy-done.4), channel_id=1, source_target_pairs={{0,3},{1,0},{2,1},{3,2},{4,7},{5,4},{6,5},{7,6},{8,11},{9,8},{10,9... | collective-permute-start | bytes 688136 | tf_op jit(solution)/shard_map/ppermute | solution.py:194
  28.9 10.1 %collective-permute-start.1 = (bf16[112,1024]{1,0:T(8,128)(2,1)S(1)}, bf16[112,1024]{1,0:T(8,128)(2,1)S(1)}, u32[]{:S(2)}, u32[]{:S(2)}) collective-permute-start(bf16[112,1024]{1,0:T(8,128)(2,1)S(1)} %copy-done.4), channel_id=1, source_target_pairs={{0,2},{1,3},{2,0},{3,1},{4,6},{5,7},{6,4},{7,5},{8,10},{9,11},{10,... | collective-permute-start | bytes 688136 | tf_op jit(solution)/shard_map/ppermute | solution.py:194
  31.7 10.1 %collective-permute-start.2 = (bf16[112,1024]{1,0:T(8,128)(2,1)S(1)}, bf16[112,1024]{1,0:T(8,128)(2,1)S(1)}, u32[]{:S(2)}, u32[]{:S(2)}) collective-permute-start(bf16[112,1024]{1,0:T(8,128)(2,1)S(1)} %copy-done.4), channel_id=1, source_target_pairs={{0,1},{1,2},{2,3},{3,0},{4,5},{5,6},{6,7},{7,4},{8,9},{9,10},{10,1... | collective-permute-start | bytes 688136 | tf_op jit(solution)/shard_map/ppermute | solution.py:194
  41.8 23.3 %collective-permute-start.3 = (bf16[448,1024]{1,0:T(8,128)(2,1)S(1)}, bf16[448,1024]{1,0:T(8,128)(2,1)S(1)}, u32[]{:S(2)}, u32[]{:S(2)}) collective-permute-start(bf16[448,1024]{1,0:T(8,128)(2,1)S(1)} %constant_dynamic-update-slice_fusion.refs_0_), channel_id=1, source_target_pairs={{0,8},{8,0},{16,24},{24,16},{1,9},{9,1},{17,25},{25,17},{2,10},{10... | collective-permute-start | bytes 2752520 | tf_op jit(solution)/shard_map/ppermute | solution.py:164
  43.4 42.8 %collective-permute-start.4 = (bf16[448,1024]{1,0:T(8,128)(2,1)S(1)}, bf16[448,1024]{1,0:T(8,128)(2,1)S(1)}, u32[]{:S(2)}, u32[]{:S(2)}) collective-permute-start(bf16[448,1024]{1,0:T(8,128)(2,1)S(1)} %constant_dynamic-update-slice_fusion.refs_0_), channel_id=1, source_target_pairs={{0,16},{8,24},{16,0},{24,8},{1,17},{9,25},{17,1},{25,9},{2,18},{10... | collective-permute-start | bytes 2752520 | tf_op jit(solution)/shard_map/ppermute | solution.py:164
  46.3 42.5 %collective-permute-start.5 = (bf16[448,1024]{1,0:T(8,128)(2,1)S(1)}, bf16[448,1024]{1,0:T(8,128)(2,1)S(1)}, u32[]{:S(2)}, u32[]{:S(2)}) collective-permute-start(bf16[448,1024]{1,0:T(8,128)(2,1)S(1)} %constant_dynamic-update-slice_fusion.refs_0_), channel_id=1, source_target_pairs={{0,24},{8,16},{16,8},{24,0},{1,25},{9,17},{17,9},{25,1},{2,26},{10... | collective-permute-start | bytes 2752520 | tf_op jit(solution)/shard_map/ppermute | solution.py:164
  46.6 42.3 %collective-permute-start.6 = (bf16[448,1024]{1,0:T(8,128)(2,1)S(1)}, bf16[448,1024]{1,0:T(8,128)(2,1)S(1)}, u32[]{:S(2)}, u32[]{:S(2)}) collective-permute-start(bf16[448,1024]{1,0:T(8,128)(2,1)S(1)} %constant_dynamic-update-slice_fusion.refs_0_), channel_id=1, source_target_pairs={{0,4},{4,0},{1,5},{5,1},{2,6},{6,2},{3,7},{7,3},{8,12},{12,8},{9,1... | collective-permute-start | bytes 2752520 | tf_op jit(solution)/shard_map/ppermute | solution.py:167
  65.1 23.8 %collective-permute-start.7 = (bf16[448,1024]{1,0:T(8,128)(2,1)S(1)}, bf16[448,1024]{1,0:T(8,128)(2,1)S(1)}, u32[]{:S(2)}, u32[]{:S(2)}) collective-permute-start(bf16[448,1024]{1,0:T(8,128)(2,1)S(1)} %collective-permute-done.3.refs_1_), channel_id=1, source_target_pairs={{0,4},{4,0},{1,5},{5,1},{2,6},{6,2},{3,7},{7,3},{8,12},{12,8},{9,1... | collective-permute-start | bytes 2752520 | tf_op jit(solution)/shard_map/ppermute | solution.py:167
  123.7 19.8 %collective-permute-start.14 = (bf16[8,56,896]{2,1,0:T(8,128)(2,1)}, bf16[8,56,896]{2,1,0:T(8,128)(2,1)S(1)}, u32[]{:S(2)}, u32[]{:S(2)}) collective-permute-start(bf16[8,56,896]{2,1,0:T(8,128)(2,1)} %hidden.1.refs_0_), channel_id=1, source_target_pairs={{0,8},{8,0},{1,9},{9,1},{2,10},{10,2},{3,11},{11,3},{4,12},{12,4},... | collective-permute-start | bytes 2408456 | tf_op jit(solution)/shard_map/ppermute | solution.py:201
  130.3 4.6 %collective-permute-start.16 = (f32[8,56]{1,0:T(8,128)S(1)}, f32[8,56]{1,0:T(8,128)S(1)}, u32[]{:S(2)}, u32[]{:S(2)}) collective-permute-start(f32[8,56]{1,0:T(8,128)S(1)} %add.158), channel_id=1, source_target_pairs={{0,64},{32,96},{64,0},{96,32},{128,192},{160,224},{192,128},{224,1... | collective-permute-start | bytes 5384 | tf_op jit(solution)/shard_map/ppermute | solution.py:32
  134.9 7.6 %collective-permute-start.17 = (f32[8,56]{1,0:T(8,128)S(1)}, f32[8,56]{1,0:T(8,128)S(1)}, u32[]{:S(2)}, u32[]{:S(2)}) collective-permute-start(f32[8,56]{1,0:T(8,128)S(1)} %add.159), channel_id=1, source_target_pairs={{0,128},{32,160},{64,192},{96,224},{128,0},{160,32},{192,64},{224,... | collective-permute-start | bytes 5384 | tf_op jit(solution)/shard_map/ppermute | solution.py:32
  137.9 23.4 %collective-permute-start.13 = (bf16[8,56,896]{2,1,0:T(8,128)(2,1)}, bf16[8,56,896]{2,1,0:T(8,128)(2,1)S(1)}, u32[]{:S(2)}, u32[]{:S(2)}) collective-permute-start(bf16[8,56,896]{2,1,0:T(8,128)(2,1)} %hidden.1.refs_0_), channel_id=1, source_target_pairs={{0,4},{4,0},{1,5},{5,1},{2,6},{6,2},{3,7},{7,3},{8,12},{12,8},{9,1... | collective-permute-start | bytes 2408456 | tf_op jit(solution)/shard_map/ppermute | solution.py:167
  144.4 16.9 %collective-permute-start.18 = (bf16[8,56,896]{2,1,0:T(8,128)(2,1)}, bf16[8,56,896]{2,1,0:T(8,128)(2,1)S(1)}, u32[]{:S(2)}, u32[]{:S(2)}) collective-permute-start(bf16[8,56,896]{2,1,0:T(8,128)(2,1)} %gate.1.refs_2_), channel_id=1, source_target_pairs={{0,4},{4,0},{1,5},{5,1},{2,6},{6,2},{3,7},{7,3},{8,12},{12,8},{9,1... | collective-permute-start | bytes 2408456 | tf_op jit(solution)/shard_map/ppermute | solution.py:167
  169.0 11.6 %collective-permute-start.24 = (bf16[120,1024]{1,0:T(8,128)(2,1)S(1)}, bf16[120,1024]{1,0:T(8,128)(2,1)S(1)}, u32[]{:S(2)}, u32[]{:S(2)}) collective-permute-start(bf16[120,1024]{1,0:T(8,128)(2,1)S(1)} %get-tuple-element.11), channel_id=1, source_target_pairs={{0,17},{1,18},{2,19},{3,16},{16,1},{17,2},{18,3},{19,0},{4,21},{5,... | collective-permute-start | bytes 737288 | tf_op jit(solution)/shard_map/ppermute | solution.py:216
  172.7 13.7 %collective-permute-start.25 = (bf16[120,1024]{1,0:T(8,128)(2,1)S(1)}, bf16[120,1024]{1,0:T(8,128)(2,1)S(1)}, u32[]{:S(2)}, u32[]{:S(2)}) collective-permute-start(bf16[120,1024]{1,0:T(8,128)(2,1)S(1)} %get-tuple-element.12), channel_id=1, source_target_pairs={{0,2},{1,3},{2,0},{3,1},{16,18},{17,19},{18,16},{19,17},{4,6},{5,7... | collective-permute-start | bytes 737288 | tf_op jit(solution)/shard_map/ppermute | solution.py:216
  173.6 15.7 %collective-permute-start.26 = (bf16[120,1024]{1,0:T(8,128)(2,1)S(1)}, bf16[120,1024]{1,0:T(8,128)(2,1)S(1)}, u32[]{:S(2)}, u32[]{:S(2)}) collective-permute-start(bf16[120,1024]{1,0:T(8,128)(2,1)S(1)} %get-tuple-element.13), channel_id=1, source_target_pairs={{0,19},{1,16},{2,17},{3,18},{16,3},{17,0},{18,1},{19,2},{4,23},{5,... | collective-permute-start | bytes 737288 | tf_op jit(solution)/shard_map/ppermute | solution.py:216
  174.7 17.5 %collective-permute-start.27 = (bf16[120,1024]{1,0:T(8,128)(2,1)S(1)}, bf16[120,1024]{1,0:T(8,128)(2,1)S(1)}, u32[]{:S(2)}, u32[]{:S(2)}) collective-permute-start(bf16[120,1024]{1,0:T(8,128)(2,1)S(1)} %get-tuple-element.14), channel_id=1, source_target_pairs={{0,18},{1,19},{2,16},{3,17},{16,2},{17,3},{18,0},{19,1},{4,22},{5,... | collective-permute-start | bytes 737288 | tf_op jit(solution)/shard_map/ppermute | solution.py:216
  180.1 16.7 %collective-permute-start.28 = (bf16[120,1024]{1,0:T(8,128)(2,1)S(1)}, bf16[120,1024]{1,0:T(8,128)(2,1)S(1)}, u32[]{:S(2)}, u32[]{:S(2)}) collective-permute-start(bf16[120,1024]{1,0:T(8,128)(2,1)S(1)} %get-tuple-element.15), channel_id=1, source_target_pairs={{0,16},{1,17},{2,18},{3,19},{16,0},{17,1},{18,2},{19,3},{4,20},{5,... | collective-permute-start | bytes 737288 | tf_op jit(solution)/shard_map/ppermute | solution.py:216
  180.6 16.2 %collective-permute-start.29 = (bf16[120,1024]{1,0:T(8,128)(2,1)S(1)}, bf16[120,1024]{1,0:T(8,128)(2,1)S(1)}, u32[]{:S(2)}, u32[]{:S(2)}) collective-permute-start(bf16[120,1024]{1,0:T(8,128)(2,1)S(1)} %get-tuple-element.16), channel_id=1, source_target_pairs={{0,1},{1,2},{2,3},{3,0},{16,17},{17,18},{18,19},{19,16},{4,5},{5,6... | collective-permute-start | bytes 737288 | tf_op jit(solution)/shard_map/ppermute | solution.py:216
  186.5 10.5 %collective-permute-start.30 = (bf16[120,1024]{1,0:T(8,128)(2,1)S(1)}, bf16[120,1024]{1,0:T(8,128)(2,1)S(1)}, u32[]{:S(2)}, u32[]{:S(2)}) collective-permute-start(bf16[120,1024]{1,0:T(8,128)(2,1)S(1)} %get-tuple-element.17), channel_id=1, source_target_pairs={{0,3},{1,0},{2,1},{3,2},{16,19},{17,16},{18,17},{19,18},{4,7},{5,4... | collective-permute-start | bytes 737288 | tf_op jit(solution)/shard_map/ppermute | solution.py:216
  (21 other events, 222.9 us)
Sparse Core Ops, SparseCore 0:
  22.3 87.2 all-gather.4
  111.4 49.8 all-gather.6

commit v7 on v6

--- a/solution.py
+++ b/solution.py
@@ -199,11 +199,13 @@
     hidden = hidden_units(mine, other, weights)
     unit_sums = sum_over(jnp.sum(hidden.astype(F32), axis=2), "z", nz)
     far = lax.ppermute(hidden, "yl", flip(2, 1))
-    (far,) = gate([far], [unit_sums])
-    hidden = [hidden, swap(hidden), far, swap(far)]
+    (passed,) = gate([far], [unit_sums])
+    hidden = [hidden, swap(hidden), far, swap(passed)]
     far = lax.ppermute(unit_sums, "yl", flip(2, 1))
     unit_sums = [unit_sums, swap(unit_sums), far, swap(far)]
-    unit_sums = jnp.concatenate(unit_sums, axis=1)[:, None, :]
+    corners = [h[0, :8, :128] for h in (hidden[1], hidden[3])]
+    (unit_sums,) = gate([jnp.concatenate(unit_sums, axis=1)], corners)
+    unit_sums = unit_sums[:, None, :]
 
     targets = [(dy, dx) for dy in range(nyh) for dx in range(nx)]
     leave = [targets.index(t) for t in ((1, 1), (0, 2), (1, 3), (1, 2), (1, 0), (0, 1), (0, 3), (0, 0))]

time: 208 us -> 206 us (level)
    unnamed x27 -> x26, local copies, waits for them, and re-layouts: 4.51 us -> 3.36 us
  transfers between devices with their start and end apart: 33 -> 33, of which waited for: 23 -> 23; matrix products, arithmetic and copies ran while one was open for 2% -> 3% of each run, Pallas kernels for 7% -> 7%
where the time goes in v7:
time: 206 us; the launch traced here: 205 us
  waiting for transfers between devices  122 us (59%)
  starting transfers between devices  34.3 us (17%)
  Pallas kernels  20.5 us (10%)
  between operations  14.3 us (7%)
  other arithmetic  7.2 us (3%)
  local copies, waits for them, and re-layouts  6.83 us (3%)
    ppermute x3, waiting for transfers between devices, across(): return lax.ppermute(array, ('yh', 'yl'), flip(nyh * nyl, mask))  42.2 us
    all_gather x1, waiting for transfers between devices, per_device(): lax.all_gather(jnp.concatenate(weights, axis=1), 'z', axis=0, tiled=False)  18.2 us
    ppermute x7, waiting for transfers between devices, per_device(): piece = lax.ppermute(piece, ('yh', 'x'), perm)  14.8 us
    ppermute x5, waiting for transfers between devices, sum_over(): value = value + lax.ppermute(value, axis, flip(n, mask))  14.1 us
    pallas_call x1, Pallas kernels, hidden_units(): pl.pallas_call(hidden_kernel, out_shape=jax.ShapeDtypeStruct((count, unit...  14 us
    ppermute x7, starting transfers between devices, per_device(): piece = lax.ppermute(piece, ('yh', 'x'), perm)  12.8 us
    ppermute x3, waiting for transfers between devices, per_device(): weights.append(piece if k == 0 else lax.ppermute(piece, ROW, flip(nrow, k)))  10.6 us
    all_gather x1, waiting for transfers between devices, per_device(): down = lax.all_gather(down, 'z', axis=0, tiled=False)  9.6 us
  transfers between devices with their start and end apart: 33, of which 23 were waited for; matrix products, arithmetic and copies ran while one was open for 3% of the time, Pallas kernels for 7%

profile of v7, /device:TPU:4, one launch (start us, length us, event | category | flops | bytes accessed | tf_op | source)
XLA Modules:
  0.0 204.9 jit_solution(3985272528763490974)
XLA Ops:
  10.6 6.6 %collective-permute-done.11 = bf16[112,1024]{1,0:T(8,128)(2,1)S(1)} collective-permute-done((bf16[112,1024]{1,0:T(8,128)(2,1)S(1)}, bf16[112,1024]{1,0:T(8,128)(2,1)S(1)}, u32[]{:S(2)}, u32[]{:S(2)}) %collective-permute-start.11) | collective-permute-done | bytes 229408 | tf_op jit(solution)/shard_map/ppermute | solution.py:174
  17.2 4.0 %collective-permute-done.12 = bf16[112,1024]{1,0:T(8,128)(2,1)S(1)} collective-permute-done((bf16[112,1024]{1,0:T(8,128)(2,1)S(1)}, bf16[112,1024]{1,0:T(8,128)(2,1)S(1)}, u32[]{:S(2)}, u32[]{:S(2)}) %collective-permute-start.12) | collective-permute-done | bytes 229408 | tf_op jit(solution)/shard_map/ppermute | solution.py:174
  28.9 2.7 %collective-permute-start.1 = (bf16[112,1024]{1,0:T(8,128)(2,1)S(1)}, bf16[112,1024]{1,0:T(8,128)(2,1)S(1)}, u32[]{:S(2)}, u32[]{:S(2)}) collective-permute-start(bf16[112,1024]{1,0:T(8,128)(2,1)S(1)} %copy-done.2), channel_id=1, source_target_pairs={{0,2},{1,3},{2,0},{3,1},{4,6},{5,7},{6,4},{7,5},{8,10},{9,11},{10,... | collective-permute-start | bytes 688136 | tf_op jit(solution)/shard_map/ppermute | solution.py:194
  33.3 3.7 %collective-permute-done = bf16[112,1024]{1,0:T(8,128)(2,1)S(1)} collective-permute-done((bf16[112,1024]{1,0:T(8,128)(2,1)S(1)}, bf16[112,1024]{1,0:T(8,128)(2,1)S(1)}, u32[]{:S(2)}, u32[]{:S(2)}) %collective-permute-start) | collective-permute-done | bytes 229408 | tf_op jit(solution)/shard_map/ppermute | solution.py:194
  37.0 2.1 %collective-permute-done.1 = bf16[112,1024]{1,0:T(8,128)(2,1)S(1)} collective-permute-done((bf16[112,1024]{1,0:T(8,128)(2,1)S(1)}, bf16[112,1024]{1,0:T(8,128)(2,1)S(1)}, u32[]{:S(2)}, u32[]{:S(2)}) %collective-permute-start.1) | collective-permute-done | bytes 229408 | tf_op jit(solution)/shard_map/ppermute | solution.py:194
  39.0 2.7 %collective-permute-done.2 = bf16[112,1024]{1,0:T(8,128)(2,1)S(1)} collective-permute-done((bf16[112,1024]{1,0:T(8,128)(2,1)S(1)}, bf16[112,1024]{1,0:T(8,128)(2,1)S(1)}, u32[]{:S(2)}, u32[]{:S(2)}) %collective-permute-start.2) | collective-permute-done | bytes 229408 | tf_op jit(solution)/shard_map/ppermute | solution.py:194
  43.4 2.9 %collective-permute-start.4 = (bf16[448,1024]{1,0:T(8,128)(2,1)S(1)}, bf16[448,1024]{1,0:T(8,128)(2,1)S(1)}, u32[]{:S(2)}, u32[]{:S(2)}) collective-permute-start(bf16[448,1024]{1,0:T(8,128)(2,1)S(1)} %constant_dynamic-update-slice_fusion.refs_0_), channel_id=1, source_target_pairs={{0,16},{8,24},{16,0},{24,8},{1,17},{9,25},{17,1},{25,9},{2,18},{10... | collective-permute-start | bytes 2752520 | tf_op jit(solution)/shard_map/ppermute | solution.py:164
  46.6 18.5 %collective-permute-done.3.refs_1_ = bf16[448,1024]{1,0:T(8,128)(2,1)S(1)} collective-permute-done((bf16[448,1024]{1,0:T(8,128)(2,1)S(1)}, bf16[448,1024]{1,0:T(8,128)(2,1)S(1)}, u32[]{:S(2)}, u32[]{:S(2)}) %collective-permute-start.3) | collective-permute-done | bytes 917536 | tf_op jit(solution)/shard_map/ppermute | solution.py:164
  65.1 21.2 %collective-permute-done.4.refs_2_ = bf16[448,1024]{1,0:T(8,128)(2,1)S(1)} collective-permute-done((bf16[448,1024]{1,0:T(8,128)(2,1)S(1)}, bf16[448,1024]{1,0:T(8,128)(2,1)S(1)}, u32[]{:S(2)}, u32[]{:S(2)}) %collective-permute-start.4) | collective-permute-done | bytes 917536 | tf_op jit(solution)/shard_map/ppermute | solution.py:164
  86.2 2.6 %collective-permute-done.5.refs_3_ = bf16[448,1024]{1,0:T(8,128)(2,1)S(1)} collective-permute-done((bf16[448,1024]{1,0:T(8,128)(2,1)S(1)}, bf16[448,1024]{1,0:T(8,128)(2,1)S(1)}, u32[]{:S(2)}, u32[]{:S(2)}) %collective-permute-start.5) | collective-permute-done | bytes 917536 | tf_op jit(solution)/shard_map/ppermute | solution.py:164
  91.4 18.2 %all-gather.5.cloned.1.call-done.refs_8_ = bf16[896,4096]{1,0:T(8,128)(2,1)} async-done(((bf16[112,4096]{1,0:T(8,128)(2,1)}), bf16[896,4096]{1,0:T(8,128)(2,1)}) %all-gather.5.cloned.1.call-update) | async-done | bytes 7340048 | tf_op jit(solution)/shard_map/all_gather | solution.py:175
  109.6 14.0 %hidden.1.refs_0_ = bf16[8,56,896]{2,1,0:T(8,128)(2,1)} custom-call(bf16[448,1024]{1,0:T(8,128)(2,1)} %copy-done.3, bf16[448,1024]{1,0:T(8,128)(2,1)} %copy-done.5, bf16[448,1024]{1,0:T(8,128)(2,1)} %copy-done.6, bf16[448,1024]{1,0:T(8,128)(2,1)} %copy-done.7, bf16[448,1024]{1,0:T(8,128)(2,1)} %copy-done.8, bf16[448,1024]{1,0:T(8,128)(2,1)} %copy-done.9, ...), custom_call_target="tpu_custom_call" | custom-call | flops 6576668672 | bytes 14680064 | tf_op jit(solution)/shard_map/hidden/pallas_call | solution.py:70
  126.6 3.6 %collective-permute-done.15 = f32[8,56]{1,0:T(8,128)S(1)} collective-permute-done((f32[8,56]{1,0:T(8,128)S(1)}, f32[8,56]{1,0:T(8,128)S(1)}, u32[]{:S(2)}, u32[]{:S(2)}) %collective-permute-start.15) | collective-permute-done | bytes 1824 | tf_op jit(solution)/shard_map/ppermute | solution.py:32
  131.7 3.2 %collective-permute-done.16 = f32[8,56]{1,0:T(8,128)S(1)} collective-permute-done((f32[8,56]{1,0:T(8,128)S(1)}, f32[8,56]{1,0:T(8,128)S(1)}, u32[]{:S(2)}, u32[]{:S(2)}) %collective-permute-start.16) | collective-permute-done | bytes 1824 | tf_op jit(solution)/shard_map/ppermute | solution.py:32
  134.9 3.0 %collective-permute-start.17 = (f32[8,56]{1,0:T(8,128)S(1)}, f32[8,56]{1,0:T(8,128)S(1)}, u32[]{:S(2)}, u32[]{:S(2)}) collective-permute-start(f32[8,56]{1,0:T(8,128)S(1)} %add.159), channel_id=1, source_target_pairs={{0,128},{32,160},{64,192},{96,224},{128,0},{160,32},{192,64},{224,... | collective-permute-start | bytes 5384 | tf_op jit(solution)/shard_map/ppermute | solution.py:32
  137.9 4.6 %collective-permute-done.17 = f32[8,56]{1,0:T(8,128)S(1)} collective-permute-done((f32[8,56]{1,0:T(8,128)S(1)}, f32[8,56]{1,0:T(8,128)S(1)}, u32[]{:S(2)}, u32[]{:S(2)}) %collective-permute-start.17) | collective-permute-done | bytes 1824 | tf_op jit(solution)/shard_map/ppermute | solution.py:32
  151.7 9.6 %all-gather.7.cloned.1.call-done = bf16[1856,1024]{1,0:T(8,128)(2,1)} async-done(((bf16[232,1024]{1,0:T(8,128)(2,1)}), bf16[1856,1024]{1,0:T(8,128)(2,1)}) %all-gather.7.cloned.1.call-update) | async-done | bytes 3801104 | tf_op jit(solution)/shard_map/all_gather | solution.py:191
  161.3 6.5 %outputs.1 = (bf16[120,1024]{1,0:T(8,128)(2,1)S(1)}, bf16[120,1024]{1,0:T(8,128)(2,1)S(1)}, bf16[120,1024]{1,0:T(8,128)(2,1)S(1)}, bf16[120,1024]{1,0:T(8,128)(2...) custom-call(bf16[8,56,896]{2,1,0:T(8,128)(2,1)S(1)} %copy-done, ...), custom_call_target="tpu_custom_call" | custom-call | flops 3288334336 | bytes 8716288 | tf_op jit(solution)/shard_map/outputs/pallas_call | solution.py:133
  167.9 3.7 %collective-permute-start.24 = (bf16[120,1024]{1,0:T(8,128)(2,1)S(1)}, bf16[120,1024]{1,0:T(8,128)(2,1)S(1)}, u32[]{:S(2)}, u32[]{:S(2)}) collective-permute-start(bf16[120,1024]{1,0:T(8,128)(2,1)S(1)} %get-tuple-element.11), channel_id=1, source_target_pairs={{0,17},{1,18},{2,19},{3,16},{16,1},{17,2},{18,3},{19,0},{4,21},{5,... | collective-permute-start | bytes 737288 | tf_op jit(solution)/shard_map/ppermute | solution.py:218
  173.5 5.4 %collective-permute-start.27 = (bf16[120,1024]{1,0:T(8,128)(2,1)S(1)}, bf16[120,1024]{1,0:T(8,128)(2,1)S(1)}, u32[]{:S(2)}, u32[]{:S(2)}) collective-permute-start(bf16[120,1024]{1,0:T(8,128)(2,1)S(1)} %get-tuple-element.14), channel_id=1, source_target_pairs={{0,18},{1,19},{2,16},{3,17},{16,2},{17,3},{18,0},{19,1},{4,22},{5,... | collective-permute-start | bytes 737288 | tf_op jit(solution)/shard_map/ppermute | solution.py:218
  180.7 4.7 %collective-permute-done.25 = bf16[120,1024]{1,0:T(8,128)(2,1)S(1)} collective-permute-done((bf16[120,1024]{1,0:T(8,128)(2,1)S(1)}, bf16[120,1024]{1,0:T(8,128)(2,1)S(1)}, u32[]{:S(2)}, u32[]{:S(2)}) %collective-permute-start.25) | collective-permute-done | bytes 245792 | tf_op jit(solution)/shard_map/ppermute | solution.py:218
  185.4 2.6 %collective-permute-done.26 = bf16[120,1024]{1,0:T(8,128)(2,1)S(1)} collective-permute-done((bf16[120,1024]{1,0:T(8,128)(2,1)S(1)}, bf16[120,1024]{1,0:T(8,128)(2,1)S(1)}, u32[]{:S(2)}, u32[]{:S(2)}) %collective-permute-start.26) | collective-permute-done | bytes 245792 | tf_op jit(solution)/shard_map/ppermute | solution.py:218
  188.1 2.9 %collective-permute-done.27 = bf16[120,1024]{1,0:T(8,128)(2,1)S(1)} collective-permute-done((bf16[120,1024]{1,0:T(8,128)(2,1)S(1)}, bf16[120,1024]{1,0:T(8,128)(2,1)S(1)}, u32[]{:S(2)}, u32[]{:S(2)}) %collective-permute-start.27) | collective-permute-done | bytes 245792 | tf_op jit(solution)/shard_map/ppermute | solution.py:218
  191.1 4.6 %collective-permute-done.28 = bf16[120,1024]{1,0:T(8,128)(2,1)S(1)} collective-permute-done((bf16[120,1024]{1,0:T(8,128)(2,1)S(1)}, bf16[120,1024]{1,0:T(8,128)(2,1)S(1)}, u32[]{:S(2)}, u32[]{:S(2)}) %collective-permute-start.28) | collective-permute-done | bytes 245792 | tf_op jit(solution)/shard_map/ppermute | solution.py:218
  (109 shorter events, 37.0 us)
Async XLA Ops:
  7.2 102.4 %all-gather.5.cloned.1.call-start = ((), (), s32[]{:S(2)}) async-start(), calls=%async_computation | async-start | bytes 8257536 | tf_op jit(solution)/shard_map/all_gather | solution.py:175
  8.7 8.5 %collective-permute-start.11 = (bf16[112,1024]{1,0:T(8,128)(2,1)S(1)}, bf16[112,1024]{1,0:T(8,128)(2,1)S(1)}, u32[]{:S(2)}, u32[]{:S(2)}) collective-permute-start(bf16[112,1024]{1,0:T(8,128)(2,1)S(1)} %bitcast.32), channel_id=1, source_target_pairs={{0,8},{4,12},{8,0},{12,4},{1,9},{5,13},{9,1},{13,5},{2,10},{6,14},... | collective-permute-start | bytes 688136 | tf_op jit(solution)/shard_map/ppermute | solution.py:174
  10.4 10.8 %collective-permute-start.12 = (bf16[112,1024]{1,0:T(8,128)(2,1)S(1)}, bf16[112,1024]{1,0:T(8,128)(2,1)S(1)}, u32[]{:S(2)}, u32[]{:S(2)}) collective-permute-start(bf16[112,1024]{1,0:T(8,128)(2,1)S(1)} %bitcast.31), channel_id=1, source_target_pairs={{0,12},{4,8},{8,4},{12,0},{1,13},{5,9},{9,5},{13,1},{2,14},{6,10},... | collective-permute-start | bytes 688136 | tf_op jit(solution)/shard_map/ppermute | solution.py:174
  22.2 139.1 %all-gather.7.cloned.1.call-start = ((), (), s32[]{:S(2)}) async-start(), calls=%async_computation.1 | async-start | bytes 4276224 | tf_op jit(solution)/shard_map/all_gather | solution.py:191
  28.3 8.6 %collective-permute-start = (bf16[112,1024]{1,0:T(8,128)(2,1)S(1)}, bf16[112,1024]{1,0:T(8,128)(2,1)S(1)}, u32[]{:S(2)}, u32[]{:S(2)}) collective-permute-start(bf16[112,1024]{1,0:T(8,128)(2,1)S(1)} %copy-done.2), channel_id=1, source_target_pairs={{0,3},{1,0},{2,1},{3,2},{4,7},{5,4},{6,5},{7,6},{8,11},{9,8},{10,9... | collective-permute-start | bytes 688136 | tf_op jit(solution)/shard_map/ppermute | solution.py:194
  28.9 10.1 %collective-permute-start.1 = (bf16[112,1024]{1,0:T(8,128)(2,1)S(1)}, bf16[112,1024]{1,0:T(8,128)(2,1)S(1)}, u32[]{:S(2)}, u32[]{:S(2)}) collective-permute-start(bf16[112,1024]{1,0:T(8,128)(2,1)S(1)} %copy-done.2), channel_id=1, source_target_pairs={{0,2},{1,3},{2,0},{3,1},{4,6},{5,7},{6,4},{7,5},{8,10},{9,11},{10,... | collective-permute-start | bytes 688136 | tf_op jit(solution)/shard_map/ppermute | solution.py:194
  31.7 10.1 %collective-permute-start.2 = (bf16[112,1024]{1,0:T(8,128)(2,1)S(1)}, bf16[112,1024]{1,0:T(8,128)(2,1)S(1)}, u32[]{:S(2)}, u32[]{:S(2)}) collective-permute-start(bf16[112,1024]{1,0:T(8,128)(2,1)S(1)} %copy-done.2), channel_id=1, source_target_pairs={{0,1},{1,2},{2,3},{3,0},{4,5},{5,6},{6,7},{7,4},{8,9},{9,10},{10,1... | collective-permute-start | bytes 688136 | tf_op jit(solution)/shard_map/ppermute | solution.py:194
  41.8 23.3 %collective-permute-start.3 = (bf16[448,1024]{1,0:T(8,128)(2,1)S(1)}, bf16[448,1024]{1,0:T(8,128)(2,1)S(1)}, u32[]{:S(2)}, u32[]{:S(2)}) collective-permute-start(bf16[448,1024]{1,0:T(8,128)(2,1)S(1)} %constant_dynamic-update-slice_fusion.refs_0_), channel_id=1, source_target_pairs={{0,8},{8,0},{16,24},{24,16},{1,9},{9,1},{17,25},{25,17},{2,10},{10... | collective-permute-start | bytes 2752520 | tf_op jit(solution)/shard_map/ppermute | solution.py:164
  43.4 42.8 %collective-permute-start.4 = (bf16[448,1024]{1,0:T(8,128)(2,1)S(1)}, bf16[448,1024]{1,0:T(8,128)(2,1)S(1)}, u32[]{:S(2)}, u32[]{:S(2)}) collective-permute-start(bf16[448,1024]{1,0:T(8,128)(2,1)S(1)} %constant_dynamic-update-slice_fusion.refs_0_), channel_id=1, source_target_pairs={{0,16},{8,24},{16,0},{24,8},{1,17},{9,25},{17,1},{25,9},{2,18},{10... | collective-permute-start | bytes 2752520 | tf_op jit(solution)/shard_map/ppermute | solution.py:164
  46.3 42.5 %collective-permute-start.5 = (bf16[448,1024]{1,0:T(8,128)(2,1)S(1)}, bf16[448,1024]{1,0:T(8,128)(2,1)S(1)}, u32[]{:S(2)}, u32[]{:S(2)}) collective-permute-start(bf16[448,1024]{1,0:T(8,128)(2,1)S(1)} %constant_dynamic-update-slice_fusion.refs_0_), channel_id=1, source_target_pairs={{0,24},{8,16},{16,8},{24,0},{1,25},{9,17},{17,9},{25,1},{2,26},{10... | collective-permute-start | bytes 2752520 | tf_op jit(solution)/shard_map/ppermute | solution.py:164
  46.6 42.3 %collective-permute-start.6 = (bf16[448,1024]{1,0:T(8,128)(2,1)S(1)}, bf16[448,1024]{1,0:T(8,128)(2,1)S(1)}, u32[]{:S(2)}, u32[]{:S(2)}) collective-permute-start(bf16[448,1024]{1,0:T(8,128)(2,1)S(1)} %constant_dynamic-update-slice_fusion.refs_0_), channel_id=1, source_target_pairs={{0,4},{4,0},{1,5},{5,1},{2,6},{6,2},{3,7},{7,3},{8,12},{12,8},{9,1... | collective-permute-start | bytes 2752520 | tf_op jit(solution)/shard_map/ppermute | solution.py:167
  65.1 23.8 %collective-permute-start.7 = (bf16[448,1024]{1,0:T(8,128)(2,1)S(1)}, bf16[448,1024]{1,0:T(8,128)(2,1)S(1)}, u32[]{:S(2)}, u32[]{:S(2)}) collective-permute-start(bf16[448,1024]{1,0:T(8,128)(2,1)S(1)} %collective-permute-done.3.refs_1_), channel_id=1, source_target_pairs={{0,4},{4,0},{1,5},{5,1},{2,6},{6,2},{3,7},{7,3},{8,12},{12,8},{9,1... | collective-permute-start | bytes 2752520 | tf_op jit(solution)/shard_map/ppermute | solution.py:167
  123.6 19.8 %collective-permute-start.14 = (bf16[8,56,896]{2,1,0:T(8,128)(2,1)}, bf16[8,56,896]{2,1,0:T(8,128)(2,1)S(1)}, u32[]{:S(2)}, u32[]{:S(2)}) collective-permute-start(bf16[8,56,896]{2,1,0:T(8,128)(2,1)} %hidden.1.refs_0_), channel_id=1, source_target_pairs={{0,8},{8,0},{1,9},{9,1},{2,10},{10,2},{3,11},{11,3},{4,12},{12,4},... | collective-permute-start | bytes 2408456 | tf_op jit(solution)/shard_map/ppermute | solution.py:201
  125.1 24.7 %collective-permute-start.13 = (bf16[8,56,896]{2,1,0:T(8,128)(2,1)}, bf16[8,56,896]{2,1,0:T(8,128)(2,1)S(1)}, u32[]{:S(2)}, u32[]{:S(2)}) collective-permute-start(bf16[8,56,896]{2,1,0:T(8,128)(2,1)} %hidden.1.refs_0_), channel_id=1, source_target_pairs={{0,4},{4,0},{1,5},{5,1},{2,6},{6,2},{3,7},{7,3},{8,12},{12,8},{9,1... | collective-permute-start | bytes 2408456 | tf_op jit(solution)/shard_map/ppermute | solution.py:167
  130.2 4.6 %collective-permute-start.16 = (f32[8,56]{1,0:T(8,128)S(1)}, f32[8,56]{1,0:T(8,128)S(1)}, u32[]{:S(2)}, u32[]{:S(2)}) collective-permute-start(f32[8,56]{1,0:T(8,128)S(1)} %add.158), channel_id=1, source_target_pairs={{0,64},{32,96},{64,0},{96,32},{128,192},{160,224},{192,128},{224,1... | collective-permute-start | bytes 5384 | tf_op jit(solution)/shard_map/ppermute | solution.py:32
  134.9 7.6 %collective-permute-start.17 = (f32[8,56]{1,0:T(8,128)S(1)}, f32[8,56]{1,0:T(8,128)S(1)}, u32[]{:S(2)}, u32[]{:S(2)}) collective-permute-start(f32[8,56]{1,0:T(8,128)S(1)} %add.159), channel_id=1, source_target_pairs={{0,128},{32,160},{64,192},{96,224},{128,0},{160,32},{192,64},{224,... | collective-permute-start | bytes 5384 | tf_op jit(solution)/shard_map/ppermute | solution.py:32
  144.4 6.0 %collective-permute-start.18 = (bf16[8,56,896]{2,1,0:T(8,128)(2,1)}, bf16[8,56,896]{2,1,0:T(8,128)(2,1)S(1)}, u32[]{:S(2)}, u32[]{:S(2)}) collective-permute-start(bf16[8,56,896]{2,1,0:T(8,128)(2,1)} %gate.2), channel_id=1, source_target_pairs={{0,4},{4,0},{1,5},{5,1},{2,6},{6,2},{3,7},{7,3},{8,12},{12,8},{9,1... | collective-permute-start | bytes 2408456 | tf_op jit(solution)/shard_map/ppermute | solution.py:167
  167.9 11.6 %collective-permute-start.24 = (bf16[120,1024]{1,0:T(8,128)(2,1)S(1)}, bf16[120,1024]{1,0:T(8,128)(2,1)S(1)}, u32[]{:S(2)}, u32[]{:S(2)}) collective-permute-start(bf16[120,1024]{1,0:T(8,128)(2,1)S(1)} %get-tuple-element.11), channel_id=1, source_target_pairs={{0,17},{1,18},{2,19},{3,16},{16,1},{17,2},{18,3},{19,0},{4,21},{5,... | collective-permute-start | bytes 737288 | tf_op jit(solution)/shard_map/ppermute | solution.py:218
  171.6 13.7 %collective-permute-start.25 = (bf16[120,1024]{1,0:T(8,128)(2,1)S(1)}, bf16[120,1024]{1,0:T(8,128)(2,1)S(1)}, u32[]{:S(2)}, u32[]{:S(2)}) collective-permute-start(bf16[120,1024]{1,0:T(8,128)(2,1)S(1)} %get-tuple-element.12), channel_id=1, source_target_pairs={{0,2},{1,3},{2,0},{3,1},{16,18},{17,19},{18,16},{19,17},{4,6},{5,7... | collective-permute-start | bytes 737288 | tf_op jit(solution)/shard_map/ppermute | solution.py:218
  172.4 15.7 %collective-permute-start.26 = (bf16[120,1024]{1,0:T(8,128)(2,1)S(1)}, bf16[120,1024]{1,0:T(8,128)(2,1)S(1)}, u32[]{:S(2)}, u32[]{:S(2)}) collective-permute-start(bf16[120,1024]{1,0:T(8,128)(2,1)S(1)} %get-tuple-element.13), channel_id=1, source_target_pairs={{0,19},{1,16},{2,17},{3,18},{16,3},{17,0},{18,1},{19,2},{4,23},{5,... | collective-permute-start | bytes 737288 | tf_op jit(solution)/shard_map/ppermute | solution.py:218
  173.5 17.5 %collective-permute-start.27 = (bf16[120,1024]{1,0:T(8,128)(2,1)S(1)}, bf16[120,1024]{1,0:T(8,128)(2,1)S(1)}, u32[]{:S(2)}, u32[]{:S(2)}) collective-permute-start(bf16[120,1024]{1,0:T(8,128)(2,1)S(1)} %get-tuple-element.14), channel_id=1, source_target_pairs={{0,18},{1,19},{2,16},{3,17},{16,2},{17,3},{18,0},{19,1},{4,22},{5,... | collective-permute-start | bytes 737288 | tf_op jit(solution)/shard_map/ppermute | solution.py:218
  178.9 16.7 %collective-permute-start.28 = (bf16[120,1024]{1,0:T(8,128)(2,1)S(1)}, bf16[120,1024]{1,0:T(8,128)(2,1)S(1)}, u32[]{:S(2)}, u32[]{:S(2)}) collective-permute-start(bf16[120,1024]{1,0:T(8,128)(2,1)S(1)} %get-tuple-element.15), channel_id=1, source_target_pairs={{0,16},{1,17},{2,18},{3,19},{16,0},{17,1},{18,2},{19,3},{4,20},{5,... | collective-permute-start | bytes 737288 | tf_op jit(solution)/shard_map/ppermute | solution.py:218
  179.5 16.2 %collective-permute-start.29 = (bf16[120,1024]{1,0:T(8,128)(2,1)S(1)}, bf16[120,1024]{1,0:T(8,128)(2,1)S(1)}, u32[]{:S(2)}, u32[]{:S(2)}) collective-permute-start(bf16[120,1024]{1,0:T(8,128)(2,1)S(1)} %get-tuple-element.16), channel_id=1, source_target_pairs={{0,1},{1,2},{2,3},{3,0},{16,17},{17,18},{18,19},{19,16},{4,5},{5,6... | collective-permute-start | bytes 737288 | tf_op jit(solution)/shard_map/ppermute | solution.py:218
  185.3 10.5 %collective-permute-start.30 = (bf16[120,1024]{1,0:T(8,128)(2,1)S(1)}, bf16[120,1024]{1,0:T(8,128)(2,1)S(1)}, u32[]{:S(2)}, u32[]{:S(2)}) collective-permute-start(bf16[120,1024]{1,0:T(8,128)(2,1)S(1)} %get-tuple-element.17), channel_id=1, source_target_pairs={{0,3},{1,0},{2,1},{3,2},{16,19},{17,16},{18,17},{19,18},{4,7},{5,4... | collective-permute-start | bytes 737288 | tf_op jit(solution)/shard_map/ppermute | solution.py:218
  (20 other events, 218.9 us)
Sparse Core Ops, SparseCore 0:
  22.3 87.2 all-gather.4
  111.4 49.8 all-gather.6

commit v8 on v7

--- a/solution.py
+++ b/solution.py
@@ -48,7 +48,7 @@
 
 
 def hidden_kernel(*refs):
-    x_refs, weights_ref, out_ref = refs[:8], refs[8], refs[9]
+    x_refs, weights_ref, out_ref = refs[:8], refs[8], refs[-1]
     count, part = out_ref.shape[:2]
     depth = x_refs[0].shape[1]
     total = None
@@ -64,7 +64,7 @@
         out_ref[j] = (gate / (1.0 + jnp.exp(-gate)) * up).astype(BF16)
 
 
-def hidden_units(mine, other, weights):
+def hidden_units(mine, other, weights, waited):
     count, units, wide = weights.shape
     total = 2 * mine[0].shape[0]
     return pl.pallas_call(
@@ -77,12 +77,12 @@
             bytes_accessed=2 * (total + count * units) * wide,
         ),
         name="hidden",
-    )(*mine, *other, weights.reshape(count * units, wide))
+    )(*mine, *other, weights.reshape(count * units, wide), waited)
 
 
 def output_kernel(pieces, blocks, *refs):
-    hidden_refs, (down_ref, units_ref) = refs[:pieces], refs[pieces : pieces + 2]
-    out_refs, (total, col, row) = refs[pieces + 2 : -3], refs[-3:]
+    hidden_refs, (down_ref, units_ref, weights_ref) = refs[:pieces], refs[pieces : pieces + 3]
+    out_refs, (total, col, row) = refs[pieces + 3 : -3], refs[-3:]
     group, _, units = units_ref.shape
     width = down_ref.shape[2]
     rows = total.shape[0] // blocks
@@ -95,16 +95,16 @@
     hidden = jnp.concatenate([r[i] for i in range(group) for r in hidden_refs])
     down = jnp.concatenate([down_ref[i, pl.ds(0, units), :] for i in range(group)])
     total[...] += lax.dot_general(hidden, down, MAJOR, preferred_element_type=F32)
-    for i in range(group):
-        span = slice(i * units, (i + 1) * units)
-        sums = units_ref[i]
+    def terms(sums):
         high = sums.astype(BF16).astype(F32)
         middle = (sums - high).astype(BF16).astype(F32)
         rest = jnp.zeros((EXTRA - 3, units), F32)
-        terms = jnp.concatenate([high, middle, sums - high - middle, rest]).astype(BF16)
-        col[...] += jnp.dot(terms, down[span], preferred_element_type=F32)
-        weights = down_ref[i, pl.ds(units, EXTRA), pl.ds(0, units)]
-        row[...] += jnp.dot(weights, hidden[span], preferred_element_type=F32)
+        return jnp.concatenate([high, middle, sums - high - middle, rest]).astype(BF16)
+
+    for i in range(group):
+        span = slice(i * units, (i + 1) * units)
+        col[...] += jnp.dot(terms(units_ref[i]), down[span], preferred_element_type=F32)
+        row[...] += jnp.dot(terms(weights_ref[i]), hidden[span], preferred_element_type=F32)
 
     @pl.when(pl.program_id(0) == pl.num_programs(0) - 1)
     def _():
@@ -124,11 +124,11 @@
             out_refs[j][pl.ds(rows, EXTRA), :] = lines
 
 
-def outputs(hidden, down, unit_sums, blocks):
+def outputs(hidden, down, unit_sums, weight_sums, blocks):
     steps, _, total = hidden[0].shape
     units = sum(h.shape[1] for h in hidden)
     width = down.shape[2]
-    operands = [*hidden, down, unit_sums]
+    operands = [*hidden, down, unit_sums, weight_sums]
     piece = (total // blocks + EXTRA, width)
     return pl.pallas_call(
         functools.partial(output_kernel, len(hidden), blocks),
@@ -183,11 +183,9 @@
 
     sums = jnp.sum(down_weight.astype(F32), axis=1)
     sums = ordered(sum_over(sum_over(sums, "c", 2), "yl", 2)).reshape(1, units)
-    high = lax.reduce_precision(sums, 8, 7)
-    middle = lax.reduce_precision(sums - high, 8, 7)
-    lines = jnp.concatenate([high, middle, sums - high - middle]).astype(BF16)
-    lines = jnp.pad(lines, ((0, EXTRA - 3), (0, width - units)))
-    down = jnp.concatenate([ordered(down_weight), lines])
+    here = (jnp.arange(nz) == lax.axis_index("z"))[:, None]
+    weight_sums = sum_over(jnp.where(here, sums, 0.0), "z", nz)
+    down = ordered(down_weight)
     down = lax.all_gather(down, "z", axis=0, tiled=False)
 
     mine = jnp.concatenate(
@@ -196,7 +194,7 @@
     mine = [mine] + [across(mine, k) for k in range(1, nyh * nyl)]
     other = [swap(m) for m in mine]
 
-    hidden = hidden_units(mine, other, weights)
+    hidden = hidden_units(mine, other, weights, weight_sums)
     unit_sums = sum_over(jnp.sum(hidden.astype(F32), axis=2), "z", nz)
     far = lax.ppermute(hidden, "yl", flip(2, 1))
     (passed,) = gate([far], [unit_sums])
@@ -204,12 +202,12 @@
     far = lax.ppermute(unit_sums, "yl", flip(2, 1))
     unit_sums = [unit_sums, swap(unit_sums), far, swap(far)]
     corners = [h[0, :8, :128] for h in (hidden[1], hidden[3])]
-    (unit_sums,) = gate([jnp.concatenate(unit_sums, axis=1)], corners)
-    unit_sums = unit_sums[:, None, :]
+    unit_sums, weight_sums = gate([jnp.concatenate(unit_sums, axis=1), weight_sums], corners)
+    unit_sums, weight_sums = unit_sums[:, None, :], weight_sums[:, None, :]
 
     targets = [(dy, dx) for dy in range(nyh) for dx in range(nx)]
     leave = [targets.index(t) for t in ((1, 1), (0, 2), (1, 3), (1, 2), (1, 0), (0, 1), (0, 3), (0, 0))]
-    sent = outputs(hidden, down, unit_sums, len(targets))
+    sent = outputs(hidden, down, unit_sums, weight_sums, len(targets))
     received = {}
     for j in leave:
         (dy, dx), piece = targets[j], sent[j]

time: 206 us -> 206 us (level)
  waiting for transfers between devices: 122 us -> 110 us
  starting transfers between devices: 34.3 us -> 46 us
    ppermute x5 -> x8, waiting for transfers between devices: 14.1 us -> 53 us  [sum_over(): value = value + lax.ppermute(value, axis, flip(n, mask))]
    ppermute x3, waiting for transfers between devices: 42.2 us -> 4.55 us  [across(): return lax.ppermute(array, ('yh', 'yl'), flip(nyh * nyl, mask))]
    all_gather x1, waiting for transfers between devices: 18.2 us -> 6.38 us  [per_device(): lax.all_gather(jnp.concatenate(weights, axis=1), 'z', axis=0, tiled=False)]
    ppermute x5 -> x8, starting transfers between devices: 6.54 us -> 17.7 us  [sum_over(): value = value + lax.ppermute(value, axis, flip(n, mask))]
    unnamed x26 -> x18, local copies, waits for them, and re-layouts: 3.36 us -> 0.99 us
  transfers between devices with their start and end apart: 33 -> 36, of which waited for: 23 -> 24; matrix products, arithmetic and copies ran while one was open for 3% -> 4% of each run, Pallas kernels for 7% -> 7%
where the time goes in v8:
time: 206 us; the launch traced here: 204 us
  waiting for transfers between devices  110 us (53%)
  starting transfers between devices  46 us (22%)
  Pallas kernels  20.5 us (10%)
  between operations  14.3 us (7%)
  other arithmetic  7.95 us (4%)
  local copies, waits for them, and re-layouts  5.17 us (3%)
    ppermute x8, waiting for transfers between devices, sum_over(): value = value + lax.ppermute(value, axis, flip(n, mask))  53 us
    ppermute x8, starting transfers between devices, sum_over(): value = value + lax.ppermute(value, axis, flip(n, mask))  17.7 us
    ppermute x7, waiting for transfers between devices, per_device(): piece = lax.ppermute(piece, ('yh', 'x'), perm)  14.8 us
    pallas_call x1, Pallas kernels, hidden_units(): pl.pallas_call(hidden_kernel, out_shape=jax.ShapeDtypeStruct((count, unit...  14 us
    ppermute x7, starting transfers between devices, per_device(): piece = lax.ppermute(piece, ('yh', 'x'), perm)  12.8 us
    ppermute x3, waiting for transfers between devices, per_device(): weights.append(piece if k == 0 else lax.ppermute(piece, ROW, flip(nrow, k)))  10.6 us
    ppermute x3, waiting for transfers between devices, per_device(): lax.ppermute(tokens, 'x', shift(nx, -k))  9.55 us
    all_gather x1, waiting for transfers between devices, per_device(): down = lax.all_gather(down, 'z', axis=0, tiled=False)  8.02 us
  transfers between devices with their start and end apart: 36, of which 24 were waited for; matrix products, arithmetic and copies ran while one was open for 4% of the time, Pallas kernels for 7%

profile of v8, /device:TPU:4, one launch (start us, length us, event | category | flops | bytes accessed | tf_op | source)
XLA Modules:
  0.0 204.3 jit_solution(4244638533003563183)
XLA Ops:
  10.6 6.6 %collective-permute-done.11 = bf16[112,1024]{1,0:T(8,128)(2,1)S(1)} collective-permute-done((bf16[112,1024]{1,0:T(8,128)(2,1)S(1)}, bf16[112,1024]{1,0:T(8,128)(2,1)S(1)}, u32[]{:S(2)}, u32[]{:S(2)}) %collective-permute-start.11) | collective-permute-done | bytes 229408 | tf_op jit(solution)/shard_map/ppermute | solution.py:174
  17.2 4.0 %collective-permute-done.12 = bf16[112,1024]{1,0:T(8,128)(2,1)S(1)} collective-permute-done((bf16[112,1024]{1,0:T(8,128)(2,1)S(1)}, bf16[112,1024]{1,0:T(8,128)(2,1)S(1)}, u32[]{:S(2)}, u32[]{:S(2)}) %collective-permute-start.12) | collective-permute-done | bytes 229408 | tf_op jit(solution)/shard_map/ppermute | solution.py:174
  23.8 2.7 %collective-permute-start.1 = (bf16[112,1024]{1,0:T(8,128)(2,1)S(1)}, bf16[112,1024]{1,0:T(8,128)(2,1)S(1)}, u32[]{:S(2)}, u32[]{:S(2)}) collective-permute-start(bf16[112,1024]{1,0:T(8,128)(2,1)S(1)} %copy-done.2), channel_id=1, source_target_pairs={{0,2},{1,3},{2,0},{3,1},{4,6},{5,7},{6,4},{7,5},{8,10},{9,11},{10,... | collective-permute-start | bytes 688136 | tf_op jit(solution)/shard_map/ppermute | solution.py:192
  28.2 3.5 %collective-permute-done = bf16[112,1024]{1,0:T(8,128)(2,1)S(1)} collective-permute-done((bf16[112,1024]{1,0:T(8,128)(2,1)S(1)}, bf16[112,1024]{1,0:T(8,128)(2,1)S(1)}, u32[]{:S(2)}, u32[]{:S(2)}) %collective-permute-start) | collective-permute-done | bytes 229408 | tf_op jit(solution)/shard_map/ppermute | solution.py:192
  33.9 3.9 %collective-permute-done.2 = bf16[112,1024]{1,0:T(8,128)(2,1)S(1)} collective-permute-done((bf16[112,1024]{1,0:T(8,128)(2,1)S(1)}, bf16[112,1024]{1,0:T(8,128)(2,1)S(1)}, u32[]{:S(2)}, u32[]{:S(2)}) %collective-permute-start.2) | collective-permute-done | bytes 229408 | tf_op jit(solution)/shard_map/ppermute | solution.py:192
  39.5 2.9 %collective-permute-start.4 = (bf16[448,1024]{1,0:T(8,128)(2,1)S(1)}, bf16[448,1024]{1,0:T(8,128)(2,1)S(1)}, u32[]{:S(2)}, u32[]{:S(2)}) collective-permute-start(bf16[448,1024]{1,0:T(8,128)(2,1)S(1)} %constant_dynamic-update-slice_fusion.refs_0_), channel_id=1, source_target_pairs={{0,16},{8,24},{16,0},{24,8},{1,17},{9,25},{17,1},{25,9},{2,18},{10... | collective-permute-start | bytes 2752520 | tf_op jit(solution)/shard_map/ppermute | solution.py:164
  44.3 35.6 %collective-permute-done.14 = f32[224]{0:T(256)S(1)} collective-permute-done((f32[224]{0:T(256)S(1)}, f32[224]{0:T(256)S(1)}, u32[]{:S(2)}, u32[]{:S(2)}) %collective-permute-start.14) | collective-permute-done | bytes 928 | tf_op jit(solution)/shard_map/ppermute | solution.py:32
  82.4 2.7 %collective-permute-done.5.refs_3_ = bf16[448,1024]{1,0:T(8,128)(2,1)} collective-permute-done((bf16[448,1024]{1,0:T(8,128)(2,1)S(1)}, bf16[448,1024]{1,0:T(8,128)(2,1)}, u32[]{:S(2)}, u32[]{:S(2)}) %collective-permute-start.5) | collective-permute-done | bytes 917536 | tf_op jit(solution)/shard_map/ppermute | solution.py:164
  89.1 3.4 %collective-permute-start.16 = (f32[8,224]{1,0:T(8,128)S(1)}, f32[8,224]{1,0:T(8,128)S(1)}, u32[]{:S(2)}, u32[]{:S(2)}) collective-permute-start(f32[8,224]{1,0:T(8,128)S(1)} %fusion.2), channel_id=1, source_target_pairs={{0,64},{32,96},{64,0},{96,32},{128,192},{160,224},{192,128},{224,1... | collective-permute-start | bytes 21512 | tf_op jit(solution)/shard_map/ppermute | solution.py:32
  94.4 6.8 %collective-permute-start.17 = (f32[8,224]{1,0:T(8,128)S(1)}, f32[8,224]{1,0:T(8,128)S(1)}, u32[]{:S(2)}, u32[]{:S(2)}) collective-permute-start(f32[8,224]{1,0:T(8,128)S(1)} %fusion.10), channel_id=1, source_target_pairs={{0,128},{32,160},{64,192},{96,224},{128,0},{160,32},{192,64},{224,... | collective-permute-start | bytes 21512 | tf_op jit(solution)/shard_map/ppermute | solution.py:32
  103.6 6.4 %all-gather.6.cloned.1.call-done.refs_8_ = bf16[896,4096]{1,0:T(8,128)(2,1)} async-done(((bf16[112,4096]{1,0:T(8,128)(2,1)}), bf16[896,4096]{1,0:T(8,128)(2,1)}) %all-gather.6.cloned.1.call-update) | async-done | bytes 7340048 | tf_op jit(solution)/shard_map/all_gather | solution.py:175
  110.0 14.0 %hidden.1.refs_0_ = bf16[8,56,896]{2,1,0:T(8,128)(2,1)} custom-call(bf16[448,1024]{1,0:T(8,128)(2,1)} %copy-done.3, bf16[448,1024]{1,0:T(8,128)(2,1)} %copy-done.5, bf16[448,1024]{1,0:T(8,128)(2,1)} %copy-done.6, bf16[448,1024]{1,0:T(8,128)(2,1)} %collective-permute-done.5.refs_3_, bf16[448,1024]{1,0:T(8,128)(2,1)} %collective-permute-done.6.refs_4_, ...), custom_call_target="tpu_custom_call" | custom-call | flops 6576668672 | bytes 14680064 | tf_op jit(solution)/shard_map/hidden/pallas_call | solution.py:70
  127.1 3.6 %collective-permute-done.20 = f32[8,56]{1,0:T(8,128)S(1)} collective-permute-done((f32[8,56]{1,0:T(8,128)S(1)}, f32[8,56]{1,0:T(8,128)S(1)}, u32[]{:S(2)}, u32[]{:S(2)}) %collective-permute-start.20) | collective-permute-done | bytes 1824 | tf_op jit(solution)/shard_map/ppermute | solution.py:32
  132.1 3.2 %collective-permute-done.21 = f32[8,56]{1,0:T(8,128)S(1)} collective-permute-done((f32[8,56]{1,0:T(8,128)S(1)}, f32[8,56]{1,0:T(8,128)S(1)}, u32[]{:S(2)}, u32[]{:S(2)}) %collective-permute-start.21) | collective-permute-done | bytes 1824 | tf_op jit(solution)/shard_map/ppermute | solution.py:32
  135.2 3.4 %collective-permute-start.22 = (f32[8,56]{1,0:T(8,128)S(1)}, f32[8,56]{1,0:T(8,128)S(1)}, u32[]{:S(2)}, u32[]{:S(2)}) collective-permute-start(f32[8,56]{1,0:T(8,128)S(1)} %add.171), channel_id=1, source_target_pairs={{0,128},{32,160},{64,192},{96,224},{128,0},{160,32},{192,64},{224,... | collective-permute-start | bytes 5384 | tf_op jit(solution)/shard_map/ppermute | solution.py:32
  138.6 4.2 %collective-permute-done.22 = f32[8,56]{1,0:T(8,128)S(1)} collective-permute-done((f32[8,56]{1,0:T(8,128)S(1)}, f32[8,56]{1,0:T(8,128)S(1)}, u32[]{:S(2)}, u32[]{:S(2)}) %collective-permute-start.22) | collective-permute-done | bytes 1824 | tf_op jit(solution)/shard_map/ppermute | solution.py:32
  152.8 8.0 %all-gather.4.cloned.1.call-done.refs_4_ = bf16[8,224,1024]{2,1,0:T(8,128)(2,1)} async-done(((bf16[1,224,1024]{2,1,0:T(8,128)(2,1)}), bf16[8,224,1024]{2,1,0:T(8,128)(2,1)}) %all-gather.4.cloned.1.call-update) | async-done | bytes 3670032 | tf_op jit(solution)/shard_map/all_gather | solution.py:189
  160.8 6.5 %outputs.1 = (bf16[120,1024]{1,0:T(8,128)(2,1)S(1)}, bf16[120,1024]{1,0:T(8,128)(2,1)S(1)}, bf16[120,1024]{1,0:T(8,128)(2,1)S(1)}, bf16[120,1024]{1,0:T(8,128)(2...) custom-call(bf16[8,56,896]{2,1,0:T(8,128)(2,1)S(1)} %copy-done, ...), custom_call_target="tpu_custom_call" | custom-call | flops 3288334336 | bytes 8716288 | tf_op jit(solution)/shard_map/outputs/pallas_call | solution.py:133
  167.3 3.7 %collective-permute-start.27 = (bf16[120,1024]{1,0:T(8,128)(2,1)S(1)}, bf16[120,1024]{1,0:T(8,128)(2,1)S(1)}, u32[]{:S(2)}, u32[]{:S(2)}) collective-permute-start(bf16[120,1024]{1,0:T(8,128)(2,1)S(1)} %get-tuple-element.15), channel_id=1, source_target_pairs={{0,17},{1,18},{2,19},{3,16},{16,1},{17,2},{18,3},{19,0},{4,21},{5,... | collective-permute-start | bytes 737288 | tf_op jit(solution)/shard_map/ppermute | solution.py:216
  173.0 5.4 %collective-permute-start.30 = (bf16[120,1024]{1,0:T(8,128)(2,1)S(1)}, bf16[120,1024]{1,0:T(8,128)(2,1)S(1)}, u32[]{:S(2)}, u32[]{:S(2)}) collective-permute-start(bf16[120,1024]{1,0:T(8,128)(2,1)S(1)} %get-tuple-element.18), channel_id=1, source_target_pairs={{0,18},{1,19},{2,16},{3,17},{16,2},{17,3},{18,0},{19,1},{4,22},{5,... | collective-permute-start | bytes 737288 | tf_op jit(solution)/shard_map/ppermute | solution.py:216
  180.1 4.6 %collective-permute-done.28 = bf16[120,1024]{1,0:T(8,128)(2,1)S(1)} collective-permute-done((bf16[120,1024]{1,0:T(8,128)(2,1)S(1)}, bf16[120,1024]{1,0:T(8,128)(2,1)S(1)}, u32[]{:S(2)}, u32[]{:S(2)}) %collective-permute-start.28) | collective-permute-done | bytes 245792 | tf_op jit(solution)/shard_map/ppermute | solution.py:216
  184.9 2.6 %collective-permute-done.29 = bf16[120,1024]{1,0:T(8,128)(2,1)S(1)} collective-permute-done((bf16[120,1024]{1,0:T(8,128)(2,1)S(1)}, bf16[120,1024]{1,0:T(8,128)(2,1)S(1)}, u32[]{:S(2)}, u32[]{:S(2)}) %collective-permute-start.29) | collective-permute-done | bytes 245792 | tf_op jit(solution)/shard_map/ppermute | solution.py:216
  187.6 2.9 %collective-permute-done.30 = bf16[120,1024]{1,0:T(8,128)(2,1)S(1)} collective-permute-done((bf16[120,1024]{1,0:T(8,128)(2,1)S(1)}, bf16[120,1024]{1,0:T(8,128)(2,1)S(1)}, u32[]{:S(2)}, u32[]{:S(2)}) %collective-permute-start.30) | collective-permute-done | bytes 245792 | tf_op jit(solution)/shard_map/ppermute | solution.py:216
  190.5 4.6 %collective-permute-done.31 = bf16[120,1024]{1,0:T(8,128)(2,1)S(1)} collective-permute-done((bf16[120,1024]{1,0:T(8,128)(2,1)S(1)}, bf16[120,1024]{1,0:T(8,128)(2,1)S(1)}, u32[]{:S(2)}, u32[]{:S(2)}) %collective-permute-start.31) | collective-permute-done | bytes 245792 | tf_op jit(solution)/shard_map/ppermute | solution.py:216
  (110 shorter events, 44.8 us)
Async XLA Ops:
  7.2 102.8 %all-gather.6.cloned.1.call-start = ((), (), s32[]{:S(2)}) async-start(), calls=%async_computation.1 | async-start | bytes 8257536 | tf_op jit(solution)/shard_map/all_gather | solution.py:175
  10.4 10.8 %collective-permute-start.12 = (bf16[112,1024]{1,0:T(8,128)(2,1)S(1)}, bf16[112,1024]{1,0:T(8,128)(2,1)S(1)}, u32[]{:S(2)}, u32[]{:S(2)}) collective-permute-start(bf16[112,1024]{1,0:T(8,128)(2,1)S(1)} %bitcast.30), channel_id=1, source_target_pairs={{0,12},{4,8},{8,4},{12,0},{1,13},{5,9},{9,5},{13,1},{2,14},{6,10},... | collective-permute-start | bytes 688136 | tf_op jit(solution)/shard_map/ppermute | solution.py:174
  22.2 138.6 %all-gather.4.cloned.1.call-start = ((), (), s32[]{:S(2)}) async-start(), calls=%async_computation | async-start | bytes 4128768 | tf_op jit(solution)/shard_map/all_gather | solution.py:189
  23.2 8.5 %collective-permute-start = (bf16[112,1024]{1,0:T(8,128)(2,1)S(1)}, bf16[112,1024]{1,0:T(8,128)(2,1)S(1)}, u32[]{:S(2)}, u32[]{:S(2)}) collective-permute-start(bf16[112,1024]{1,0:T(8,128)(2,1)S(1)} %copy-done.2), channel_id=1, source_target_pairs={{0,3},{1,0},{2,1},{3,2},{4,7},{5,4},{6,5},{7,6},{8,11},{9,8},{10,9... | collective-permute-start | bytes 688136 | tf_op jit(solution)/shard_map/ppermute | solution.py:192
  23.8 10.0 %collective-permute-start.1 = (bf16[112,1024]{1,0:T(8,128)(2,1)S(1)}, bf16[112,1024]{1,0:T(8,128)(2,1)S(1)}, u32[]{:S(2)}, u32[]{:S(2)}) collective-permute-start(bf16[112,1024]{1,0:T(8,128)(2,1)S(1)} %copy-done.2), channel_id=1, source_target_pairs={{0,2},{1,3},{2,0},{3,1},{4,6},{5,7},{6,4},{7,5},{8,10},{9,11},{10,... | collective-permute-start | bytes 688136 | tf_op jit(solution)/shard_map/ppermute | solution.py:192
  26.6 11.2 %collective-permute-start.2 = (bf16[112,1024]{1,0:T(8,128)(2,1)S(1)}, bf16[112,1024]{1,0:T(8,128)(2,1)S(1)}, u32[]{:S(2)}, u32[]{:S(2)}) collective-permute-start(bf16[112,1024]{1,0:T(8,128)(2,1)S(1)} %copy-done.2), channel_id=1, source_target_pairs={{0,1},{1,2},{2,3},{3,0},{4,5},{5,6},{6,7},{7,4},{8,9},{9,10},{10,1... | collective-permute-start | bytes 688136 | tf_op jit(solution)/shard_map/ppermute | solution.py:192
  37.8 42.2 %collective-permute-start.3 = (bf16[448,1024]{1,0:T(8,128)(2,1)S(1)}, bf16[448,1024]{1,0:T(8,128)(2,1)S(1)}, u32[]{:S(2)}, u32[]{:S(2)}) collective-permute-start(bf16[448,1024]{1,0:T(8,128)(2,1)S(1)} %constant_dynamic-update-slice_fusion.refs_0_), channel_id=1, source_target_pairs={{0,8},{8,0},{16,24},{24,16},{1,9},{9,1},{17,25},{25,17},{2,10},{10... | collective-permute-start | bytes 2752520 | tf_op jit(solution)/shard_map/ppermute | solution.py:164
  39.5 42.9 %collective-permute-start.4 = (bf16[448,1024]{1,0:T(8,128)(2,1)S(1)}, bf16[448,1024]{1,0:T(8,128)(2,1)S(1)}, u32[]{:S(2)}, u32[]{:S(2)}) collective-permute-start(bf16[448,1024]{1,0:T(8,128)(2,1)S(1)} %constant_dynamic-update-slice_fusion.refs_0_), channel_id=1, source_target_pairs={{0,16},{8,24},{16,0},{24,8},{1,17},{9,25},{17,1},{25,9},{2,18},{10... | collective-permute-start | bytes 2752520 | tf_op jit(solution)/shard_map/ppermute | solution.py:164
  42.4 42.7 %collective-permute-start.5 = (bf16[448,1024]{1,0:T(8,128)(2,1)S(1)}, bf16[448,1024]{1,0:T(8,128)(2,1)}, u32[]{:S(2)}, u32[]{:S(2)}) collective-permute-start(bf16[448,1024]{1,0:T(8,128)(2,1)S(1)} %constant_dynamic-update-slice_fusion.refs_0_), channel_id=1, source_target_pairs={{0,24},{8,16},{16,8},{24,0},{1,25},{9,17},{17,9},{25,1},{2,26},{10... | collective-permute-start | bytes 2752520 | tf_op jit(solution)/shard_map/ppermute | solution.py:164
  44.0 35.9 %collective-permute-start.14 = (f32[224]{0:T(256)S(1)}, f32[224]{0:T(256)S(1)}, u32[]{:S(2)}, u32[]{:S(2)}) collective-permute-start(f32[224]{0:T(256)S(1)} %add.165), channel_id=1, source_target_pairs={{0,8},{8,0},{1,9},{9,1},{2,10},{10,2},{3,11},{11,3},{4,12},{12,4},... | collective-permute-start | bytes 2696 | tf_op jit(solution)/shard_map/ppermute | solution.py:32
  80.0 23.6 %collective-permute-start.6 = (bf16[448,1024]{1,0:T(8,128)(2,1)S(1)}, bf16[448,1024]{1,0:T(8,128)(2,1)}, u32[]{:S(2)}, u32[]{:S(2)}) collective-permute-start(bf16[448,1024]{1,0:T(8,128)(2,1)S(1)} %constant_dynamic-update-slice_fusion.refs_0_), channel_id=1, source_target_pairs={{0,4},{4,0},{1,5},{5,1},{2,6},{6,2},{3,7},{7,3},{8,12},{12,8},{9,1... | collective-permute-start | bytes 2752520 | tf_op jit(solution)/shard_map/ppermute | solution.py:167
  80.0 23.6 %collective-permute-start.7 = (bf16[448,1024]{1,0:T(8,128)(2,1)S(1)}, bf16[448,1024]{1,0:T(8,128)(2,1)}, u32[]{:S(2)}, u32[]{:S(2)}) collective-permute-start(bf16[448,1024]{1,0:T(8,128)(2,1)S(1)} %collective-permute-done.3.refs_1_), channel_id=1, source_target_pairs={{0,4},{4,0},{1,5},{5,1},{2,6},{6,2},{3,7},{7,3},{8,12},{12,8},{9,1... | collective-permute-start | bytes 2752520 | tf_op jit(solution)/shard_map/ppermute | solution.py:167
  82.4 21.2 %collective-permute-start.8 = (bf16[448,1024]{1,0:T(8,128)(2,1)S(1)}, bf16[448,1024]{1,0:T(8,128)(2,1)}, u32[]{:S(2)}, u32[]{:S(2)}) collective-permute-start(bf16[448,1024]{1,0:T(8,128)(2,1)S(1)} %collective-permute-done.4.refs_2_), channel_id=1, source_target_pairs={{0,4},{4,0},{1,5},{5,1},{2,6},{6,2},{3,7},{7,3},{8,12},{12,8},{9,1... | collective-permute-start | bytes 2752520 | tf_op jit(solution)/shard_map/ppermute | solution.py:167
  85.1 18.5 %collective-permute-start.9 = (bf16[448,1024]{1,0:T(8,128)(2,1)}, bf16[448,1024]{1,0:T(8,128)(2,1)}, u32[]{:S(2)}, u32[]{:S(2)}) collective-permute-start(bf16[448,1024]{1,0:T(8,128)(2,1)} %collective-permute-done.5.refs_3_), channel_id=1, source_target_pairs={{0,4},{4,0},{1,5},{5,1},{2,6},{6,2},{3,7},{7,3},{8,12},{12,8},{9,1... | collective-permute-start | bytes 2752520 | tf_op jit(solution)/shard_map/ppermute | solution.py:167
  94.4 8.6 %collective-permute-start.17 = (f32[8,224]{1,0:T(8,128)S(1)}, f32[8,224]{1,0:T(8,128)S(1)}, u32[]{:S(2)}, u32[]{:S(2)}) collective-permute-start(f32[8,224]{1,0:T(8,128)S(1)} %fusion.10), channel_id=1, source_target_pairs={{0,128},{32,160},{64,192},{96,224},{128,0},{160,32},{192,64},{224,... | collective-permute-start | bytes 21512 | tf_op jit(solution)/shard_map/ppermute | solution.py:32
  124.0 19.8 %collective-permute-start.19 = (bf16[8,56,896]{2,1,0:T(8,128)(2,1)}, bf16[8,56,896]{2,1,0:T(8,128)(2,1)S(1)}, u32[]{:S(2)}, u32[]{:S(2)}) collective-permute-start(bf16[8,56,896]{2,1,0:T(8,128)(2,1)} %hidden.1.refs_0_), channel_id=1, source_target_pairs={{0,8},{8,0},{1,9},{9,1},{2,10},{10,2},{3,11},{11,3},{4,12},{12,4},... | collective-permute-start | bytes 2408456 | tf_op jit(solution)/shard_map/ppermute | solution.py:199
  125.5 24.7 %collective-permute-start.18 = (bf16[8,56,896]{2,1,0:T(8,128)(2,1)}, bf16[8,56,896]{2,1,0:T(8,128)(2,1)S(1)}, u32[]{:S(2)}, u32[]{:S(2)}) collective-permute-start(bf16[8,56,896]{2,1,0:T(8,128)(2,1)} %hidden.1.refs_0_), channel_id=1, source_target_pairs={{0,4},{4,0},{1,5},{5,1},{2,6},{6,2},{3,7},{7,3},{8,12},{12,8},{9,1... | collective-permute-start | bytes 2408456 | tf_op jit(solution)/shard_map/ppermute | solution.py:167
  167.3 11.6 %collective-permute-start.27 = (bf16[120,1024]{1,0:T(8,128)(2,1)S(1)}, bf16[120,1024]{1,0:T(8,128)(2,1)S(1)}, u32[]{:S(2)}, u32[]{:S(2)}) collective-permute-start(bf16[120,1024]{1,0:T(8,128)(2,1)S(1)} %get-tuple-element.15), channel_id=1, source_target_pairs={{0,17},{1,18},{2,19},{3,16},{16,1},{17,2},{18,3},{19,0},{4,21},{5,... | collective-permute-start | bytes 737288 | tf_op jit(solution)/shard_map/ppermute | solution.py:216
  171.0 13.7 %collective-permute-start.28 = (bf16[120,1024]{1,0:T(8,128)(2,1)S(1)}, bf16[120,1024]{1,0:T(8,128)(2,1)S(1)}, u32[]{:S(2)}, u32[]{:S(2)}) collective-permute-start(bf16[120,1024]{1,0:T(8,128)(2,1)S(1)} %get-tuple-element.16), channel_id=1, source_target_pairs={{0,2},{1,3},{2,0},{3,1},{16,18},{17,19},{18,16},{19,17},{4,6},{5,7... | collective-permute-start | bytes 737288 | tf_op jit(solution)/shard_map/ppermute | solution.py:216
  171.9 15.7 %collective-permute-start.29 = (bf16[120,1024]{1,0:T(8,128)(2,1)S(1)}, bf16[120,1024]{1,0:T(8,128)(2,1)S(1)}, u32[]{:S(2)}, u32[]{:S(2)}) collective-permute-start(bf16[120,1024]{1,0:T(8,128)(2,1)S(1)} %get-tuple-element.17), channel_id=1, source_target_pairs={{0,19},{1,16},{2,17},{3,18},{16,3},{17,0},{18,1},{19,2},{4,23},{5,... | collective-permute-start | bytes 737288 | tf_op jit(solution)/shard_map/ppermute | solution.py:216
  173.0 17.5 %collective-permute-start.30 = (bf16[120,1024]{1,0:T(8,128)(2,1)S(1)}, bf16[120,1024]{1,0:T(8,128)(2,1)S(1)}, u32[]{:S(2)}, u32[]{:S(2)}) collective-permute-start(bf16[120,1024]{1,0:T(8,128)(2,1)S(1)} %get-tuple-element.18), channel_id=1, source_target_pairs={{0,18},{1,19},{2,16},{3,17},{16,2},{17,3},{18,0},{19,1},{4,22},{5,... | collective-permute-start | bytes 737288 | tf_op jit(solution)/shard_map/ppermute | solution.py:216
  178.4 16.7 %collective-permute-start.31 = (bf16[120,1024]{1,0:T(8,128)(2,1)S(1)}, bf16[120,1024]{1,0:T(8,128)(2,1)S(1)}, u32[]{:S(2)}, u32[]{:S(2)}) collective-permute-start(bf16[120,1024]{1,0:T(8,128)(2,1)S(1)} %get-tuple-element.19), channel_id=1, source_target_pairs={{0,16},{1,17},{2,18},{3,19},{16,0},{17,1},{18,2},{19,3},{4,20},{5,... | collective-permute-start | bytes 737288 | tf_op jit(solution)/shard_map/ppermute | solution.py:216
  178.9 16.2 %collective-permute-start.32 = (bf16[120,1024]{1,0:T(8,128)(2,1)S(1)}, bf16[120,1024]{1,0:T(8,128)(2,1)S(1)}, u32[]{:S(2)}, u32[]{:S(2)}) collective-permute-start(bf16[120,1024]{1,0:T(8,128)(2,1)S(1)} %get-tuple-element.20), channel_id=1, source_target_pairs={{0,1},{1,2},{2,3},{3,0},{16,17},{17,18},{18,19},{19,16},{4,5},{5,6... | collective-permute-start | bytes 737288 | tf_op jit(solution)/shard_map/ppermute | solution.py:216
  184.8 10.5 %collective-permute-start.33 = (bf16[120,1024]{1,0:T(8,128)(2,1)S(1)}, bf16[120,1024]{1,0:T(8,128)(2,1)S(1)}, u32[]{:S(2)}, u32[]{:S(2)}) collective-permute-start(bf16[120,1024]{1,0:T(8,128)(2,1)S(1)} %get-tuple-element.21), channel_id=1, source_target_pairs={{0,3},{1,0},{2,1},{3,2},{16,19},{17,16},{18,17},{19,18},{4,7},{5,4... | collective-permute-start | bytes 737288 | tf_op jit(solution)/shard_map/ppermute | solution.py:216
  (19 other events, 229.3 us)
Sparse Core Ops, SparseCore 0:
  22.4 87.5 all-gather.5
  111.8 49.0 all-gather.3
